TPU v7x, 32 devices: a whole 2x2x4 slice. The times are simulated.
32 devices in a mesh: gx: 8 (over z, core), gy: 4 (over y, x).
Axes of the slice: x: 2, y: 2, z: 4, core: 2. Of those that a mesh axis runs over, the one named last changes fastest.
Arguments:
- bin_state: float32 [132, 64, 512], P(None, 'gx', 'gy'), may hold values from 0.05 to 2
- courant_x: float32 [64, 512], P('gx', 'gy'), may hold values from -0.4 to 0.4
- courant_y: float32 [64, 512], P('gx', 'gy'), may hold values from -0.4 to 0.4
- cloudy_order: int32 [8, 4, 8], P('gx', 'gy'), may hold values from 0 to 7, each once within a row
- block_count: int32 [4, 8], P('gy', 'gx'), may hold values from 1 to 8, 40 in all within a row
- gain_kernel: bfloat16 [10, 33, 1089], replicated, may hold values from -0.059814453 to 0.059814453
- loss_rate: bfloat16 [10, 33, 33], replicated, may hold values from 9.9658966e-05 to 0.029907227
Outputs:
- state_out: float32 [132, 64, 512], P(None, 'gx', 'gy')
Inputs may be any that keep to these rules, and one draw needn't show every extreme that they name: `cloudy_order`: each device's row holds each of its 8 block numbers once. `block_count`: each row of 8 counts sums to 40, and its largest count is 8.
All inputs are finite; a program needn't handle non-finite values. No bound on the sum of `block_count` on one device may be relied on, other than what follows from the above.
Results may differ from a plain program's by a relative error of at most 0.0034.
Values may be sent and summed in bfloat16 or wider, within the bound.
No kernel may reach another device: no remote copies, remote signals or barrier semaphores. Data moves between devices by JAX's collectives and lax.ppermute only.
A program may use at most 128 MiB of HBM per device.

v0:
```python
import jax
import jax.numpy as jnp
from jax import lax
from jax.sharding import PartitionSpec as P

BINS = 33
CLASSES = 4
LEV = 4
STEPS = 2


pair_table = (
    (0, 0, 1),
    (0, 1, 1),
    (0, 2, 2),
    (0, 3, 3),
    (1, 1, 1),
    (1, 2, 3),
    (1, 3, 3),
    (2, 2, 3),
    (2, 3, 3),
    (3, 3, 3),
)


def with_halo(shard, sides, width):
    for axis, dim in sides:
        size, length = (lax.axis_size(axis), shard.shape[dim])
        up = [(i, (i + 1) % size) for i in range(size)]
        down = [(j, i) for i, j in up]
        last = lax.slice_in_dim(shard, length - width, length, axis=dim)
        leading = lax.slice_in_dim(shard, 0, width, axis=dim)
        before = lax.ppermute(last, axis, up)
        after = lax.ppermute(leading, axis, down)
        shard = jnp.concatenate([before, shard, after], axis=dim)
    return shard


def upwind(centre, minus_one, minus_two, plus_one, plus_two, courant):
    rising = (2.0 * plus_one + 3.0 * centre - 6.0 * minus_one + minus_two) / 6.0
    falling = (6.0 * plus_one - plus_two - 3.0 * centre - 2.0 * minus_one) / 6.0
    return jnp.where(courant > 0.0, rising, falling)


def transport(fields, courant_x, courant_y):
    wide_x = with_halo(fields, (("gx", 1),), 2)
    along_x = upwind(
        fields, wide_x[:, 1:-3], wide_x[:, :-4], wide_x[:, 3:-1], wide_x[:, 4:], courant_x[None]
    )
    wide_y = with_halo(fields, (("gy", 2),), 2 * LEV)
    along_y = upwind(
        fields,
        wide_y[:, :, LEV : -3 * LEV],
        wide_y[:, :, : -4 * LEV],
        wide_y[:, :, 3 * LEV : -LEV],
        wide_y[:, :, 4 * LEV :],
        courant_y[None],
    )
    return jnp.maximum(fields - courant_x[None] * along_x - courant_y[None] * along_y, 0.0)


def collide(bin_values, gain_kernel, loss_rate):
    column_count = bin_values.shape[1]
    tendency = [jnp.zeros((BINS, column_count), jnp.float32) for member in range(CLASSES)]
    for pair_index, (former, latter, target) in enumerate(pair_table):
        former_bins = bin_values[former * BINS : (former + 1) * BINS]
        latter_bins = bin_values[latter * BINS : (latter + 1) * BINS]
        product = (former_bins[:, None, :] * latter_bins[None, :, :]).reshape(
            BINS * BINS, column_count
        )
        tendency[target] = tendency[target] + jnp.dot(
            gain_kernel[pair_index], product, preferred_element_type=jnp.float32
        )
        tendency[former] = tendency[former] - former_bins.astype(jnp.float32) * jnp.dot(
            loss_rate[pair_index], latter_bins, preferred_element_type=jnp.float32
        )
        tendency[latter] = tendency[latter] - latter_bins.astype(jnp.float32) * jnp.dot(
            loss_rate[pair_index].T, former_bins, preferred_element_type=jnp.float32
        )
    return jnp.concatenate(tendency, axis=0)


def per_device(bin_state, courant_x, courant_y, cloudy_order, block_count, gain_kernel, loss_rate):
    state_now = bin_state
    block_rows = state_now.shape[1]
    block_order = cloudy_order[0, 0]
    own_count = block_count[0, 0]
    row_numbers = jnp.arange(block_rows, dtype=jnp.int32)
    matches = (block_order[:, None] == row_numbers[None, :]).astype(jnp.int32)
    position = jnp.sum(matches * row_numbers[:, None], axis=0)
    cloudy = position < own_count
    for step_index in range(STEPS):
        state_now = transport(state_now, courant_x, courant_y)
        bin_values = state_now.astype(jnp.bfloat16)
        shaped = bin_values.shape
        gained = collide(
            bin_values.reshape(shaped[0], shaped[1] * shaped[2]), gain_kernel, loss_rate
        )
        gained = gained.astype(jnp.bfloat16).reshape(shaped)
        tendency = jnp.where(cloudy[None, :, None], gained, jnp.zeros((), jnp.bfloat16))
        state_now = state_now + tendency.astype(jnp.float32)
    return state_now


def solution(mesh):
    placed = (
        P(None, "gx", "gy"),
        P("gx", "gy"),
        P("gx", "gy"),
        P("gx", "gy", None),
        P("gy", "gx"),
        P(),
        P(),
    )
    return jax.shard_map(
        per_device, mesh=mesh, in_specs=placed, out_specs=P(None, "gx", "gy"), check_vma=False
    )
```

profile of v0, /device:TPU:0, one launch (start us, length us, event | category | flops | bytes accessed | tf_op | source)
XLA Modules:
  0.0 186.7 jit_solution(10292095170510436309)
XLA Ops:
  0.0 1.5 fusion.278
  1.8 4.0 %collective-permute-start.2 = (f32[132,8,8]{0,2,1:T(8,128)S(1)}, f32[132,8,8]{0,2,1:T(8,128)S(1)}, u32[]{:S(2)}, u32[]{:S(2)}) collective-permute-start(f32[132,8,8]{0,2,1:T(8,128)S(1)} %copy.74), channel_id=1, source_target_pairs={{1,0},{2,1},{3,2},{0,3},{5,4},{6,5},{7,6},{4,7},{9,8},{10,9},{11,1... | collective-permute-start | bytes 101384 | tf_op jit(solution)/shard_map/ppermute | solution.py:34
  6.3 3.5 %collective-permute-start = (f32[132,2,128]{2,0,1:T(8,128)S(1)}, f32[132,2,128]{2,0,1:T(8,128)S(1)}, u32[]{:S(2)}, u32[]{:S(2)}) collective-permute-start(f32[132,2,128]{2,0,1:T(8,128)S(1)} %get-tuple-element.14), channel_id=1, source_target_pairs={{4,0},{8,4},{12,8},{16,12},{20,16},{24,20},{28,24},{0,28},{5,1},{9... | collective-permute-start | bytes 405512 | tf_op jit(solution)/shard_map/ppermute | solution.py:34
  12.8 1.9 %fusion.273 = (bf16[132,8,128]{2,0,1:T(8,128)(2,1)S(1)}, f32[132,8,128]{2,0,1:T(8,128)}) fusion(f32[132,8,8]{2,0,1:T(8,128)S(1)} %copy.49, f32[132,8,128]{2,0,1:T(8,128)S(1)} %copy.46, f32[132,8,8]{2,0,1:T(8,128)S(1)} %copy.51, pred[8,128]{1,0:T(8,128)(4,1)S(1)} %get-tuple-element.47, f32[8,128]{1,0:T(8,128)S(1)} %copy-done.13, ...), kind=kLoop, calls=%fused_computation.386 | loop fusion | flops 5001216 | bytes 3592192 | tf_op jit(solution)/shard_map/convert_element_type | solution.py:94
  15.1 8.2 %broadcast_multiply_fusion.18 = (bf16[33,33,1024]{2,1,0:T(8,128)(2,1)}, bf16[33,33,1024]{2,1,0:T(8,128)(2,1)}, bf16[33,33,1024]{2,1,0:T(8,128)(2,1)}, bf16[33,33...) fusion(bf16[33,1024]{1,0:T(8,128)(2,1)S(1)} %bitcast.603, ...), kind=kLoop, calls=%fused_computation.18 | loop fusion | flops 11151360 | bytes 22573056 | tf_op jit(solution)/shard_map/mul | solution.py:68
  23.3 4.6 %mul.688 = bf16[1089,1024]{1,0:T(8,128)(2,1)} reshape(bf16[33,33,1024]{2,1,0:T(8,128)(2,1)} %get-tuple-element.43) | data formatting | bytes 4460544 | tf_op jit(solution)/shard_map/mul | solution.py:68
  27.9 4.6 %mul.684 = bf16[1089,1024]{1,0:T(8,128)(2,1)} reshape(bf16[33,33,1024]{2,1,0:T(8,128)(2,1)} %get-tuple-element.40) | data formatting | bytes 4460544 | tf_op jit(solution)/shard_map/mul | solution.py:68
  32.5 2.9 %convolution_bitcast_fusion.48 = f32[33,1024]{1,0:T(8,128)} fusion(bf16[1089,1024]{1,0:T(8,128)(2,1)} %mul.688, bf16[10,33,1089]{2,1,0:T(8,128)(2,1)} %param.12), kind=kOutput, calls=%fused_computation.162 | convolution fusion | flops 73598976 | bytes 2471936 | tf_op jit(solution)/shard_map/dot_general | solution.py:71
  36.8 4.6 %mul.682 = bf16[1089,1024]{1,0:T(8,128)(2,1)} reshape(bf16[33,33,1024]{2,1,0:T(8,128)(2,1)} %get-tuple-element.44) | data formatting | bytes 4460544 | tf_op jit(solution)/shard_map/mul | solution.py:68
  41.5 2.1 %convolution_bitcast_fusion.50 = f32[33,1024]{1,0:T(8,128)S(1)} fusion(bf16[1089,1024]{1,0:T(8,128)(2,1)} %mul.682, bf16[10,33,1089]{2,1,0:T(8,128)(2,1)} %param.12), kind=kOutput, calls=%fused_computation.164 | convolution fusion | flops 73598976 | bytes 2471936 | tf_op jit(solution)/shard_map/dot_general | solution.py:71
  43.6 4.6 %mul.678 = bf16[1089,1024]{1,0:T(8,128)(2,1)} reshape(bf16[33,33,1024]{2,1,0:T(8,128)(2,1)} %get-tuple-element.42) | data formatting | bytes 4460544 | tf_op jit(solution)/shard_map/mul | solution.py:68
  48.2 2.8 %convolution_bitcast_fusion.51 = f32[33,1024]{1,0:T(8,128)} fusion(bf16[1089,1024]{1,0:T(8,128)(2,1)} %mul.678, bf16[10,33,1089]{2,1,0:T(8,128)(2,1)} %param.12), kind=kOutput, calls=%fused_computation.165 | convolution fusion | flops 73598976 | bytes 2471936 | tf_op jit(solution)/shard_map/dot_general | solution.py:71
  51.0 4.6 %mul.676 = bf16[1089,1024]{1,0:T(8,128)(2,1)} reshape(bf16[33,33,1024]{2,1,0:T(8,128)(2,1)} %get-tuple-element.39) | data formatting | bytes 4460544 | tf_op jit(solution)/shard_map/mul | solution.py:68
  55.6 2.8 %convolution_bitcast_fusion.52 = f32[33,1024]{1,0:T(8,128)} fusion(bf16[1089,1024]{1,0:T(8,128)(2,1)} %mul.676, bf16[10,33,1089]{2,1,0:T(8,128)(2,1)} %param.12), kind=kOutput, calls=%fused_computation.166 | convolution fusion | flops 73598976 | bytes 2471936 | tf_op jit(solution)/shard_map/dot_general | solution.py:71
  58.4 4.6 %mul.673 = bf16[1089,1024]{1,0:T(8,128)(2,1)} reshape(bf16[33,33,1024]{2,1,0:T(8,128)(2,1)} %get-tuple-element.41) | data formatting | bytes 4460544 | tf_op jit(solution)/shard_map/mul | solution.py:68
  63.0 2.2 %convolution_bitcast_fusion.53 = f32[33,1024]{1,0:T(8,128)S(1)} fusion(bf16[1089,1024]{1,0:T(8,128)(2,1)} %mul.673, bf16[10,33,1089]{2,1,0:T(8,128)(2,1)} %param.12), kind=kOutput, calls=%fused_computation.167 | convolution fusion | flops 73598976 | bytes 2471936 | tf_op jit(solution)/shard_map/dot_general | solution.py:71
  67.2 4.6 %mul.665 = bf16[1089,1024]{1,0:T(8,128)(2,1)} reshape(bf16[33,33,1024]{2,1,0:T(8,128)(2,1)} %get-tuple-element.38) | data formatting | bytes 4460544 | tf_op jit(solution)/shard_map/mul | solution.py:68
  71.8 2.1 %convolution_bitcast_fusion.54 = f32[33,1024]{1,0:T(8,128)S(1)} fusion(bf16[1089,1024]{1,0:T(8,128)(2,1)} %mul.665, bf16[10,33,1089]{2,1,0:T(8,128)(2,1)} %param.12), kind=kOutput, calls=%fused_computation.168 | convolution fusion | flops 73598976 | bytes 2471936 | tf_op jit(solution)/shard_map/dot_general | solution.py:71
  74.9 4.6 %mul.658 = bf16[1089,1024]{1,0:T(8,128)(2,1)} reshape(bf16[33,33,1024]{2,1,0:T(8,128)(2,1)} %get-tuple-element.46) | data formatting | bytes 4460544 | tf_op jit(solution)/shard_map/mul | solution.py:68
  79.5 2.1 %convolution_bitcast_fusion.55 = f32[33,1024]{1,0:T(8,128)S(1)} fusion(bf16[1089,1024]{1,0:T(8,128)(2,1)} %mul.658, bf16[10,33,1089]{2,1,0:T(8,128)(2,1)} %param.12), kind=kOutput, calls=%fused_computation.169 | convolution fusion | flops 73598976 | bytes 2471936 | tf_op jit(solution)/shard_map/dot_general | solution.py:71
  81.7 2.1 %mul.651 = bf16[1089,1024]{1,0:T(8,128)(2,1)} reshape(bf16[33,33,1024]{2,1,0:T(8,128)(2,1)S(1)} %get-tuple-element.45) | data formatting | bytes 4460544 | tf_op jit(solution)/shard_map/mul | solution.py:68
  83.8 2.1 %fusion.169 = f32[1024,33]{0,1:T(8,128)S(1)} fusion(bf16[1089,1024]{1,0:T(8,128)(2,1)} %mul.651, bf16[10,33,1089]{2,1,0:T(8,128)(2,1)} %param.12), kind=kOutput, calls=%fused_computation.274 | convolution fusion | flops 73598976 | bytes 2471936 | tf_op jit(solution)/shard_map/dot_general | solution.py:71
  85.9 3.5 %mul.654 = bf16[1089,1024]{1,0:T(8,128)(2,1)S(1)} reshape(bf16[33,33,1024]{2,1,0:T(8,128)(2,1)} %get-tuple-element.37) | data formatting | bytes 4460544 | tf_op jit(solution)/shard_map/mul | solution.py:68
  92.7 3.5 %collective-permute-start.4 = (f32[132,2,128]{2,0,1:T(8,128)S(1)}, f32[132,2,128]{2,0,1:T(8,128)S(1)}, u32[]{:S(2)}, u32[]{:S(2)}) collective-permute-start(f32[132,2,128]{2,0,1:T(8,128)S(1)} %get-tuple-element.10), channel_id=1, source_target_pairs={{4,0},{8,4},{12,8},{16,12},{20,16},{24,20},{28,24},{0,28},{5,1},{9... | collective-permute-start | bytes 405512 | tf_op jit(solution)/shard_map/ppermute | solution.py:34
  96.7 2.9 %collective-permute-start.6 = (f32[132,8,8]{0,2,1:T(8,128)S(1)}, f32[132,8,8]{0,2,1:T(8,128)S(1)}, u32[]{:S(2)}, u32[]{:S(2)}) collective-permute-start(f32[132,8,8]{0,2,1:T(8,128)S(1)} %copy.61), channel_id=1, source_target_pairs={{1,0},{2,1},{3,2},{0,3},{5,4},{6,5},{7,6},{4,7},{9,8},{10,9},{11,1... | collective-permute-start | bytes 101384 | tf_op jit(solution)/shard_map/ppermute | solution.py:34
  100.0 1.6 collective-permute-done.6
  101.8 3.4 %collective-permute-done.7 = f32[132,8,8]{0,2,1:T(8,128)S(1)} collective-permute-done((f32[132,8,8]{0,2,1:T(8,128)S(1)}, f32[132,8,8]{0,2,1:T(8,128)S(1)}, u32[]{:S(2)}, u32[]{:S(2)}) %collective-permute-start.7) | collective-permute-done | bytes 33824 | tf_op jit(solution)/shard_map/ppermute | solution.py:33
  105.4 1.9 %fusion.271 = (bf16[132,8,128]{2,0,1:T(8,128)(2,1)S(1)}, f32[132,8,128]{2,0,1:T(8,128)}) fusion(f32[132,8,8]{2,0,1:T(8,128)S(1)} %copy.62, f32[132,8,128]{2,0,1:T(8,128)S(1)} %convert_add_fusion.1, f32[132,8,8]{2,0,1:T(8,128)S(1)} %copy.64, pred[8,128]{1,0:T(8,128)(4,1)S(1)} %get-tuple-element.47, f32[8,128]{1,0:T(8,128)S(1)} %copy-done.13, ...), kind=kLoop, calls=%fused_computation.385 | loop fusion | flops 5541888 | bytes 1699840 | tf_op jit(solution)/shard_map/convert_element_type | solution.py:94
  108.4 8.2 %broadcast_multiply_fusion.8 = (bf16[33,33,1024]{2,1,0:T(8,128)(2,1)}, bf16[33,33,1024]{2,1,0:T(8,128)(2,1)}, bf16[33,33,1024]{2,1,0:T(8,128)(2,1)}, bf16[33,33,...) fusion(bf16[33,1024]{1,0:T(8,128)(2,1)S(1)} %bitcast.585, ...), kind=kLoop, calls=%fused_computation.8 | loop fusion | flops 11151360 | bytes 22573056 | tf_op jit(solution)/shard_map/mul | solution.py:68
  116.6 4.6 %mul.747 = bf16[1089,1024]{1,0:T(8,128)(2,1)} reshape(bf16[33,33,1024]{2,1,0:T(8,128)(2,1)} %get-tuple-element.33) | data formatting | bytes 4460544 | tf_op jit(solution)/shard_map/mul | solution.py:68
  121.2 2.8 %convolution_bitcast_fusion.40 = f32[33,1024]{1,0:T(8,128)} fusion(bf16[1089,1024]{1,0:T(8,128)(2,1)} %mul.747, bf16[10,33,1089]{2,1,0:T(8,128)(2,1)} %param.12), kind=kOutput, calls=%fused_computation.152 | convolution fusion | flops 73598976 | bytes 2471936 | tf_op jit(solution)/shard_map/dot_general | solution.py:71
  124.0 4.6 %mul.743 = bf16[1089,1024]{1,0:T(8,128)(2,1)} reshape(bf16[33,33,1024]{2,1,0:T(8,128)(2,1)} %get-tuple-element.30) | data formatting | bytes 4460544 | tf_op jit(solution)/shard_map/mul | solution.py:68
  128.6 2.1 %convolution_bitcast_fusion.41 = f32[33,1024]{1,0:T(8,128)S(1)} fusion(bf16[1089,1024]{1,0:T(8,128)(2,1)} %mul.743, bf16[10,33,1089]{2,1,0:T(8,128)(2,1)} %param.12), kind=kOutput, calls=%fused_computation.153 | convolution fusion | flops 73598976 | bytes 2471936 | tf_op jit(solution)/shard_map/dot_general | solution.py:71
  130.8 4.6 %mul.741 = bf16[1089,1024]{1,0:T(8,128)(2,1)} reshape(bf16[33,33,1024]{2,1,0:T(8,128)(2,1)} %get-tuple-element.34) | data formatting | bytes 4460544 | tf_op jit(solution)/shard_map/mul | solution.py:68
  135.4 2.1 %convolution_bitcast_fusion.42 = f32[33,1024]{1,0:T(8,128)S(1)} fusion(bf16[1089,1024]{1,0:T(8,128)(2,1)} %mul.741, bf16[10,33,1089]{2,1,0:T(8,128)(2,1)} %param.12), kind=kOutput, calls=%fused_computation.154 | convolution fusion | flops 73598976 | bytes 2471936 | tf_op jit(solution)/shard_map/dot_general | solution.py:71
  137.5 4.6 %mul.737 = bf16[1089,1024]{1,0:T(8,128)(2,1)} reshape(bf16[33,33,1024]{2,1,0:T(8,128)(2,1)} %get-tuple-element.32) | data formatting | bytes 4460544 | tf_op jit(solution)/shard_map/mul | solution.py:68
  142.1 2.8 %convolution_bitcast_fusion.43 = f32[33,1024]{1,0:T(8,128)} fusion(bf16[1089,1024]{1,0:T(8,128)(2,1)} %mul.737, bf16[10,33,1089]{2,1,0:T(8,128)(2,1)} %param.12), kind=kOutput, calls=%fused_computation.155 | convolution fusion | flops 73598976 | bytes 2471936 | tf_op jit(solution)/shard_map/dot_general | solution.py:71
  144.9 4.6 %mul.735 = bf16[1089,1024]{1,0:T(8,128)(2,1)} reshape(bf16[33,33,1024]{2,1,0:T(8,128)(2,1)} %get-tuple-element.29) | data formatting | bytes 4460544 | tf_op jit(solution)/shard_map/mul | solution.py:68
  149.5 2.8 %convolution_bitcast_fusion.44 = f32[33,1024]{1,0:T(8,128)} fusion(bf16[1089,1024]{1,0:T(8,128)(2,1)} %mul.735, bf16[10,33,1089]{2,1,0:T(8,128)(2,1)} %param.12), kind=kOutput, calls=%fused_computation.156 | convolution fusion | flops 73598976 | bytes 2471936 | tf_op jit(solution)/shard_map/dot_general | solution.py:71
  152.3 4.6 %mul.732 = bf16[1089,1024]{1,0:T(8,128)(2,1)} reshape(bf16[33,33,1024]{2,1,0:T(8,128)(2,1)} %get-tuple-element.31) | data formatting | bytes 4460544 | tf_op jit(solution)/shard_map/mul | solution.py:68
  156.9 2.2 %convolution_bitcast_fusion.45 = f32[33,1024]{1,0:T(8,128)S(1)} fusion(bf16[1089,1024]{1,0:T(8,128)(2,1)} %mul.732, bf16[10,33,1089]{2,1,0:T(8,128)(2,1)} %param.12), kind=kOutput, calls=%fused_computation.157 | convolution fusion | flops 73598976 | bytes 2471936 | tf_op jit(solution)/shard_map/dot_general | solution.py:71
  160.2 4.6 %mul.724 = bf16[1089,1024]{1,0:T(8,128)(2,1)} reshape(bf16[33,33,1024]{2,1,0:T(8,128)(2,1)} %get-tuple-element.28) | data formatting | bytes 4460544 | tf_op jit(solution)/shard_map/mul | solution.py:68
  164.9 2.1 %convolution_bitcast_fusion.46 = f32[33,1024]{1,0:T(8,128)S(1)} fusion(bf16[1089,1024]{1,0:T(8,128)(2,1)} %mul.724, bf16[10,33,1089]{2,1,0:T(8,128)(2,1)} %param.12), kind=kOutput, calls=%fused_computation.158 | convolution fusion | flops 73598976 | bytes 2471936 | tf_op jit(solution)/shard_map/dot_general | solution.py:71
  168.0 4.6 %mul.717 = bf16[1089,1024]{1,0:T(8,128)(2,1)} reshape(bf16[33,33,1024]{2,1,0:T(8,128)(2,1)} %get-tuple-element.36) | data formatting | bytes 4460544 | tf_op jit(solution)/shard_map/mul | solution.py:68
  172.6 2.1 %convolution_bitcast_fusion.47 = f32[33,1024]{1,0:T(8,128)S(1)} fusion(bf16[1089,1024]{1,0:T(8,128)(2,1)} %mul.717, bf16[10,33,1089]{2,1,0:T(8,128)(2,1)} %param.12), kind=kOutput, calls=%fused_computation.159 | convolution fusion | flops 73598976 | bytes 2471936 | tf_op jit(solution)/shard_map/dot_general | solution.py:71
  174.8 2.1 %mul.710 = bf16[1089,1024]{1,0:T(8,128)(2,1)} reshape(bf16[33,33,1024]{2,1,0:T(8,128)(2,1)S(1)} %get-tuple-element.35) | data formatting | bytes 4460544 | tf_op jit(solution)/shard_map/mul | solution.py:68
  176.9 2.1 %fusion.167 = f32[1024,33]{0,1:T(8,128)S(1)} fusion(bf16[1089,1024]{1,0:T(8,128)(2,1)} %mul.710, bf16[10,33,1089]{2,1,0:T(8,128)(2,1)} %param.12), kind=kOutput, calls=%fused_computation.272 | convolution fusion | flops 73598976 | bytes 2471936 | tf_op jit(solution)/shard_map/dot_general | solution.py:71
  179.0 3.5 %mul.713 = bf16[1089,1024]{1,0:T(8,128)(2,1)S(1)} reshape(bf16[33,33,1024]{2,1,0:T(8,128)(2,1)} %get-tuple-element.27) | data formatting | bytes 4460544 | tf_op jit(solution)/shard_map/mul | solution.py:68
  (156 shorter events, 19.1 us)
Async XLA Ops:
  0.0 6.1 %copy-start.1 = (f32[132,8,128]{2,1,0:T(8,128)S(1)}, f32[132,8,128]{2,1,0:T(8,128)}, u32[]{:S(2)}) copy-start(f32[132,8,128]{2,1,0:T(8,128)} %param.7) | copy-start | bytes 1622020
  0.0 9.8 %copy-start.15 = (s32[1,1,8]{2,1,0:T(1,128)S(1)}, s32[1,1,8]{2,1,0:T(1,128)}, u32[]{:S(2)}) copy-start(s32[1,1,8]{2,1,0:T(1,128)} %param.10) | copy-start | bytes 100
  0.0 10.6 %copy-start.13 = (f32[8,128]{1,0:T(8,128)S(1)}, f32[8,128]{1,0:T(8,128)}, u32[]{:S(2)}) copy-start(f32[8,128]{1,0:T(8,128)} %param.9) | copy-start | bytes 12292
  0.0 10.6 %copy-start.14 = (f32[8,128]{1,0:T(8,128)S(1)}, f32[8,128]{1,0:T(8,128)}, u32[]{:S(2)}) copy-start(f32[8,128]{1,0:T(8,128)} %param.8) | copy-start | bytes 12292
  1.8 8.8 %collective-permute-start.2 = (f32[132,8,8]{0,2,1:T(8,128)S(1)}, f32[132,8,8]{0,2,1:T(8,128)S(1)}, u32[]{:S(2)}, u32[]{:S(2)}) collective-permute-start(f32[132,8,8]{0,2,1:T(8,128)S(1)} %copy.74), channel_id=1, source_target_pairs={{1,0},{2,1},{3,2},{0,3},{5,4},{6,5},{7,6},{4,7},{9,8},{10,9},{11,1... | collective-permute-start | bytes 101384 | tf_op jit(solution)/shard_map/ppermute | solution.py:34
  6.0 5.2 %collective-permute-start.3 = (f32[132,8,8]{0,2,1:T(8,128)S(1)}, f32[132,8,8]{0,2,1:T(8,128)S(1)}, u32[]{:S(2)}, u32[]{:S(2)}) collective-permute-start(f32[132,8,8]{0,2,1:T(8,128)S(1)} %copy.75), channel_id=1, source_target_pairs={{0,1},{1,2},{2,3},{3,0},{4,5},{5,6},{6,7},{7,4},{8,9},{9,10},{10,1... | collective-permute-start | bytes 101384 | tf_op jit(solution)/shard_map/ppermute | solution.py:33
  6.2 6.4 %collective-permute-start.1 = (f32[132,2,128]{2,0,1:T(8,128)S(1)}, f32[132,2,128]{2,0,1:T(8,128)S(1)}, u32[]{:S(2)}, u32[]{:S(2)}) collective-permute-start(f32[132,2,128]{2,0,1:T(8,128)S(1)} %get-tuple-element.13), channel_id=1, source_target_pairs={{0,4},{4,8},{8,12},{12,16},{16,20},{20,24},{24,28},{28,0},{1,5},{5... | collective-permute-start | bytes 405512 | tf_op jit(solution)/shard_map/ppermute | solution.py:33
  6.3 6.5 %collective-permute-start = (f32[132,2,128]{2,0,1:T(8,128)S(1)}, f32[132,2,128]{2,0,1:T(8,128)S(1)}, u32[]{:S(2)}, u32[]{:S(2)}) collective-permute-start(f32[132,2,128]{2,0,1:T(8,128)S(1)} %get-tuple-element.14), channel_id=1, source_target_pairs={{4,0},{8,4},{12,8},{16,12},{20,16},{24,20},{28,24},{0,28},{5,1},{9... | collective-permute-start | bytes 405512 | tf_op jit(solution)/shard_map/ppermute | solution.py:34
  32.5 3.0 %copy-start = (bf16[1089,1024]{1,0:T(8,128)(2,1)S(1)}, bf16[1089,1024]{1,0:T(8,128)(2,1)}, u32[]{:S(2)}) copy-start(bf16[1089,1024]{1,0:T(8,128)(2,1)} %mul.684) | copy-start | bytes 6690820
  63.0 2.2 %copy-start.4 = (bf16[10,33,33]{2,1,0:T(8,128)(2,1)S(1)}, bf16[10,33,33]{2,1,0:T(8,128)(2,1)}, u32[]{:S(2)}) copy-start(bf16[10,33,33]{2,1,0:T(8,128)(2,1)} %param.13) | copy-start | bytes 65344
  63.0 3.0 %copy-start.5 = (f32[33,1024]{1,0:T(8,128)S(1)}, f32[33,1024]{1,0:T(8,128)}, u32[]{:S(2)}) copy-start(f32[33,1024]{1,0:T(8,128)} %convolution_bitcast_fusion.51) | copy-start | bytes 405508
  63.0 3.0 %copy-start.7 = (f32[33,1024]{1,0:T(8,128)S(1)}, f32[33,1024]{1,0:T(8,128)}, u32[]{:S(2)}) copy-start(f32[33,1024]{1,0:T(8,128)} %convolution_bitcast_fusion.52) | copy-start | bytes 405508
  63.0 3.5 %copy-start.10 = (f32[33,1024]{1,0:T(8,128)S(1)}, f32[33,1024]{1,0:T(8,128)}, u32[]{:S(2)}) copy-start(f32[33,1024]{1,0:T(8,128)} %convolution_bitcast_fusion.48) | copy-start | bytes 405508
  90.8 1.0 copy-start.12
  91.0 1.5 copy-start.2
  92.7 12.7 %collective-permute-start.4 = (f32[132,2,128]{2,0,1:T(8,128)S(1)}, f32[132,2,128]{2,0,1:T(8,128)S(1)}, u32[]{:S(2)}, u32[]{:S(2)}) collective-permute-start(f32[132,2,128]{2,0,1:T(8,128)S(1)} %get-tuple-element.10), channel_id=1, source_target_pairs={{4,0},{8,4},{12,8},{16,12},{20,16},{24,20},{28,24},{0,28},{5,1},{9... | collective-permute-start | bytes 405512 | tf_op jit(solution)/shard_map/ppermute | solution.py:34
  96.2 9.2 %collective-permute-start.5 = (f32[132,2,128]{2,0,1:T(8,128)S(1)}, f32[132,2,128]{2,0,1:T(8,128)S(1)}, u32[]{:S(2)}, u32[]{:S(2)}) collective-permute-start(f32[132,2,128]{2,0,1:T(8,128)S(1)} %get-tuple-element.9), channel_id=1, source_target_pairs={{0,4},{4,8},{8,12},{12,16},{16,20},{20,24},{24,28},{28,0},{1,5},{5... | collective-permute-start | bytes 405512 | tf_op jit(solution)/shard_map/ppermute | solution.py:33
  96.7 4.8 %collective-permute-start.6 = (f32[132,8,8]{0,2,1:T(8,128)S(1)}, f32[132,8,8]{0,2,1:T(8,128)S(1)}, u32[]{:S(2)}, u32[]{:S(2)}) collective-permute-start(f32[132,8,8]{0,2,1:T(8,128)S(1)} %copy.61), channel_id=1, source_target_pairs={{1,0},{2,1},{3,2},{0,3},{5,4},{6,5},{7,6},{4,7},{9,8},{10,9},{11,1... | collective-permute-start | bytes 101384 | tf_op jit(solution)/shard_map/ppermute | solution.py:34
  100.0 5.2 %collective-permute-start.7 = (f32[132,8,8]{0,2,1:T(8,128)S(1)}, f32[132,8,8]{0,2,1:T(8,128)S(1)}, u32[]{:S(2)}, u32[]{:S(2)}) collective-permute-start(f32[132,8,8]{0,2,1:T(8,128)S(1)} %copy.63), channel_id=1, source_target_pairs={{0,1},{1,2},{2,3},{3,0},{4,5},{5,6},{6,7},{7,4},{8,9},{9,10},{10,1... | collective-permute-start | bytes 101384 | tf_op jit(solution)/shard_map/ppermute | solution.py:33
  156.9 2.2 %copy-start.6 = (f32[33,1024]{1,0:T(8,128)S(1)}, f32[33,1024]{1,0:T(8,128)}, u32[]{:S(2)}) copy-start(f32[33,1024]{1,0:T(8,128)} %convolution_bitcast_fusion.43) | copy-start | bytes 405508
  156.9 2.2 %copy-start.8 = (f32[33,1024]{1,0:T(8,128)S(1)}, f32[33,1024]{1,0:T(8,128)}, u32[]{:S(2)}) copy-start(f32[33,1024]{1,0:T(8,128)} %convolution_bitcast_fusion.44) | copy-start | bytes 405508
  156.9 2.7 %copy-start.9 = (f32[33,1024]{1,0:T(8,128)S(1)}, f32[33,1024]{1,0:T(8,128)}, u32[]{:S(2)}) copy-start(f32[33,1024]{1,0:T(8,128)} %convolution_bitcast_fusion.40) | copy-start | bytes 405508
  183.9 1.0 copy-start.11
  184.1 1.5 copy-start.3
where the time goes:
time: 190 us; the launch traced here: 187 us
  local copies, waits for them, and re-layouts  90.6 us (48%)
  matrix products  53.3 us (28%)
  other arithmetic  20.6 us (11%)
  starting transfers between devices  14.1 us (7%)
  waiting for transfers between devices  6.55 us (3%)
    mul x20, local copies, waits for them, and re-layouts, collide(): former_bins[:, None, :] * latter_bins[None, :, :]  84.9 us
    dot_general x20, matrix products, collide(): jnp.dot(gain_kernel[pair_index], product, preferred_element_type=jnp.floa...  44.6 us
    mul x2, other arithmetic, collide(): former_bins[:, None, :] * latter_bins[None, :, :]  16.4 us
    ppermute x4, starting transfers between devices, with_halo(): after = lax.ppermute(leading, axis, down)  13.9 us
    ppermute x4, waiting for transfers between devices, with_halo(): before = lax.ppermute(last, axis, up)  4.98 us
    dot_general x20, matrix products, collide(): jnp.dot(loss_rate[pair_index], latter_bins, preferred_element_type=jnp.fl...  4.41 us
    dot_general x20, matrix products, collide(): jnp.dot(loss_rate[pair_index].T, former_bins, preferred_element_type=jnp....  4.29 us
    convert_element_type x2, other arithmetic, per_device(): bin_values = state_now.astype(jnp.bfloat16)  3.84 us
  transfers between devices with their start and end apart: 8, of which 4 were waited for; matrix products, arithmetic and copies ran while one was open for 1% of the time, Pallas kernels for 0%

commit v1 on v0

v1 whole, which is shorter than its diff:
```python
import functools
import jax
import jax.numpy as jnp
from jax import lax
from jax.experimental import pallas as pl
from jax.experimental.pallas import tpu as pltpu
from jax.sharding import PartitionSpec as P

BINS = 33
CLASSES = 4
LEV = 4
STEPS = 2
LANES = 128
OFF = (0, 40, 80, 128)
ROWS = 168
PAD = 40
HEAD = 32
LOOK = 14

GROUPS = (
    (1, 0, ((0, 0, False), (1, 1, False))),
    (1, 1, ((4, 1, False),)),
    (2, 0, ((2, 2, False),)),
    (3, 3, ((3, 0, True), (6, 1, True), (8, 2, True), (9, 3, False))),
    (3, 2, ((5, 1, True), (7, 2, False))),
)
PAIRS = ((0, 0), (0, 1), (0, 2), (0, 3), (1, 1), (1, 2), (1, 3), (2, 2), (2, 3), (3, 3))
NG = len(GROUPS)
F32 = jnp.float32
BF16 = jnp.bfloat16


def with_halo(shard, sides, width):
    for axis, dim in sides:
        size, length = (lax.axis_size(axis), shard.shape[dim])
        up = [(i, (i + 1) % size) for i in range(size)]
        down = [(j, i) for i, j in up]
        last = lax.slice_in_dim(shard, length - width, length, axis=dim)
        leading = lax.slice_in_dim(shard, 0, width, axis=dim)
        before = lax.ppermute(last, axis, up)
        after = lax.ppermute(leading, axis, down)
        shard = jnp.concatenate([before, shard, after], axis=dim)
    return shard


def upwind(centre, minus_one, minus_two, plus_one, plus_two, courant):
    rising = (2.0 * plus_one + 3.0 * centre - 6.0 * minus_one + minus_two) / 6.0
    falling = (6.0 * plus_one - plus_two - 3.0 * centre - 2.0 * minus_one) / 6.0
    return jnp.where(courant > 0.0, rising, falling)


def transport(fields, courant_x, courant_y):
    wide_x = with_halo(fields, (("gx", 1),), 2)
    along_x = upwind(
        fields, wide_x[:, 1:-3], wide_x[:, :-4], wide_x[:, 3:-1], wide_x[:, 4:], courant_x[None]
    )
    wide_y = with_halo(fields, (("gy", 2),), 2 * LEV)
    along_y = upwind(
        fields,
        wide_y[:, :, LEV : -3 * LEV],
        wide_y[:, :, : -4 * LEV],
        wide_y[:, :, 3 * LEV : -LEV],
        wide_y[:, :, 4 * LEV :],
        courant_y[None],
    )
    return jnp.maximum(fields - courant_x[None] * along_x - courant_y[None] * along_y, 0.0)


def prepare_kernel(gain, loss, blocks, tails, losses, wide, turned, upper, last_rows):
    lane = lax.broadcasted_iota(jnp.int32, (PAD, LANES), 1)
    tiles = wide.shape[2] // LANES
    turned[...] = jnp.zeros_like(turned)
    slot_of = {}
    for _, _, members in GROUPS:
        for pair, _, second in members:
            if second:
                slot_of[pair] = len(slot_of)
    for pair in range(len(PAIRS)):
        wide[pair] = jnp.zeros((PAD, tiles * LANES), F32)
        wide[pair, :BINS, : BINS * BINS] = gain[pair].astype(F32)
        if pair in slot_of:
            for tile in range(tiles):
                part = wide[pair, :, tile * LANES : (tile + 1) * LANES]
                part = jnp.concatenate([part, jnp.zeros((LANES - PAD, LANES), F32)], axis=0)
                turned[slot_of[pair], tile * LANES : (tile + 1) * LANES, :] = part.T
    last_rows[...] = jnp.zeros_like(last_rows)
    for group, (_, _, members) in enumerate(GROUPS):
        for factor in range(BINS):
            halves = [jnp.zeros((PAD, LANES), F32), jnp.zeros((PAD, LANES), F32)]
            second_members = [m for m in members if m[2]]
            if second_members:
                rows = []
                for other in range(CLASSES - 1):
                    found = [m for m in second_members if m[1] == other]
                    if found:
                        piece = turned[slot_of[found[0][0]], pl.ds(factor, PAD, stride=BINS), :]
                        rows.append(piece)
                    else:
                        rows.append(jnp.zeros((PAD, LANES), F32))
                rows.append(jnp.zeros((LANES - 3 * PAD, LANES), F32))
                halves[0] = jnp.concatenate(rows, axis=0).T[:PAD]
            for pair, other, second in members:
                if second:
                    continue
                start = BINS * factor
                tile, inside = divmod(start, LANES)
                half, at = divmod(OFF[other], LANES)
                shift = (at - inside) % LANES
                first = wide[pair, :, tile * LANES : (tile + 1) * LANES]
                first = pltpu.roll(first, shift, 1) if shift else first
                if inside + BINS > LANES:
                    rest = wide[pair, :, (tile + 1) * LANES : (tile + 2) * LANES]
                    rest = pltpu.roll(rest, shift, 1) if shift else rest
                    first = jnp.where(lane < at + LANES - inside, first, rest)
                halves[half] = jnp.where((lane >= at) & (lane < at + BINS), first, halves[half])
            full = jnp.concatenate(halves, axis=1)
            blocks[group, factor * HEAD : (factor + 1) * HEAD, :] = full[:HEAD].astype(BF16)
            last_rows[group * PAD + factor : group * PAD + factor + 1, :] = full[HEAD : HEAD + 1]
    tails[...] = last_rows[...].astype(BF16)
    upper[...] = jnp.zeros_like(upper)
    for pair, (first, second) in enumerate(PAIRS):
        half, at = divmod(OFF[second], LANES)
        rates = jnp.concatenate(
            [loss[pair].astype(F32), jnp.zeros((BINS, LANES - BINS), F32)], axis=1
        )
        rates = pltpu.roll(rates, at, 1) if at else rates
        rows = slice(OFF[first], OFF[first] + BINS)
        span = slice(half * LANES, (half + 1) * LANES)
        upper[rows, span] = upper[rows, span] + rates
    whole = upper[...]
    losses[...] = (whole + whole.T)[: losses.shape[0]].astype(BF16)


def prepare(gain_kernel, loss_rate):
    wide = -(-BINS * BINS // LANES) * LANES
    tail = -(-NG * PAD // 16) * 16
    rows = -(-ROWS // 16) * 16
    return pl.pallas_call(
        prepare_kernel,
        out_shape=(
            jax.ShapeDtypeStruct((NG, BINS * HEAD, 2 * LANES), BF16),
            jax.ShapeDtypeStruct((tail, 2 * LANES), BF16),
            jax.ShapeDtypeStruct((rows, 2 * LANES), BF16),
        ),
        scratch_shapes=[
            pltpu.VMEM((len(PAIRS), PAD, wide), F32),
            pltpu.VMEM((4, BINS * PAD + BINS, LANES), F32),
            pltpu.VMEM((2 * LANES, 2 * LANES), F32),
            pltpu.VMEM((tail, 2 * LANES), F32),
        ],
    )(gain_kernel, loss_rate)


def collide_tiles(bins, row0, blocks, tails, losses, slots, ends, sinks, emit):
    for unit in range(2):
        right = jnp.concatenate([bins[row0 + 2 * unit], bins[row0 + 2 * unit + 1]], axis=1)
        right = jnp.concatenate(
            [right, jnp.zeros((2 * LANES - ROWS, 2 * LANES), F32)], axis=0
        ).astype(BF16)
        pltpu.matmul_push_rhs(right, 0, unit)
    for unit in range(2):
        pltpu.matmul_acc_lhs(ends[unit], tails[...], 0)
    for unit in range(2):
        pltpu.matmul_acc_lhs(sinks[unit], losses[...])
    depth = len(slots[0])
    pending, count = [], 0
    parts = {t: [[jnp.zeros((HEAD, LANES), F32) for _ in range(2)] for _ in range(2)] for t in (1, 2, 3)}

    def drain():
        target, source, factor, slot = pending.pop(0)
        for unit in range(2):
            block = pltpu.matmul_pop(slots[unit][slot])
            for half in range(2):
                scale = bins[row0 + 2 * unit + half, pl.ds(OFF[source] + factor, 1), :]
                part = block[:, half * LANES : (half + 1) * LANES]
                parts[target][unit][half] = parts[target][unit][half] + part * scale

    last = [[[jnp.zeros((PAD, LANES), F32) for _ in range(2)] for _ in range(2)] for _ in range(4)]
    for unit in range(2):
        block = pltpu.matmul_pop(ends[unit])
        for group, (target, source, _) in enumerate(GROUPS):
            for half in range(2):
                scale = bins[row0 + 2 * unit + half, OFF[source] : OFF[source] + PAD, :]
                piece = block[group * PAD : (group + 1) * PAD, half * LANES : (half + 1) * LANES]
                last[target][unit][half] = last[target][unit][half] + piece * scale
    drop = [pltpu.matmul_pop(sinks[unit]) for unit in range(2)]
    for unit in range(2):
        for half in range(2):
            row = row0 + 2 * unit + half
            for member in range(CLASSES):
                rows = slice(OFF[member], OFF[member] + PAD)
                lost = drop[unit][rows, half * LANES : (half + 1) * LANES] * bins[row, rows, :]
                if member:
                    bottom = jnp.sum(last[member][unit][half], axis=0, keepdims=True)
                    bottom = jnp.concatenate([bottom, jnp.zeros((PAD - HEAD - 1, LANES), F32)], axis=0)
                    base = jnp.concatenate([-lost[:HEAD], bottom - lost[HEAD:]], axis=0)
                else:
                    base = -lost
                emit(row, member, None, base)
    for target in (1, 2, 3):
        order = [
            (group, source, factor)
            for factor in range(BINS)
            for group, (aim, source, _) in enumerate(GROUPS)
            if aim == target
        ]
        for group, source, factor in order:
            slot = count % depth
            count += 1
            left = blocks[group, factor * HEAD : (factor + 1) * HEAD, :]
            for unit in range(2):
                pltpu.matmul_acc_lhs(slots[unit][slot], left)
            pending.append((target, source, factor, slot))
            if len(pending) > LOOK:
                drain()
        while pending:
            drain()
        for unit in range(2):
            for half in range(2):
                emit(row0 + 2 * unit + half, target, parts[target][unit][half], None)


def collide_kernel(flags, field, blocks, tails, losses, out, bins, change):
    rows_x = field.shape[1]
    flat = field.reshape(field.shape[0] * rows_x, LANES)
    flat_out = out.reshape(field.shape[0] * rows_x, LANES)
    bins[...] = jnp.zeros_like(bins)
    for row in range(rows_x):
        for member in range(CLASSES):
            part = flat[pl.ds(member * BINS * rows_x + row, BINS, stride=rows_x), :]
            bins[row, OFF[member] : OFF[member] + BINS, :] = part.astype(BF16).astype(F32)
    tail, rows = tails.shape[0], losses.shape[0]
    depth = LOOK + 2

    def inside(*refs):
        slots = (refs[:depth], refs[depth : 2 * depth])
        ends = refs[2 * depth : 2 * depth + 2]
        sinks = refs[2 * depth + 2 :]

        @pl.loop(0, rows_x // 4)
        def _(step):
            def emit(row, member, gained, base):
                top = slice(OFF[member], OFF[member] + HEAD)
                if base is not None:
                    change[row, OFF[member] : OFF[member] + PAD, :] = base
                else:
                    change[row, top, :] = change[row, top, :] + gained

            collide_tiles(bins, 4 * step, blocks, tails, losses, slots, ends, sinks, emit)

    pl.run_scoped(
        inside,
        *[pltpu.ACC(unit)((HEAD, 2 * LANES), F32) for unit in range(2) for _ in range(depth)],
        *[pltpu.ACC(unit)((tail, 2 * LANES), F32) for unit in range(2)],
        *[pltpu.ACC(unit)((rows, 2 * LANES), F32) for unit in range(2)],
    )
    for row in range(rows_x):
        cloudy = flags[row] > 0
        for member in range(CLASSES):
            span = pl.ds(member * BINS * rows_x + row, BINS, stride=rows_x)
            part = change[row, OFF[member] : OFF[member] + BINS, :].astype(BF16).astype(F32)
            flat_out[span, :] = flat[span, :] + jnp.where(cloudy, part, 0.0)


def collide(field, flags, prepared):
    vmem = pl.BlockSpec(memory_space=pltpu.VMEM)
    rows_x = field.shape[1]
    return pl.pallas_call(
        collide_kernel,
        out_shape=jax.ShapeDtypeStruct(field.shape, F32),
        in_specs=[pl.BlockSpec(memory_space=pltpu.SMEM), vmem, vmem, vmem, vmem],
        out_specs=vmem,
        scratch_shapes=[
            pltpu.VMEM((rows_x, ROWS, LANES), F32),
            pltpu.VMEM((rows_x, ROWS, LANES), F32),
        ],
    )(flags, field, *prepared)


def per_device(bin_state, courant_x, courant_y, cloudy_order, block_count, gain_kernel, loss_rate):
    state_now = bin_state
    block_rows = state_now.shape[1]
    block_order = cloudy_order[0, 0]
    own_count = block_count[0, 0]
    row_numbers = jnp.arange(block_rows, dtype=jnp.int32)
    matches = (block_order[:, None] == row_numbers[None, :]).astype(jnp.int32)
    position = jnp.sum(matches * row_numbers[:, None], axis=0)
    cloudy = (position < own_count).astype(jnp.int32)
    prepared = prepare(gain_kernel, loss_rate)
    for step_index in range(STEPS):
        state_now = transport(state_now, courant_x, courant_y)
        state_now = collide(state_now, cloudy, prepared)
    return state_now


def solution(mesh):
    placed = (
        P(None, "gx", "gy"),
        P("gx", "gy"),
        P("gx", "gy"),
        P("gx", "gy", None),
        P("gy", "gx"),
        P(),
        P(),
    )
    sharded = jax.shard_map(
        per_device, mesh=mesh, in_specs=placed, out_specs=P(None, "gx", "gy"), check_vma=False
    )

    def run(*arguments):
        with jax.sharding.use_abstract_mesh(mesh.abstract_mesh):
            return sharded(*arguments)

    return run
```

time: 190 us -> 47.6 us (0.25); the launches traced: 187 us -> 47.4 us
  local copies, waits for them, and re-layouts: 90.6 us -> 6.01 us
  matrix products: 53.3 us -> 0 us
  Pallas kernels: 0 us -> 18 us
  other arithmetic: 20.6 us -> 5.34 us
  waiting for transfers between devices: 6.55 us -> 2.93 us
    mul x20 -> x0, local copies, waits for them, and re-layouts: 84.9 us -> none  [collide(): former_bins[:, None, :] * latter_bins[None, :, :]]
    dot_general x60 -> x0, matrix products: 53.3 us -> none  [the longest x20 44.6 us: collide(): jnp.dot(gain_kernel[pair_index], product, preferred_element_type=jnp.floa...]
    pallas_call x0 -> x3, Pallas kernels: none -> 18 us  [the longest x2 12.7 us: collide(): pl.pallas_call(collide_kernel, out_shape=jax.ShapeDtypeStruct(field.shape...]
    mul x2 -> x0, other arithmetic: 16.4 us -> none  [collide(): former_bins[:, None, :] * latter_bins[None, :, :]]
    max x0 -> x2, other arithmetic: none -> 4.67 us  [transport(): jnp.maximum(fields - courant_x[None] * along_x - courant_y[None] * along_...]
    convert_element_type x2 -> x1, other arithmetic: 3.84 us -> 0.58 us  [per_device(): cloudy = (position < own_count).astype(jnp.int32)]
    ppermute x4, waiting for transfers between devices: 4.98 us -> 1.73 us  [with_halo(): before = lax.ppermute(last, axis, up)]
    ppermute x4, starting transfers between devices: 0.13 us -> 2.63 us  [with_halo(): before = lax.ppermute(last, axis, up)]
  transfers between devices with their start and end apart: 8 -> 8, of which waited for: 4 -> 2; matrix products, arithmetic and copies ran while one was open for 1% -> 8% of each run, Pallas kernels for 0% -> 11%
where the time goes in v1:
time: 47.6 us; the launch traced here: 47.4 us
  Pallas kernels  18 us (38%)
  starting transfers between devices  14.3 us (30%)
  local copies, waits for them, and re-layouts  6.01 us (13%)
  other arithmetic  5.34 us (11%)
  waiting for transfers between devices  2.93 us (6%)
  between operations  0.81 us (2%)
    pallas_call x2, Pallas kernels, collide(): pl.pallas_call(collide_kernel, out_shape=jax.ShapeDtypeStruct(field.shape...  12.7 us
    ppermute x4, starting transfers between devices, with_halo(): after = lax.ppermute(leading, axis, down)  11.7 us
    pallas_call x1, Pallas kernels, prepare(): pl.pallas_call(prepare_kernel, out_shape=(jax.ShapeDtypeStruct((NG, BINS...  5.26 us
    max x2, other arithmetic, transport(): jnp.maximum(fields - courant_x[None] * along_x - courant_y[None] * along_...  4.67 us
    slice x5, local copies, waits for them, and re-layouts, with_halo(): last = lax.slice_in_dim(shard, length - width, length, axis=dim)  3.5 us
    ppermute x4, starting transfers between devices, with_halo(): before = lax.ppermute(last, axis, up)  2.63 us
    ppermute x4, waiting for transfers between devices, with_halo(): before = lax.ppermute(last, axis, up)  1.73 us
    ppermute x4, waiting for transfers between devices, with_halo(): after = lax.ppermute(leading, axis, down)  1.2 us
  transfers between devices with their start and end apart: 8, of which 2 were waited for; matrix products, arithmetic and copies ran while one was open for 8% of the time, Pallas kernels for 11%

profile of v1, /device:TPU:0, one launch (start us, length us, event | category | flops | bytes accessed | tf_op | source)
XLA Modules:
  0.0 47.4 jit_solution(862750710424530892)
XLA Ops:
  0.0 0.0 copy-start
  0.0 1.4 %fusion.50 = (f32[132,2,128]{2,1,0:T(2,128)S(1)}, f32[132,2,128]{2,1,0:T(2,128)S(1)}) fusion(f32[132,8,128]{2,1,0:T(8,128)} %param.7), kind=kLoop, calls=%fused_computation.83 | loop fusion | bytes 540672 | tf_op jit(solution)/shard_map/slice | solution.py:38
  1.4 0.5 %collective-permute-start.1 = (f32[132,2,128]{2,1,0:T(2,128)S(1)}, f32[132,2,128]{2,1,0:T(2,128)S(1)}, u32[]{:S(2)}, u32[]{:S(2)}) collective-permute-start(f32[132,2,128]{2,1,0:T(2,128)S(1)} %get-tuple-element.15), channel_id=1, source_target_pairs={{0,4},{4,8},{8,12},{12,16},{16,20},{20,24},{24,28},{28,0},{1,5},{5... | collective-permute-start | bytes 405512 | tf_op jit(solution)/shard_map/ppermute | solution.py:40
  2.0 4.1 %collective-permute-start = (f32[132,2,128]{2,1,0:T(2,128)S(1)}, f32[132,2,128]{2,1,0:T(2,128)S(1)}, u32[]{:S(2)}, u32[]{:S(2)}) collective-permute-start(f32[132,2,128]{2,1,0:T(2,128)S(1)} %get-tuple-element.16), channel_id=1, source_target_pairs={{4,0},{8,4},{12,8},{16,12},{20,16},{24,20},{28,24},{0,28},{5,1},{9... | collective-permute-start | bytes 405512 | tf_op jit(solution)/shard_map/ppermute | solution.py:41
  6.1 0.0 copy-done
  6.1 0.2 fusion.51
  6.3 0.0 copy-start.4
  6.3 0.0 copy-start.2
  6.3 0.0 copy-start.3
  6.3 0.3 copy.24
  6.6 2.9 %collective-permute-start.2 = (f32[132,8,8]{0,2,1:T(8,128)S(1)}, f32[132,8,8]{0,2,1:T(8,128)S(1)}, u32[]{:S(2)}, u32[]{:S(2)}) collective-permute-start(f32[132,8,8]{0,2,1:T(8,128)S(1)} %copy.24), channel_id=1, source_target_pairs={{1,0},{2,1},{3,2},{0,3},{5,4},{6,5},{7,6},{4,7},{9,8},{10,9},{11,1... | collective-permute-start | bytes 101384 | tf_op jit(solution)/shard_map/ppermute | solution.py:41
  9.5 0.3 copy.25
  9.8 0.0 collective-permute-start.3
  10.5 0.0 copy-done.4
  10.5 0.1 select_reduce_fusion
  10.6 0.0 copy-done.2
  10.6 0.0 copy-done.3
  10.6 0.6 %compare_convert_fusion.flags = s32[8]{0:T(128)} fusion(s32[8]{0:T(128)S(1)} %select_reduce_fusion, s32[]{:T(128)} %bitcast.2), kind=kLoop, calls=%fused_computation.80 | loop fusion | flops 16 | bytes 68 | tf_op jit(solution)/shard_map/convert_element_type | solution.py:288
  11.2 5.3 %shard_map.73 = (bf16[5,1056,256]{2,1,0:T(8,128)(2,1)}, bf16[208,256]{1,0:T(8,128)(2,1)}, bf16[176,256]{1,0:T(8,128)(2,1)}) custom-call(bf16[10,33,1089]{2,1,0:T(8,128)(2,1)} %gain.1, bf16[10,33,33]{2,1,0:T(8,128)(2,1)} %loss.1), custom_call_target="tpu_custom_call" | custom-call | tf_op jit(solution)/shard_map/pallas_call | solution.py:138
  16.5 0.0 collective-permute-done.3
  16.5 0.4 copy.19
  16.9 0.0 collective-permute-done.2
  16.9 0.4 copy.17
  17.3 0.0 collective-permute-done
  17.3 0.1 constant_dynamic-update-slice_fusion
  17.4 0.0 collective-permute-done.1
  17.4 2.2 %fusion.35.field = f32[132,8,128]{2,1,0:T(8,128)} fusion(f32[132,8,8]{2,1,0:T(8,128)S(1)} %copy.17, f32[132,8,128]{2,1,0:T(8,128)S(1)} %copy-done, f32[132,8,8]{2,1,0:T(8,128)S(1)} %copy.19, f32[132,10,128]{2,1,0:T(8,128)S(1)} %constant_dynamic-update-slice_fusion, f32[132,2,128]{2,1,0:T(2,128)S(1)} %collective-permute-done.1, f32[8,128]{1,0:T(8,128)S(1)} %copy-done.2, ...), kind=kLoop, calls=%fused_computation.56 | loop fusion | flops 5136384 | bytes 2375680 | tf_op jit(solution)/shard_map/max | solution.py:66
  19.6 6.4 %shard_map.74 = f32[132,8,128]{2,1,0:T(8,128)} custom-call(s32[8]{0:T(128)} %compare_convert_fusion.flags, f32[132,8,128]{2,1,0:T(8,128)} %fusion.35.field, bf16[5,1056,256]{2,1,0:T(8,128)(2,1)} %get-tuple-element.8.blocks, bf16[208,256]{1,0:T(8,128)(2,1)} %get-tuple-element.9.tails, bf16[176,256]{1,0:T(8,128)(2,1)} %get-tuple-element.10.losses), custom_call_target="tpu_custom_call" | custom-call | tf_op jit(solution)/shard_map/pallas_call | solution.py:268
  26.0 0.0 copy-start.1
  26.0 1.4 %fusion.48 = (f32[132,2,128]{2,1,0:T(2,128)S(1)}, f32[132,2,128]{2,1,0:T(2,128)S(1)}) fusion(f32[132,8,128]{2,1,0:T(8,128)} %shard_map.74), kind=kLoop, calls=%fused_computation.81 | loop fusion | bytes 540672 | tf_op jit(solution)/shard_map/slice | solution.py:38
  27.3 0.1 collective-permute-start.5
  27.4 3.5 %collective-permute-start.4 = (f32[132,2,128]{2,1,0:T(2,128)S(1)}, f32[132,2,128]{2,1,0:T(2,128)S(1)}, u32[]{:S(2)}, u32[]{:S(2)}) collective-permute-start(f32[132,2,128]{2,1,0:T(2,128)S(1)} %get-tuple-element.12), channel_id=1, source_target_pairs={{4,0},{8,4},{12,8},{16,12},{20,16},{24,20},{28,24},{0,28},{5,1},{9... | collective-permute-start | bytes 405512 | tf_op jit(solution)/shard_map/ppermute | solution.py:41
  30.9 0.0 copy-done.1
  30.9 0.2 fusion.49
  31.1 0.3 copy.22
  31.4 2.0 %collective-permute-start.7 = (f32[132,8,8]{0,2,1:T(8,128)S(1)}, f32[132,8,8]{0,2,1:T(8,128)S(1)}, u32[]{:S(2)}, u32[]{:S(2)}) collective-permute-start(f32[132,8,8]{0,2,1:T(8,128)S(1)} %copy.22), channel_id=1, source_target_pairs={{0,1},{1,2},{2,3},{3,0},{4,5},{5,6},{6,7},{7,4},{8,9},{9,10},{10,1... | collective-permute-start | bytes 101384 | tf_op jit(solution)/shard_map/ppermute | solution.py:40
  33.4 0.3 copy.20
  33.7 1.2 %collective-permute-start.6 = (f32[132,8,8]{0,2,1:T(8,128)S(1)}, f32[132,8,8]{0,2,1:T(8,128)S(1)}, u32[]{:S(2)}, u32[]{:S(2)}) collective-permute-start(f32[132,8,8]{0,2,1:T(8,128)S(1)} %copy.20), channel_id=1, source_target_pairs={{1,0},{2,1},{3,2},{0,3},{5,4},{6,5},{7,6},{4,7},{9,8},{10,9},{11,1... | collective-permute-start | bytes 101384 | tf_op jit(solution)/shard_map/ppermute | solution.py:41
  34.9 1.7 %collective-permute-done.7 = f32[132,8,8]{0,2,1:T(8,128)S(1)} collective-permute-done((f32[132,8,8]{0,2,1:T(8,128)S(1)}, f32[132,8,8]{0,2,1:T(8,128)S(1)}, u32[]{:S(2)}, u32[]{:S(2)}) %collective-permute-start.7) | collective-permute-done | bytes 33824 | tf_op jit(solution)/shard_map/ppermute | solution.py:40
  36.6 0.4 copy.23
  37.0 1.2 %collective-permute-done.6 = f32[132,8,8]{0,2,1:T(8,128)S(1)} collective-permute-done((f32[132,8,8]{0,2,1:T(8,128)S(1)}, f32[132,8,8]{0,2,1:T(8,128)S(1)}, u32[]{:S(2)}, u32[]{:S(2)}) %collective-permute-start.6) | collective-permute-done | bytes 33824 | tf_op jit(solution)/shard_map/ppermute | solution.py:41
  38.2 0.4 copy.21
  38.6 0.0 collective-permute-done.5
  38.6 0.0 collective-permute-done.4
  38.6 2.5 %fusion.14.field = f32[132,8,128]{2,1,0:T(8,128)} fusion(f32[132,8,8]{2,1,0:T(8,128)S(1)} %copy.21, f32[132,8,128]{2,1,0:T(8,128)S(1)} %copy-done.1, f32[132,8,8]{2,1,0:T(8,128)S(1)} %copy.23, f32[132,2,128]{2,1,0:T(2,128)S(1)} %collective-permute-done.4, f32[132,2,128]{2,1,0:T(2,128)S(1)} %collective-permute-done.5, f32[8,128]{1,0:T(8,128)S(1)} %copy-done.2, ...), kind=kLoop, calls=%fused_computation.29 | loop fusion | flops 5406720 | bytes 1429504 | tf_op jit(solution)/shard_map/max | solution.py:66
  41.1 6.4 %shard_map.75 = f32[132,8,128]{2,1,0:T(8,128)} custom-call(s32[8]{0:T(128)} %compare_convert_fusion.flags, f32[132,8,128]{2,1,0:T(8,128)} %fusion.14.field, bf16[5,1056,256]{2,1,0:T(8,128)(2,1)} %get-tuple-element.8.blocks, bf16[208,256]{1,0:T(8,128)(2,1)} %get-tuple-element.9.tails, bf16[176,256]{1,0:T(8,128)(2,1)} %get-tuple-element.10.losses), custom_call_target="tpu_custom_call" | custom-call | tf_op jit(solution)/shard_map/pallas_call | solution.py:268
  (2 shorter events, 0.0 us)
Async XLA Ops:
  0.0 6.1 %copy-start = (f32[132,8,128]{2,1,0:T(8,128)S(1)}, f32[132,8,128]{2,1,0:T(8,128)}, u32[]{:S(2)}) copy-start(f32[132,8,128]{2,1,0:T(8,128)} %param.7) | copy-start | bytes 1622020
  1.4 15.9 %collective-permute-start.1 = (f32[132,2,128]{2,1,0:T(2,128)S(1)}, f32[132,2,128]{2,1,0:T(2,128)S(1)}, u32[]{:S(2)}, u32[]{:S(2)}) collective-permute-start(f32[132,2,128]{2,1,0:T(2,128)S(1)} %get-tuple-element.15), channel_id=1, source_target_pairs={{0,4},{4,8},{8,12},{12,16},{16,20},{20,24},{24,28},{28,0},{1,5},{5... | collective-permute-start | bytes 405512 | tf_op jit(solution)/shard_map/ppermute | solution.py:40
  2.0 15.3 %collective-permute-start = (f32[132,2,128]{2,1,0:T(2,128)S(1)}, f32[132,2,128]{2,1,0:T(2,128)S(1)}, u32[]{:S(2)}, u32[]{:S(2)}) collective-permute-start(f32[132,2,128]{2,1,0:T(2,128)S(1)} %get-tuple-element.16), channel_id=1, source_target_pairs={{4,0},{8,4},{12,8},{16,12},{20,16},{24,20},{28,24},{0,28},{5,1},{9... | collective-permute-start | bytes 405512 | tf_op jit(solution)/shard_map/ppermute | solution.py:41
  6.3 4.2 %copy-start.4 = (s32[1,1,8]{2,1,0:T(1,128)S(1)}, s32[1,1,8]{2,1,0:T(1,128)}, u32[]{:S(2)}) copy-start(s32[1,1,8]{2,1,0:T(1,128)} %param.10) | copy-start | bytes 100
  6.3 4.3 %copy-start.2 = (f32[8,128]{1,0:T(8,128)S(1)}, f32[8,128]{1,0:T(8,128)}, u32[]{:S(2)}) copy-start(f32[8,128]{1,0:T(8,128)} %param.9) | copy-start | bytes 12292
  6.3 4.3 %copy-start.3 = (f32[8,128]{1,0:T(8,128)S(1)}, f32[8,128]{1,0:T(8,128)}, u32[]{:S(2)}) copy-start(f32[8,128]{1,0:T(8,128)} %param.8) | copy-start | bytes 12292
  6.6 10.3 %collective-permute-start.2 = (f32[132,8,8]{0,2,1:T(8,128)S(1)}, f32[132,8,8]{0,2,1:T(8,128)S(1)}, u32[]{:S(2)}, u32[]{:S(2)}) collective-permute-start(f32[132,8,8]{0,2,1:T(8,128)S(1)} %copy.24), channel_id=1, source_target_pairs={{1,0},{2,1},{3,2},{0,3},{5,4},{6,5},{7,6},{4,7},{9,8},{10,9},{11,1... | collective-permute-start | bytes 101384 | tf_op jit(solution)/shard_map/ppermute | solution.py:41
  9.8 6.7 %collective-permute-start.3 = (f32[132,8,8]{0,2,1:T(8,128)S(1)}, f32[132,8,8]{0,2,1:T(8,128)S(1)}, u32[]{:S(2)}, u32[]{:S(2)}) collective-permute-start(f32[132,8,8]{0,2,1:T(8,128)S(1)} %copy.25), channel_id=1, source_target_pairs={{0,1},{1,2},{2,3},{3,0},{4,5},{5,6},{6,7},{7,4},{8,9},{9,10},{10,1... | collective-permute-start | bytes 101384 | tf_op jit(solution)/shard_map/ppermute | solution.py:40
  26.0 5.0 %copy-start.1 = (f32[132,8,128]{2,1,0:T(8,128)S(1)}, f32[132,8,128]{2,1,0:T(8,128)}, u32[]{:S(2)}) copy-start(f32[132,8,128]{2,1,0:T(8,128)} %shard_map.74) | copy-start | bytes 1622020
  27.3 11.3 %collective-permute-start.5 = (f32[132,2,128]{2,1,0:T(2,128)S(1)}, f32[132,2,128]{2,1,0:T(2,128)S(1)}, u32[]{:S(2)}, u32[]{:S(2)}) collective-permute-start(f32[132,2,128]{2,1,0:T(2,128)S(1)} %get-tuple-element.11), channel_id=1, source_target_pairs={{0,4},{4,8},{8,12},{12,16},{16,20},{20,24},{24,28},{28,0},{1,5},{5... | collective-permute-start | bytes 405512 | tf_op jit(solution)/shard_map/ppermute | solution.py:40
  27.4 11.2 %collective-permute-start.4 = (f32[132,2,128]{2,1,0:T(2,128)S(1)}, f32[132,2,128]{2,1,0:T(2,128)S(1)}, u32[]{:S(2)}, u32[]{:S(2)}) collective-permute-start(f32[132,2,128]{2,1,0:T(2,128)S(1)} %get-tuple-element.12), channel_id=1, source_target_pairs={{4,0},{8,4},{12,8},{16,12},{20,16},{24,20},{28,24},{0,28},{5,1},{9... | collective-permute-start | bytes 405512 | tf_op jit(solution)/shard_map/ppermute | solution.py:41
  31.4 5.2 %collective-permute-start.7 = (f32[132,8,8]{0,2,1:T(8,128)S(1)}, f32[132,8,8]{0,2,1:T(8,128)S(1)}, u32[]{:S(2)}, u32[]{:S(2)}) collective-permute-start(f32[132,8,8]{0,2,1:T(8,128)S(1)} %copy.22), channel_id=1, source_target_pairs={{0,1},{1,2},{2,3},{3,0},{4,5},{5,6},{6,7},{7,4},{8,9},{9,10},{10,1... | collective-permute-start | bytes 101384 | tf_op jit(solution)/shard_map/ppermute | solution.py:40
  33.7 4.5 %collective-permute-start.6 = (f32[132,8,8]{0,2,1:T(8,128)S(1)}, f32[132,8,8]{0,2,1:T(8,128)S(1)}, u32[]{:S(2)}, u32[]{:S(2)}) collective-permute-start(f32[132,8,8]{0,2,1:T(8,128)S(1)} %copy.20), channel_id=1, source_target_pairs={{1,0},{2,1},{3,2},{0,3},{5,4},{6,5},{7,6},{4,7},{9,8},{10,9},{11,1... | collective-permute-start | bytes 101384 | tf_op jit(solution)/shard_map/ppermute | solution.py:41

commit v2 on v1

--- a/solution.py
+++ b/solution.py
@@ -16,6 +16,12 @@
 PAD = 40
 HEAD = 32
 LOOK = 14
+HALO = 2 * STEPS
+GROUP = HALO * LEV
+AUX = BINS
+FLAG = AUX + 4
+CHUNKS = tuple((OFF[member], OFF[member] + PAD) for member in range(CLASSES))
+VMEM_LIMIT = 24 << 20
 
 GROUPS = (
     (1, 0, ((0, 0, False), (1, 1, False))),
@@ -28,42 +34,6 @@
 NG = len(GROUPS)
 F32 = jnp.float32
 BF16 = jnp.bfloat16
-
-
-def with_halo(shard, sides, width):
-    for axis, dim in sides:
-        size, length = (lax.axis_size(axis), shard.shape[dim])
-        up = [(i, (i + 1) % size) for i in range(size)]
-        down = [(j, i) for i, j in up]
-        last = lax.slice_in_dim(shard, length - width, length, axis=dim)
-        leading = lax.slice_in_dim(shard, 0, width, axis=dim)
-        before = lax.ppermute(last, axis, up)
-        after = lax.ppermute(leading, axis, down)
-        shard = jnp.concatenate([before, shard, after], axis=dim)
-    return shard
-
-
-def upwind(centre, minus_one, minus_two, plus_one, plus_two, courant):
-    rising = (2.0 * plus_one + 3.0 * centre - 6.0 * minus_one + minus_two) / 6.0
-    falling = (6.0 * plus_one - plus_two - 3.0 * centre - 2.0 * minus_one) / 6.0
-    return jnp.where(courant > 0.0, rising, falling)
-
-
-def transport(fields, courant_x, courant_y):
-    wide_x = with_halo(fields, (("gx", 1),), 2)
-    along_x = upwind(
-        fields, wide_x[:, 1:-3], wide_x[:, :-4], wide_x[:, 3:-1], wide_x[:, 4:], courant_x[None]
-    )
-    wide_y = with_halo(fields, (("gy", 2),), 2 * LEV)
-    along_y = upwind(
-        fields,
-        wide_y[:, :, LEV : -3 * LEV],
-        wide_y[:, :, : -4 * LEV],
-        wide_y[:, :, 3 * LEV : -LEV],
-        wide_y[:, :, 4 * LEV :],
-        courant_y[None],
-    )
-    return jnp.maximum(fields - courant_x[None] * along_x - courant_y[None] * along_y, 0.0)
 
 
 def prepare_kernel(gain, loss, blocks, tails, losses, wide, turned, upper, last_rows):
@@ -148,6 +118,8 @@
             pltpu.VMEM((2 * LANES, 2 * LANES), F32),
             pltpu.VMEM((tail, 2 * LANES), F32),
         ],
+        compiler_params=pltpu.CompilerParams(vmem_limit_bytes=VMEM_LIMIT),
+        cost_estimate=pl.CostEstimate(flops=2 * 10**9, bytes_accessed=4 << 20, transcendentals=0),
     )(gain_kernel, loss_rate)
 
 
@@ -196,7 +168,7 @@
                     base = jnp.concatenate([-lost[:HEAD], bottom - lost[HEAD:]], axis=0)
                 else:
                     base = -lost
-                emit(row, member, None, base)
+                emit(2 * unit + half, member, None, base)
     for target in (1, 2, 3):
         order = [
             (group, source, factor)
@@ -217,80 +189,402 @@
             drain()
         for unit in range(2):
             for half in range(2):
-                emit(row0 + 2 * unit + half, target, parts[target][unit][half], None)
-
-
-def collide_kernel(flags, field, blocks, tails, losses, out, bins, change):
-    rows_x = field.shape[1]
-    flat = field.reshape(field.shape[0] * rows_x, LANES)
-    flat_out = out.reshape(field.shape[0] * rows_x, LANES)
-    bins[...] = jnp.zeros_like(bins)
+                emit(2 * unit + half, target, parts[target][unit][half], None)
+
+
+def accumulators(depth, tail, rows):
+    return (
+        [pltpu.ACC(unit)((HEAD, 2 * LANES), F32) for unit in range(2) for _ in range(depth)]
+        + [pltpu.ACC(unit)((tail, 2 * LANES), F32) for unit in range(2)]
+        + [pltpu.ACC(unit)((rows, 2 * LANES), F32) for unit in range(2)]
+    )
+
+
+def settle(field, mask, change, row, place):
+    def emit(index, member, gained, base):
+        at = row(index)
+        start = OFF[member]
+        if base is not None and member:
+            change[place(index), start : start + PAD, :] = base
+            return
+        if member:
+            base = change[place(index), start : start + PAD, :]
+            base = jnp.concatenate([base[:HEAD] + gained, base[HEAD:]], axis=0)
+        part = jnp.where(mask[at, :1, :] > 0.5, base.astype(BF16).astype(F32), 0.0)
+        span = slice(start, start + PAD)
+        field[at, span, :] = field[at, span, :] + part
+
+    return emit
+
+
+def four_rows(bins, row0, matrices, refs, field, mask, change):
+    depth = LOOK + 2
+    slots = (refs[:depth], refs[depth : 2 * depth])
+    ends, sinks = refs[2 * depth : 2 * depth + 2], refs[2 * depth + 2 :]
+    emit = settle(field, mask, change, lambda index: row0 + index, lambda index: index)
+    collide_tiles(bins, row0, *matrices, slots, ends, sinks, emit)
+
+
+def one_row(bins, row, matrices, refs, field, mask, change):
+    blocks, tails, losses = matrices
+    depth = LOOK + 2
+    slots = (refs[:depth], refs[depth : 2 * depth])
+    end, sink = refs[2 * depth], refs[2 * depth + 3]
+    right = bins[row]
+    right = jnp.concatenate([right, jnp.zeros((2 * LANES - ROWS, LANES), F32)], axis=0)
+    right = jnp.concatenate([right, jnp.zeros((2 * LANES, LANES), F32)], axis=1).astype(BF16)
+    for unit in range(2):
+        pltpu.matmul_push_rhs(right, 0, unit)
+    pltpu.matmul_acc_lhs(end, tails[...], 0)
+    pltpu.matmul_acc_lhs(sink, losses[...], 0)
+    emit = settle(field, mask, change, lambda index: row, lambda index: 0)
+    block = pltpu.matmul_pop(end)[:, :LANES]
+    last = [jnp.zeros((PAD, LANES), F32) for _ in range(CLASSES)]
+    for group, (target, source, _) in enumerate(GROUPS):
+        scale = bins[row, OFF[source] : OFF[source] + PAD, :]
+        last[target] = last[target] + block[group * PAD : (group + 1) * PAD] * scale
+    drop = pltpu.matmul_pop(sink)[:, :LANES]
+    for member in range(CLASSES):
+        span = slice(OFF[member], OFF[member] + PAD)
+        base = -drop[span] * bins[row, span, :]
+        if member:
+            bottom = jnp.sum(last[member], axis=0, keepdims=True)
+            bottom = jnp.concatenate([bottom, jnp.zeros((PAD - HEAD - 1, LANES), F32)], axis=0)
+            base = jnp.concatenate([base[:HEAD], bottom + base[HEAD:]], axis=0)
+        emit(0, member, None, base)
+    parts = {t: [jnp.zeros((HEAD, LANES), F32) for _ in range(2)] for t in (1, 2, 3)}
+    pending, count = [], 0
+
+    def drain():
+        target, source, factor, unit, slot = pending.pop(0)
+        part = pltpu.matmul_pop(slots[unit][slot])[:, :LANES]
+        scale = bins[row, OFF[source] + factor : OFF[source] + factor + 1, :]
+        parts[target][unit] = parts[target][unit] + part * scale
+
+    for target in (1, 2, 3):
+        order = [
+            (group, source, factor)
+            for factor in range(BINS)
+            for group, (aim, source, _) in enumerate(GROUPS)
+            if aim == target
+        ]
+        for group, source, factor in order:
+            unit, slot = count % 2, (count // 2) % len(slots[0])
+            count += 1
+            left = blocks[group, factor * HEAD : (factor + 1) * HEAD, :]
+            pltpu.matmul_acc_lhs(slots[unit][slot], left)
+            pending.append((target, source, factor, unit, slot))
+            if len(pending) > 2 * LOOK:
+                drain()
+        while pending:
+            drain()
+        emit(0, target, parts[target][0] + parts[target][1], None)
+
+
+def weights(tile, row):
+    out, centre = [], 1.0
+    for axis in range(2):
+        pair = tile[row, AUX + 2 * axis : AUX + 2 * axis + 2, :]
+        speed = (pair[:1] + pair[1:]) * (1.0 / 6.0)
+        rising, falling = jnp.maximum(speed, 0.0), jnp.minimum(speed, 0.0)
+        centre = centre - 3.0 * (rising - falling)
+        out.append(
+            (
+                6.0 * rising + 2.0 * falling,
+                -rising,
+                -2.0 * rising - 6.0 * falling,
+                falling,
+            )
+        )
+    return centre, out
+
+
+def advance(centre, along_x, along_y, coefficients):
+    middle, (for_x, for_y) = coefficients
+    total = middle * centre
+    for values, factors in ((along_x, for_x), (along_y, for_y)):
+        for value, factor in zip(values, factors):
+            total = total + factor * value
+    return jnp.maximum(total, 0.0)
+
+
+def shifted(value, amount):
+    amount = amount % LANES
+    return pltpu.roll(value, amount, 1) if amount else value
+
+
+def beside(centre, edge, lane):
+    return (
+        shifted(jnp.where(lane >= LANES - LEV, edge, centre), LEV),
+        shifted(jnp.where(lane >= LANES - 2 * LEV, edge, centre), 2 * LEV),
+        shifted(jnp.where(lane < LEV, edge, centre), -LEV),
+        shifted(jnp.where(lane < 2 * LEV, edge, centre), -2 * LEV),
+    )
+
+
+def lanes():
+    return lax.broadcasted_iota(jnp.int32, (PAD, LANES), 1)
+
+
+def put(field, bins, row, span, value):
+    field[row, span, :] = value
+    bins[row, span, :] = value.astype(BF16).astype(F32)
+
+
+def clear_gap(*arrays):
+    gap = slice(OFF[2] + PAD, OFF[3])
+    for array in arrays:
+        for row in range(array.shape[0]):
+            array[row, gap, :] = jnp.zeros((OFF[3] - OFF[2] - PAD, LANES), F32)
+
+
+def stage_kernel(order, count, state, courant_x, courant_y, rows, edges, low, high):
+    rows_x = state.shape[1]
+    flat = state.reshape(state.shape[0] * rows_x, LANES)
+    spare = jnp.zeros((PAD - BINS, LANES), F32)
     for row in range(rows_x):
+        cloudy = jnp.int32(0)
+        for place in range(rows_x):
+            hit = (order[0, 0, place] == row) & (place < count[0, 0])
+            cloudy = cloudy | hit.astype(jnp.int32)
         for member in range(CLASSES):
             part = flat[pl.ds(member * BINS * rows_x + row, BINS, stride=rows_x), :]
-            bins[row, OFF[member] : OFF[member] + BINS, :] = part.astype(BF16).astype(F32)
-    tail, rows = tails.shape[0], losses.shape[0]
-    depth = LOOK + 2
-
-    def inside(*refs):
-        slots = (refs[:depth], refs[depth : 2 * depth])
-        ends = refs[2 * depth : 2 * depth + 2]
-        sinks = refs[2 * depth + 2 :]
+            rows[row, OFF[member] : OFF[member] + BINS, :] = part
+            rows[row, OFF[member] + BINS : OFF[member] + PAD, :] = spare
+        for axis, courant in enumerate((courant_x, courant_y)):
+            speed = courant[row : row + 1, :]
+            upper = speed.astype(BF16).astype(F32)
+            rows[row, AUX + 2 * axis : AUX + 2 * axis + 1, :] = upper
+            rows[row, AUX + 2 * axis + 1 : AUX + 2 * axis + 2, :] = speed - upper
+        rows[row, FLAG : FLAG + 1, :] = jnp.full((1, LANES), cloudy.astype(F32), F32)
+    clear_gap(rows, edges)
+    owner = lanes() // GROUP
+    for start, stop in CHUNKS:
+        left = jnp.zeros((PAD, LANES), F32)
+        right = left
+        for row in range(rows_x):
+            value = rows[row, start:stop, :]
+            left = jnp.where(owner == row, shifted(value, GROUP * row), left)
+            right = jnp.where(owner == row, shifted(value, GROUP * (row + 1)), right)
+        edges[0, start:stop, :] = left
+        edges[1, start:stop, :] = right
+    low[...] = edges[0].astype(BF16)
+    high[...] = edges[1].astype(BF16)
+
+
+def widen_kernel(rows, before, after, around, to_right, to_left):
+    rows_x = rows.shape[0]
+    inner = lax.broadcasted_iota(jnp.int32, (ROWS, LANES), 1) % GROUP < GROUP // 2
+    near = jnp.where(
+        inner,
+        shifted(before[...].astype(F32), -GROUP // 2),
+        shifted(after[...].astype(F32), GROUP // 2),
+    )
+    around[0] = near
+    for index in range(HALO):
+        to_right[index] = rows[rows_x - HALO + index].astype(BF16)
+        to_left[index] = rows[index].astype(BF16)
+    to_right[HALO] = near.astype(BF16)
+    to_left[HALO] = near.astype(BF16)
+
+
+def inner_kernel(rows, around, blocks, tails, losses, out, bins, change, mask):
+    rows_x = rows.shape[0]
+    lane = lanes()
+    clear_gap(out, bins)
+    for index in range(rows_x - HALO):
+        row = index + HALO // 2
+        coefficients = weights(rows, row)
+        mask[index] = jnp.broadcast_to(rows[row, FLAG : FLAG + 1, :], mask.shape[1:])
+        for start, stop in CHUNKS:
+            span = slice(start, stop)
+            centre = rows[row, span, :]
+            along_x = [rows[row + d, span, :] for d in (-1, -2, 1, 2)]
+            edge = shifted(around[0, span, :], -GROUP * row - GROUP // 2)
+            value = advance(centre, along_x, beside(centre, edge, lane), coefficients)
+            put(out, bins, index, span, value)
+    matrices = (blocks, tails, losses)
+    pl.run_scoped(
+        lambda *refs: four_rows(bins, 0, matrices, refs, out, mask, change),
+        *accumulators(LOOK + 2, tails.shape[0], losses.shape[0]),
+    )
+
+
+def outer_kernel(
+    rows, edges, before, after, around, from_left, from_right, middle, blocks, tails, losses,
+    out, left, right, field, bins, change, mask, second,
+):
+    rows_x = rows.shape[0]
+    lane = lanes()
+    outside = rows_x + HALO
+    for index in range(HALO + 1):
+        left[index] = from_left[index].astype(F32)
+        right[index] = from_right[index].astype(F32)
+    clear_gap(field, bins, second)
+
+    def column(x):
+        if x < 0:
+            return left, x + HALO
+        if x >= rows_x:
+            return right, x - rows_x
+        return rows, x
+
+    def edge_of(x, span):
+        if x < 0:
+            return shifted(left[HALO, span, :], -GROUP * (x + rows_x) - GROUP // 2)
+        if x >= rows_x:
+            return shifted(right[HALO, span, :], -GROUP * (x - rows_x) - GROUP // 2)
+        return shifted(around[0, span, :], -GROUP * x - GROUP // 2)
+
+    reach = HALO // 2
+    for x in list(range(-reach, reach)) + list(range(rows_x - reach, rows_x + reach)):
+        tile, row = column(x)
+        coefficients = weights(tile, row)
+        mask[x + reach] = jnp.broadcast_to(tile[row, FLAG : FLAG + 1, :], mask.shape[1:])
+        for start, stop in CHUNKS:
+            span = slice(start, stop)
+            centre = tile[row, span, :]
+            along_x = []
+            for d in (-1, -2, 1, 2):
+                other, at = column(x + d)
+                along_x.append(other[at, span, :])
+            value = advance(
+                centre, along_x, beside(centre, edge_of(x, span), lane), coefficients
+            )
+            put(field, bins, x + reach, span, value)
+    coefficients = weights(around, 0)
+    mask[outside] = jnp.broadcast_to(around[0, FLAG : FLAG + 1, :], mask.shape[1:])
+    inside = lane % GROUP
+    half = GROUP // 2
+    for start, stop in CHUNKS:
+        span = slice(start, stop)
+        lower, upper = before[span, :].astype(F32), after[span, :].astype(F32)
+        first, last = edges[0, span, :], edges[1, span, :]
+        centre = around[0, span, :]
+        along_y = (
+            jnp.where(
+                inside < half + LEV,
+                shifted(jnp.where(inside < half + LEV, lower, last), -LEV),
+                shifted(upper, half + LEV),
+            ),
+            jnp.where(inside < half, lower, last),
+            jnp.where(
+                inside < LEV,
+                shifted(lower, -half - LEV),
+                shifted(jnp.where(inside < LEV, first, upper), LEV),
+            ),
+            jnp.where(inside < half, first, upper),
+        )
+        beyond = jnp.where(lane >= LANES // 2, left[HALO, span, :], right[HALO, span, :])
+        along_x = (
+            shifted(jnp.where(lane >= LANES - GROUP, beyond, centre), GROUP),
+            shifted(jnp.where(lane >= LANES - 2 * GROUP, beyond, centre), 2 * GROUP),
+            shifted(jnp.where(lane < GROUP, beyond, centre), -GROUP),
+            shifted(jnp.where(lane < 2 * GROUP, beyond, centre), -2 * GROUP),
+        )
+        put(field, bins, outside, span, advance(centre, along_x, along_y, coefficients))
+    for index in range(rows_x - HALO):
+        field[index + HALO] = middle[index]
+        row = index + reach
+        mask[index + HALO] = jnp.broadcast_to(rows[row, FLAG : FLAG + 1, :], mask.shape[1:])
+    matrices = (blocks, tails, losses)
+
+    def collisions(*refs):
+        one_row(bins, outside, matrices, refs, field, mask, change)
+
+        @pl.loop(0, 2)
+        def _(step):
+            four_rows(bins, rows_x * step, matrices, refs, field, mask, change)
+
+        for x in range(rows_x):
+            coefficients = weights(rows, x)
+            for start, stop in CHUNKS:
+                span = slice(start, stop)
+                centre = field[x + reach, span, :]
+                along_x = [field[x + reach + d, span, :] for d in (-1, -2, 1, 2)]
+                edge = shifted(field[outside, span, :], -GROUP * x - GROUP // 2)
+                value = advance(centre, along_x, beside(centre, edge, lane), coefficients)
+                put(second, bins, x + reach, span, value)
 
         @pl.loop(0, rows_x // 4)
         def _(step):
-            def emit(row, member, gained, base):
-                top = slice(OFF[member], OFF[member] + HEAD)
-                if base is not None:
-                    change[row, OFF[member] : OFF[member] + PAD, :] = base
-                else:
-                    change[row, top, :] = change[row, top, :] + gained
-
-            collide_tiles(bins, 4 * step, blocks, tails, losses, slots, ends, sinks, emit)
-
-    pl.run_scoped(
-        inside,
-        *[pltpu.ACC(unit)((HEAD, 2 * LANES), F32) for unit in range(2) for _ in range(depth)],
-        *[pltpu.ACC(unit)((tail, 2 * LANES), F32) for unit in range(2)],
-        *[pltpu.ACC(unit)((rows, 2 * LANES), F32) for unit in range(2)],
-    )
-    for row in range(rows_x):
-        cloudy = flags[row] > 0
+            four_rows(bins, reach + 4 * step, matrices, refs, second, mask, change)
+
+    pl.run_scoped(collisions, *accumulators(LOOK + 2, tails.shape[0], losses.shape[0]))
+    flat = out.reshape(out.shape[0] * rows_x, LANES)
+    for x in range(rows_x):
         for member in range(CLASSES):
-            span = pl.ds(member * BINS * rows_x + row, BINS, stride=rows_x)
-            part = change[row, OFF[member] : OFF[member] + BINS, :].astype(BF16).astype(F32)
-            flat_out[span, :] = flat[span, :] + jnp.where(cloudy, part, 0.0)
-
-
-def collide(field, flags, prepared):
+            span = pl.ds(member * BINS * rows_x + x, BINS, stride=rows_x)
+            flat[span, :] = second[x + reach, OFF[member] : OFF[member] + BINS, :]
+
+
+def call(kernel, outs, scratch, *arguments, scalars=0, flops=0):
     vmem = pl.BlockSpec(memory_space=pltpu.VMEM)
-    rows_x = field.shape[1]
+    smem = pl.BlockSpec(memory_space=pltpu.SMEM)
+    shapes = tuple(jax.ShapeDtypeStruct(shape, dtype) for shape, dtype in outs)
+    moved = sum(a.size * a.dtype.itemsize for a in arguments)
     return pl.pallas_call(
-        collide_kernel,
-        out_shape=jax.ShapeDtypeStruct(field.shape, F32),
-        in_specs=[pl.BlockSpec(memory_space=pltpu.SMEM), vmem, vmem, vmem, vmem],
-        out_specs=vmem,
-        scratch_shapes=[
-            pltpu.VMEM((rows_x, ROWS, LANES), F32),
-            pltpu.VMEM((rows_x, ROWS, LANES), F32),
+        kernel,
+        out_shape=shapes,
+        in_specs=[smem] * scalars + [vmem] * (len(arguments) - scalars),
+        out_specs=tuple(vmem for _ in shapes),
+        scratch_shapes=[pltpu.VMEM(shape, F32) for shape in scratch],
+        compiler_params=pltpu.CompilerParams(vmem_limit_bytes=VMEM_LIMIT),
+        cost_estimate=pl.CostEstimate(flops=flops, bytes_accessed=moved, transcendentals=0),
+    )(*arguments)
+
+
+def exchange(axis, upward, downward):
+    size = lax.axis_size(axis)
+    up = [(i, (i + 1) % size) for i in range(size)]
+    down = [(j, i) for i, j in up]
+    return lax.ppermute(upward, axis, up), lax.ppermute(downward, axis, down)
+
+
+def per_device(bin_state, courant_x, courant_y, cloudy_order, block_count, gain_kernel, loss_rate):
+    rows_x = bin_state.shape[1]
+    tile = (ROWS, LANES)
+    rows, edges, low, high = call(
+        stage_kernel,
+        [((rows_x, *tile), F32), ((2, *tile), F32), (tile, BF16), (tile, BF16)],
+        [],
+        cloudy_order, block_count, bin_state, courant_x, courant_y,
+        scalars=2,
+    )
+    before, after = exchange("gy", high, low)
+    matrices = prepare(gain_kernel, loss_rate)
+    around, to_right, to_left = call(
+        widen_kernel,
+        [((1, *tile), F32), ((HALO + 1, *tile), BF16), ((HALO + 1, *tile), BF16)],
+        [],
+        rows, before, after,
+    )
+    from_left, from_right = exchange("gx", to_right, to_left)
+    inner = rows_x - HALO
+    (middle,) = call(
+        inner_kernel,
+        [((inner, *tile), F32)],
+        [(inner, *tile), (4, *tile), (inner, 8, LANES)],
+        rows, around, *matrices,
+        flops=5 * 10**9,
+    )
+    total = rows_x + HALO + 1
+    (out,) = call(
+        outer_kernel,
+        [(bin_state.shape, F32)],
+        [
+            (HALO + 1, *tile),
+            (HALO + 1, *tile),
+            (total, *tile),
+            (total, *tile),
+            (4, *tile),
+            (total, 8, LANES),
+            (total, *tile),
         ],
-    )(flags, field, *prepared)
-
-
-def per_device(bin_state, courant_x, courant_y, cloudy_order, block_count, gain_kernel, loss_rate):
-    state_now = bin_state
-    block_rows = state_now.shape[1]
-    block_order = cloudy_order[0, 0]
-    own_count = block_count[0, 0]
-    row_numbers = jnp.arange(block_rows, dtype=jnp.int32)
-    matches = (block_order[:, None] == row_numbers[None, :]).astype(jnp.int32)
-    position = jnp.sum(matches * row_numbers[:, None], axis=0)
-    cloudy = (position < own_count).astype(jnp.int32)
-    prepared = prepare(gain_kernel, loss_rate)
-    for step_index in range(STEPS):
-        state_now = transport(state_now, courant_x, courant_y)
-        state_now = collide(state_now, cloudy, prepared)
-    return state_now
+        rows, edges, before, after, around, from_left, from_right, middle, *matrices,
+        flops=20 * 10**9,
+    )
+    return out
 
 
 def solution(mesh):

time: 47.6 us -> 35.6 us (0.75)
  the two profiles are of different devices: /device:TPU:0 before, /device:TPU:1 now
where the time goes in v2:
time: 35.6 us; the launch traced here: 35.3 us
  Pallas kernels  18.8 us (53%)
  starting transfers between devices  5.71 us (16%)
  local copies, waits for them, and re-layouts  5.14 us (14%)
  waiting for transfers between devices  4.91 us (14%)
  between operations  0.71 us (2%)
    pallas_call x4, Pallas kernels, call(): pl.pallas_call(kernel, out_shape=shapes, in_specs=[smem] * scalars + [vme...  16.7 us
    ppermute x4, starting transfers between devices, exchange(): return (lax.ppermute(upward, axis, up), lax.ppermute(downward, axis, down))  5.71 us
    unnamed x12, local copies, waits for them, and re-layouts  5.14 us
    ppermute x4, waiting for transfers between devices, exchange(): return (lax.ppermute(upward, axis, up), lax.ppermute(downward, axis, down))  4.91 us
    pallas_call x1, Pallas kernels, prepare(): pl.pallas_call(prepare_kernel, out_shape=(jax.ShapeDtypeStruct((NG, BINS...  2.18 us
  transfers between devices with their start and end apart: 4, of which 2 were waited for; matrix products, arithmetic and copies ran while one was open for 0% of the time, Pallas kernels for 12%

profile of v2, /device:TPU:1, one launch (start us, length us, event | category | flops | bytes accessed | tf_op | source)
XLA Modules:
  0.0 35.3 jit_solution(2852814209113777809)
XLA Ops:
  0.7 0.0 copy-start
  0.7 1.0 %copy-done = f32[132,8,128]{2,1,0:T(8,128)S(1)} copy-done((f32[132,8,128]{2,1,0:T(8,128)S(1)}, f32[132,8,128]{2,1,0:T(8,128)}, u32[]{:S(2)}) %copy-start) | copy-done | bytes 540696
  1.7 0.0 copy-start.1
  1.7 0.7 %copy-done.1 = f32[8,128]{1,0:T(8,128)S(1)} copy-done((f32[8,128]{1,0:T(8,128)S(1)}, f32[8,128]{1,0:T(8,128)}, u32[]{:S(2)}) %copy-start.1) | copy-done | bytes 4120
  2.4 0.0 copy-start.2
  2.4 0.7 %copy-done.2 = f32[8,128]{1,0:T(8,128)S(1)} copy-done((f32[8,128]{1,0:T(8,128)S(1)}, f32[8,128]{1,0:T(8,128)}, u32[]{:S(2)}) %copy-start.2) | copy-done | bytes 4120
  3.1 0.0 copy-start.3
  3.1 0.7 %copy-done.3 = s32[1,1,8]{2,1,0:T(1,128)S(1)} copy-done((s32[1,1,8]{2,1,0:T(1,128)S(1)}, s32[1,1,8]{2,1,0:T(1,128)}, u32[]{:S(2)}) %copy-start.3) | copy-done | bytes 56
  3.7 1.0 %shard_map.73 = (f32[8,168,128]{2,1,0:T(8,128)S(1)}, f32[2,168,128]{2,1,0:T(8,128)S(1)}, bf16[168,128]{1,0:T(8,128)(2,1)S(1)}, bf16[168,128]{1,0:T(8,128)(2,1)S(1)}) custom-call(s32[1,1,8]{2,1,0:T(1,128)S(1)} %copy-done.3, s32[1,1]{1,0:T(1,128)S(6)} %copy.8.count, f32[132,8,128]{2,1,0:T(8,128)S(1)} %copy-done, f32[8,128]{1,0:T(8,128)S(1)} %copy-done.1, ...), custom_call_target="tpu_custom_call" | custom-call | bytes 548900 | tf_op jit(solution)/shard_map/pallas_call | solution.py:526
  4.7 2.1 %collective-permute-start = (bf16[168,128]{1,0:T(8,128)(2,1)S(1)}, bf16[168,128]{1,0:T(8,128)(2,1)S(1)}, u32[]{:S(2)}, u32[]{:S(2)}) collective-permute-start(bf16[168,128]{1,0:T(8,128)(2,1)S(1)} %get-tuple-element.17), channel_id=1, source_target_pairs={{0,1},{1,2},{2,3},{3,0},{4,5},{5,6},{6,7},{7,4},{8,9},{9,10},{10,1... | collective-permute-start | bytes 129032 | tf_op jit(solution)/shard_map/ppermute | solution.py:541
  6.8 1.0 %collective-permute-start.1 = (bf16[168,128]{1,0:T(8,128)(2,1)S(1)}, bf16[168,128]{1,0:T(8,128)(2,1)S(1)}, u32[]{:S(2)}, u32[]{:S(2)}) collective-permute-start(bf16[168,128]{1,0:T(8,128)(2,1)S(1)} %get-tuple-element.18), channel_id=1, source_target_pairs={{1,0},{2,1},{3,2},{0,3},{5,4},{6,5},{7,6},{4,7},{9,8},{10,9},{11,1... | collective-permute-start | bytes 129032 | tf_op jit(solution)/shard_map/ppermute | solution.py:541
  7.8 0.0 copy-start.4
  7.8 1.2 %copy-done.4 = bf16[10,33,1089]{2,1,0:T(8,128)(2,1)S(1)} copy-done((bf16[10,33,1089]{2,1,0:T(8,128)(2,1)S(1)}, bf16[10,33,1089]{2,1,0:T(8,128)(2,1)}, u32[]{:S(2)}) %copy-start.4) | copy-done | bytes 718764
  9.0 0.0 copy-start.5
  9.0 0.9 %copy-done.5 = bf16[10,33,33]{2,1,0:T(8,128)(2,1)S(1)} copy-done((bf16[10,33,33]{2,1,0:T(8,128)(2,1)S(1)}, bf16[10,33,33]{2,1,0:T(8,128)(2,1)}, u32[]{:S(2)}) %copy-start.5) | copy-done | bytes 21804
  9.9 2.2 %shard_map.75 = (bf16[5,1056,256]{2,1,0:T(8,128)(2,1)S(1)}, bf16[208,256]{1,0:T(8,128)(2,1)S(1)}, bf16[176,256]{1,0:T(8,128)(2,1)S(1)}) custom-call(bf16[10,33,1089]{2,1,0:T(8,128)(2,1)S(1)} %copy-done.4, bf16[10,33,33]{2,1,0:T(8,128)(2,1)S(1)} %copy-done.5), custom_call_target="tpu_custom_call" | custom-call | flops 2000000000 | bytes 4194304 | tf_op jit(solution)/shard_map/pallas_call | solution.py:108
  12.1 0.0 collective-permute-done.before
  12.1 0.0 collective-permute-done.1.after
  12.1 0.1 shard_map.74
  12.2 2.6 %collective-permute-start.2 = (bf16[5,168,128]{2,1,0:T(8,128)(2,1)S(1)}, bf16[5,168,128]{2,1,0:T(8,128)(2,1)S(1)}, u32[]{:S(2)}, u32[]{:S(2)}) collective-permute-start(bf16[5,168,128]{2,1,0:T(8,128)(2,1)S(1)} %get-tuple-element.20), channel_id=1, source_target_pairs={{0,4},{4,8},{8,12},{12,16},{16,20},{20,24},{24,28},{28,0},{1,5},{5... | collective-permute-start | bytes 645128 | tf_op jit(solution)/shard_map/ppermute | solution.py:541
  14.8 0.0 collective-permute-start.3
  14.8 2.2 %shard_map.76.middle = f32[4,168,128]{2,1,0:T(8,128)S(1)} custom-call(f32[8,168,128]{2,1,0:T(8,128)S(1)} %get-tuple-element.15.rows, f32[1,168,128]{2,1,0:T(8,128)S(1)} %get-tuple-element.19.around, bf16[5,1056,256]{2,1,0:T(8,128)(2,1)S(1)} %get-tuple-element.22.blocks, bf16[208,256]{1,0:T(8,128)(2,1)S(1)} %get-tuple-element.23.tails, ...), custom_call_target="tpu_custom_call" | custom-call | flops 5000000000 | bytes 3674112 | tf_op jit(solution)/shard_map/pallas_call | solution.py:526
  17.0 0.6 %collective-permute-done.2.from_left = bf16[5,168,128]{2,1,0:T(8,128)(2,1)S(1)} collective-permute-done((bf16[5,168,128]{2,1,0:T(8,128)(2,1)S(1)}, bf16[5,168,128]{2,1,0:T(8,128)(2,1)S(1)}, u32[]{:S(2)}, u32[]{:S(2)}) %collective-permute-start.2) | collective-permute-done | bytes 215072 | tf_op jit(solution)/shard_map/ppermute | solution.py:541
  17.6 4.3 %collective-permute-done.3.from_right = bf16[5,168,128]{2,1,0:T(8,128)(2,1)S(1)} collective-permute-done((bf16[5,168,128]{2,1,0:T(8,128)(2,1)S(1)}, bf16[5,168,128]{2,1,0:T(8,128)(2,1)S(1)}, u32[]{:S(2)}, u32[]{:S(2)}) %collective-permute-start.3) | collective-permute-done | bytes 215072 | tf_op jit(solution)/shard_map/ppermute | solution.py:541
  21.9 13.4 %shard_map.77 = f32[132,8,128]{2,1,0:T(8,128)} custom-call(f32[8,168,128]{2,1,0:T(8,128)S(1)} %get-tuple-element.15.rows, f32[2,168,128]{2,1,0:T(8,128)S(1)} %get-tuple-element.16.edges, bf16[168,128]{1,0:T(8,128)(2,1)S(1)} %collective-permute-done.before, bf16[168,128]{1,0:T(8,128)(2,1)S(1)} %collective-permute-done.1.after, ...), custom_call_target="tpu_custom_call" | custom-call | flops 20000000000 | bytes 4706304 | tf_op jit(solution)/shard_map/pallas_call | solution.py:526
Async XLA Ops:
  0.7 1.0 %copy-start = (f32[132,8,128]{2,1,0:T(8,128)S(1)}, f32[132,8,128]{2,1,0:T(8,128)}, u32[]{:S(2)}) copy-start(f32[132,8,128]{2,1,0:T(8,128)} %state.1) | copy-start | bytes 1622020
  1.7 0.7 %copy-start.1 = (f32[8,128]{1,0:T(8,128)S(1)}, f32[8,128]{1,0:T(8,128)}, u32[]{:S(2)}) copy-start(f32[8,128]{1,0:T(8,128)} %courant_x.1) | copy-start | bytes 12292
  2.4 0.7 %copy-start.2 = (f32[8,128]{1,0:T(8,128)S(1)}, f32[8,128]{1,0:T(8,128)}, u32[]{:S(2)}) copy-start(f32[8,128]{1,0:T(8,128)} %courant_y.1) | copy-start | bytes 12292
  3.1 0.7 %copy-start.3 = (s32[1,1,8]{2,1,0:T(1,128)S(1)}, s32[1,1,8]{2,1,0:T(1,128)}, u32[]{:S(2)}) copy-start(s32[1,1,8]{2,1,0:T(1,128)} %order.1) | copy-start | bytes 100
  4.7 7.4 %collective-permute-start = (bf16[168,128]{1,0:T(8,128)(2,1)S(1)}, bf16[168,128]{1,0:T(8,128)(2,1)S(1)}, u32[]{:S(2)}, u32[]{:S(2)}) collective-permute-start(bf16[168,128]{1,0:T(8,128)(2,1)S(1)} %get-tuple-element.17), channel_id=1, source_target_pairs={{0,1},{1,2},{2,3},{3,0},{4,5},{5,6},{6,7},{7,4},{8,9},{9,10},{10,1... | collective-permute-start | bytes 129032 | tf_op jit(solution)/shard_map/ppermute | solution.py:541
  6.8 5.3 %collective-permute-start.1 = (bf16[168,128]{1,0:T(8,128)(2,1)S(1)}, bf16[168,128]{1,0:T(8,128)(2,1)S(1)}, u32[]{:S(2)}, u32[]{:S(2)}) collective-permute-start(bf16[168,128]{1,0:T(8,128)(2,1)S(1)} %get-tuple-element.18), channel_id=1, source_target_pairs={{1,0},{2,1},{3,2},{0,3},{5,4},{6,5},{7,6},{4,7},{9,8},{10,9},{11,1... | collective-permute-start | bytes 129032 | tf_op jit(solution)/shard_map/ppermute | solution.py:541
  7.8 1.2 %copy-start.4 = (bf16[10,33,1089]{2,1,0:T(8,128)(2,1)S(1)}, bf16[10,33,1089]{2,1,0:T(8,128)(2,1)}, u32[]{:S(2)}) copy-start(bf16[10,33,1089]{2,1,0:T(8,128)(2,1)} %gain.1) | copy-start | bytes 2156224
  9.0 0.9 %copy-start.5 = (bf16[10,33,33]{2,1,0:T(8,128)(2,1)S(1)}, bf16[10,33,33]{2,1,0:T(8,128)(2,1)}, u32[]{:S(2)}) copy-start(bf16[10,33,33]{2,1,0:T(8,128)(2,1)} %loss.1) | copy-start | bytes 65344
  12.2 5.4 %collective-permute-start.2 = (bf16[5,168,128]{2,1,0:T(8,128)(2,1)S(1)}, bf16[5,168,128]{2,1,0:T(8,128)(2,1)S(1)}, u32[]{:S(2)}, u32[]{:S(2)}) collective-permute-start(bf16[5,168,128]{2,1,0:T(8,128)(2,1)S(1)} %get-tuple-element.20), channel_id=1, source_target_pairs={{0,4},{4,8},{8,12},{12,16},{16,20},{20,24},{24,28},{28,0},{1,5},{5... | collective-permute-start | bytes 645128 | tf_op jit(solution)/shard_map/ppermute | solution.py:541
  14.8 7.1 %collective-permute-start.3 = (bf16[5,168,128]{2,1,0:T(8,128)(2,1)S(1)}, bf16[5,168,128]{2,1,0:T(8,128)(2,1)S(1)}, u32[]{:S(2)}, u32[]{:S(2)}) collective-permute-start(bf16[5,168,128]{2,1,0:T(8,128)(2,1)S(1)} %get-tuple-element.21), channel_id=1, source_target_pairs={{4,0},{8,4},{12,8},{16,12},{20,16},{24,20},{28,24},{0,28},{5,1},{9... | collective-permute-start | bytes 645128 | tf_op jit(solution)/shard_map/ppermute | solution.py:541

commit v3 on v2

--- a/solution.py
+++ b/solution.py
@@ -11,8 +11,9 @@
 LEV = 4
 STEPS = 2
 LANES = 128
+SUBLANES = 8
 OFF = (0, 40, 80, 128)
-ROWS = 168
+ROWS = 176
 PAD = 40
 HEAD = 32
 LOOK = 14
@@ -20,6 +21,7 @@
 GROUP = HALO * LEV
 AUX = BINS
 FLAG = AUX + 4
+EDGE = 2 * LANES - GROUP
 CHUNKS = tuple((OFF[member], OFF[member] + PAD) for member in range(CLASSES))
 VMEM_LIMIT = 24 << 20
 
@@ -36,7 +38,7 @@
 BF16 = jnp.bfloat16
 
 
-def prepare_kernel(gain, loss, blocks, tails, losses, wide, turned, upper, last_rows):
+def prepare_kernel(gain, loss, blocks, tails, losses, moves, wide, turned, upper, last_rows):
     lane = lax.broadcasted_iota(jnp.int32, (PAD, LANES), 1)
     tiles = wide.shape[2] // LANES
     turned[...] = jnp.zeros_like(turned)
@@ -99,6 +101,23 @@
         upper[rows, span] = upper[rows, span] + rates
     whole = upper[...]
     losses[...] = (whole + whole.T)[: losses.shape[0]].astype(BF16)
+    fill_moves(moves)
+
+
+def fill_moves(moves):
+    moves[...] = jnp.zeros_like(moves)
+    for part, step in enumerate((LEV, 2 * LEV)):
+        source = lax.broadcasted_iota(jnp.int32, (LANES, LANES), 0)
+        target = lax.broadcasted_iota(jnp.int32, (LANES, LANES), 1)
+        moves[part, :LANES, :LANES] = jnp.where(source == target - step, 1.0, 0.0).astype(BF16)
+        moves[part, :LANES, LANES:] = jnp.where(source == target + step, 1.0, 0.0).astype(BF16)
+        source, target = source[:GROUP], target[:GROUP]
+        half = GROUP // 2
+        low = (target < step) & (source == target + half - step)
+        high = (target >= LANES - step) & (source == target - (LANES - step) + half)
+        rows = slice(EDGE, EDGE + GROUP)
+        moves[part, rows, :LANES] = jnp.where(low, 1.0, 0.0).astype(BF16)
+        moves[part, rows, LANES:] = jnp.where(high, 1.0, 0.0).astype(BF16)
 
 
 def prepare(gain_kernel, loss_rate):
@@ -111,6 +130,7 @@
             jax.ShapeDtypeStruct((NG, BINS * HEAD, 2 * LANES), BF16),
             jax.ShapeDtypeStruct((tail, 2 * LANES), BF16),
             jax.ShapeDtypeStruct((rows, 2 * LANES), BF16),
+            jax.ShapeDtypeStruct((2, EDGE + LANES, 2 * LANES), BF16),
         ),
         scratch_shapes=[
             pltpu.VMEM((len(PAIRS), PAD, wide), F32),
@@ -284,8 +304,11 @@
 def weights(tile, row):
     out, centre = [], 1.0
     for axis in range(2):
-        pair = tile[row, AUX + 2 * axis : AUX + 2 * axis + 2, :]
-        speed = (pair[:1] + pair[1:]) * (1.0 / 6.0)
+        first, second = (
+            jnp.broadcast_to(tile[row, pl.ds(AUX + 2 * axis + part, 1), :], (SUBLANES, LANES))
+            for part in range(2)
+        )
+        speed = (first + second) * (1.0 / 6.0)
         rising, falling = jnp.maximum(speed, 0.0), jnp.minimum(speed, 0.0)
         centre = centre - 3.0 * (rising - falling)
         out.append(
@@ -299,6 +322,10 @@
     return centre, out
 
 
+def cells(value):
+    return value.reshape(value.shape[0] // SUBLANES, SUBLANES, LANES)
+
+
 def advance(centre, along_x, along_y, coefficients):
     middle, (for_x, for_y) = coefficients
     total = middle * centre
@@ -310,37 +337,68 @@
 
 def shifted(value, amount):
     amount = amount % LANES
-    return pltpu.roll(value, amount, 1) if amount else value
-
-
-def beside(centre, edge, lane):
-    return (
-        shifted(jnp.where(lane >= LANES - LEV, edge, centre), LEV),
-        shifted(jnp.where(lane >= LANES - 2 * LEV, edge, centre), 2 * LEV),
-        shifted(jnp.where(lane < LEV, edge, centre), -LEV),
-        shifted(jnp.where(lane < 2 * LEV, edge, centre), -2 * LEV),
-    )
+    return pltpu.roll(value, amount, value.ndim - 1) if amount else value
+
+
+def travel(jobs, moves, refs, finish):
+    def issue(number, job):
+        row, outside, place = job
+        left = jnp.concatenate([row().astype(BF16), outside().astype(BF16)], axis=1)
+        for unit in range(2):
+            start = EDGE - GROUP * place
+            right = [moves[unit, :LANES, :], moves[unit, start : start + LANES, :]]
+            pltpu.matmul_push_rhs(jnp.concatenate(right, axis=0), number % 2, unit)
+            pltpu.matmul_acc_lhs(refs[2 * (number % 2) + unit], left, number % 2)
+
+    for number in range(len(jobs) + 1):
+        if number < len(jobs):
+            issue(number, jobs[number])
+        if number:
+            one, two = (pltpu.matmul_pop(refs[2 * ((number - 1) % 2) + unit]) for unit in range(2))
+            finish(number - 1, (one[:, :LANES], two[:, :LANES], one[:, LANES:], two[:, LANES:]))
+
+
+def travellers():
+    return [pltpu.ACC(unit)((ROWS, 2 * LANES), F32) for _ in range(2) for unit in range(2)]
 
 
 def lanes():
-    return lax.broadcasted_iota(jnp.int32, (PAD, LANES), 1)
+    return lax.broadcasted_iota(jnp.int32, (SUBLANES, LANES), 1)
 
 
 def put(field, bins, row, span, value):
+    value = value.reshape(PAD, LANES)
     field[row, span, :] = value
     bins[row, span, :] = value.astype(BF16).astype(F32)
 
 
 def clear_gap(*arrays):
-    gap = slice(OFF[2] + PAD, OFF[3])
-    for array in arrays:
-        for row in range(array.shape[0]):
-            array[row, gap, :] = jnp.zeros((OFF[3] - OFF[2] - PAD, LANES), F32)
-
-
-def stage_kernel(order, count, state, courant_x, courant_y, rows, edges, low, high):
+    for start, stop in ((OFF[2] + PAD, OFF[3]), (OFF[3] + PAD, ROWS)):
+        for array in arrays:
+            for row in range(array.shape[0]):
+                array[row, start:stop, :] = jnp.zeros((stop - start, LANES), F32)
+
+
+def stage_kernel(
+    order, count, state_hbm, courant_x_hbm, courant_y_hbm, gain_hbm, loss_hbm,
+    rows, edges, low, high, gain, loss, state, courant_x, courant_y, arrived,
+):
     rows_x = state.shape[1]
     flat = state.reshape(state.shape[0] * rows_x, LANES)
+    pieces = [
+        (state_hbm.at[pl.ds(member * BINS, BINS)], state.at[pl.ds(member * BINS, BINS)])
+        for member in range(CLASSES)
+    ]
+    pieces += [(courant_x_hbm, courant_x), (courant_y_hbm, courant_y)]
+    pieces += [(gain_hbm, gain), (loss_hbm, loss)]
+    copies = [
+        pltpu.make_async_copy(source, target, arrived.at[number])
+        for number, (source, target) in enumerate(pieces)
+    ]
+    for copy in copies:
+        copy.start()
+    for copy in copies[:-2]:
+        copy.wait()
     spare = jnp.zeros((PAD - BINS, LANES), F32)
     for row in range(rows_x):
         cloudy = jnp.int32(0)
@@ -360,16 +418,18 @@
     clear_gap(rows, edges)
     owner = lanes() // GROUP
     for start, stop in CHUNKS:
-        left = jnp.zeros((PAD, LANES), F32)
+        left = jnp.zeros((PAD // SUBLANES, SUBLANES, LANES), F32)
         right = left
         for row in range(rows_x):
-            value = rows[row, start:stop, :]
+            value = cells(rows[row, start:stop, :])
             left = jnp.where(owner == row, shifted(value, GROUP * row), left)
             right = jnp.where(owner == row, shifted(value, GROUP * (row + 1)), right)
-        edges[0, start:stop, :] = left
-        edges[1, start:stop, :] = right
+        edges[0, start:stop, :] = left.reshape(PAD, LANES)
+        edges[1, start:stop, :] = right.reshape(PAD, LANES)
     low[...] = edges[0].astype(BF16)
     high[...] = edges[1].astype(BF16)
+    for copy in copies[-2:]:
+        copy.wait()
 
 
 def widen_kernel(rows, before, after, around, to_right, to_left):
@@ -388,21 +448,24 @@
     to_left[HALO] = near.astype(BF16)
 
 
-def inner_kernel(rows, around, blocks, tails, losses, out, bins, change, mask):
+def inner_kernel(rows, around, moves, blocks, tails, losses, out, bins, change, mask):
     rows_x = rows.shape[0]
-    lane = lanes()
     clear_gap(out, bins)
-    for index in range(rows_x - HALO):
-        row = index + HALO // 2
+    places = [index + HALO // 2 for index in range(rows_x - HALO)]
+
+    def finish(index, along_y):
+        row = places[index]
         coefficients = weights(rows, row)
         mask[index] = jnp.broadcast_to(rows[row, FLAG : FLAG + 1, :], mask.shape[1:])
         for start, stop in CHUNKS:
             span = slice(start, stop)
-            centre = rows[row, span, :]
-            along_x = [rows[row + d, span, :] for d in (-1, -2, 1, 2)]
-            edge = shifted(around[0, span, :], -GROUP * row - GROUP // 2)
-            value = advance(centre, along_x, beside(centre, edge, lane), coefficients)
-            put(out, bins, index, span, value)
+            centre = cells(rows[row, span, :])
+            along_x = [cells(rows[row + d, span, :]) for d in (-1, -2, 1, 2)]
+            beside = [cells(value[span]) for value in along_y]
+            put(out, bins, index, span, advance(centre, along_x, beside, coefficients))
+
+    jobs = [(lambda row=row: rows[row], lambda: around[0], row) for row in places]
+    pl.run_scoped(lambda *refs: travel(jobs, moves, refs, finish), *travellers())
     matrices = (blocks, tails, losses)
     pl.run_scoped(
         lambda *refs: four_rows(bins, 0, matrices, refs, out, mask, change),
@@ -411,7 +474,7 @@
 
 
 def outer_kernel(
-    rows, edges, before, after, around, from_left, from_right, middle, blocks, tails, losses,
+    rows, edges, before, after, around, from_left, from_right, middle, moves, blocks, tails, losses,
     out, left, right, field, bins, change, mask, second,
 ):
     rows_x = rows.shape[0]
@@ -429,38 +492,46 @@
             return right, x - rows_x
         return rows, x
 
-    def edge_of(x, span):
+    def outer_columns(x):
         if x < 0:
-            return shifted(left[HALO, span, :], -GROUP * (x + rows_x) - GROUP // 2)
+            return (lambda: left[HALO]), x + rows_x
         if x >= rows_x:
-            return shifted(right[HALO, span, :], -GROUP * (x - rows_x) - GROUP // 2)
-        return shifted(around[0, span, :], -GROUP * x - GROUP // 2)
+            return (lambda: right[HALO]), x - rows_x
+        return (lambda: around[0]), x
 
     reach = HALO // 2
-    for x in list(range(-reach, reach)) + list(range(rows_x - reach, rows_x + reach)):
+    places = list(range(-reach, reach)) + list(range(rows_x - reach, rows_x + reach))
+
+    def job(x):
+        tile, row = column(x)
+        return (lambda: tile[row], *outer_columns(x))
+
+    def first_step(index, beside):
+        x = places[index]
         tile, row = column(x)
         coefficients = weights(tile, row)
         mask[x + reach] = jnp.broadcast_to(tile[row, FLAG : FLAG + 1, :], mask.shape[1:])
         for start, stop in CHUNKS:
             span = slice(start, stop)
-            centre = tile[row, span, :]
+            centre = cells(tile[row, span, :])
             along_x = []
             for d in (-1, -2, 1, 2):
                 other, at = column(x + d)
-                along_x.append(other[at, span, :])
-            value = advance(
-                centre, along_x, beside(centre, edge_of(x, span), lane), coefficients
-            )
-            put(field, bins, x + reach, span, value)
+                along_x.append(cells(other[at, span, :]))
+            along_y = [cells(value[span]) for value in beside]
+            put(field, bins, x + reach, span, advance(centre, along_x, along_y, coefficients))
+
+    jobs = [job(x) for x in places]
+    pl.run_scoped(lambda *refs: travel(jobs, moves, refs, first_step), *travellers())
     coefficients = weights(around, 0)
     mask[outside] = jnp.broadcast_to(around[0, FLAG : FLAG + 1, :], mask.shape[1:])
     inside = lane % GROUP
     half = GROUP // 2
     for start, stop in CHUNKS:
         span = slice(start, stop)
-        lower, upper = before[span, :].astype(F32), after[span, :].astype(F32)
-        first, last = edges[0, span, :], edges[1, span, :]
-        centre = around[0, span, :]
+        lower, upper = cells(before[span, :].astype(F32)), cells(after[span, :].astype(F32))
+        first, last = cells(edges[0, span, :]), cells(edges[1, span, :])
+        centre = cells(around[0, span, :])
         along_y = (
             jnp.where(
                 inside < half + LEV,
@@ -475,7 +546,9 @@
             ),
             jnp.where(inside < half, first, upper),
         )
-        beyond = jnp.where(lane >= LANES // 2, left[HALO, span, :], right[HALO, span, :])
+        beyond = jnp.where(
+            lane >= LANES // 2, cells(left[HALO, span, :]), cells(right[HALO, span, :])
+        )
         along_x = (
             shifted(jnp.where(lane >= LANES - GROUP, beyond, centre), GROUP),
             shifted(jnp.where(lane >= LANES - 2 * GROUP, beyond, centre), 2 * GROUP),
@@ -489,28 +562,32 @@
         mask[index + HALO] = jnp.broadcast_to(rows[row, FLAG : FLAG + 1, :], mask.shape[1:])
     matrices = (blocks, tails, losses)
 
-    def collisions(*refs):
+    def first_collisions(*refs):
         one_row(bins, outside, matrices, refs, field, mask, change)
 
         @pl.loop(0, 2)
         def _(step):
             four_rows(bins, rows_x * step, matrices, refs, field, mask, change)
 
-        for x in range(rows_x):
-            coefficients = weights(rows, x)
-            for start, stop in CHUNKS:
-                span = slice(start, stop)
-                centre = field[x + reach, span, :]
-                along_x = [field[x + reach + d, span, :] for d in (-1, -2, 1, 2)]
-                edge = shifted(field[outside, span, :], -GROUP * x - GROUP // 2)
-                value = advance(centre, along_x, beside(centre, edge, lane), coefficients)
-                put(second, bins, x + reach, span, value)
-
+    def second_step(x, beside):
+        coefficients = weights(rows, x)
+        for start, stop in CHUNKS:
+            span = slice(start, stop)
+            centre = cells(field[x + reach, span, :])
+            along_x = [cells(field[x + reach + d, span, :]) for d in (-1, -2, 1, 2)]
+            along_y = [cells(value[span]) for value in beside]
+            put(second, bins, x + reach, span, advance(centre, along_x, along_y, coefficients))
+
+    def second_collisions(*refs):
         @pl.loop(0, rows_x // 4)
         def _(step):
             four_rows(bins, reach + 4 * step, matrices, refs, second, mask, change)
 
-    pl.run_scoped(collisions, *accumulators(LOOK + 2, tails.shape[0], losses.shape[0]))
+    shapes = accumulators(LOOK + 2, tails.shape[0], losses.shape[0])
+    pl.run_scoped(first_collisions, *shapes)
+    later = [(lambda x=x: field[x + reach], lambda: field[outside], x) for x in range(rows_x)]
+    pl.run_scoped(lambda *refs: travel(later, moves, refs, second_step), *travellers())
+    pl.run_scoped(second_collisions, *shapes)
     flat = out.reshape(out.shape[0] * rows_x, LANES)
     for x in range(rows_x):
         for member in range(CLASSES):
@@ -518,17 +595,20 @@
             flat[span, :] = second[x + reach, OFF[member] : OFF[member] + BINS, :]
 
 
-def call(kernel, outs, scratch, *arguments, scalars=0, flops=0):
+def call(kernel, outs, scratch, *arguments, scalars=0, direct=0, flops=0):
     vmem = pl.BlockSpec(memory_space=pltpu.VMEM)
     smem = pl.BlockSpec(memory_space=pltpu.SMEM)
+    hbm = pl.BlockSpec(memory_space=pltpu.HBM)
     shapes = tuple(jax.ShapeDtypeStruct(shape, dtype) for shape, dtype in outs)
     moved = sum(a.size * a.dtype.itemsize for a in arguments)
+    staged = len(arguments) - scalars - direct
+    waits = [pltpu.SemaphoreType.DMA((direct + CLASSES - 1,))] if direct else []
     return pl.pallas_call(
         kernel,
         out_shape=shapes,
-        in_specs=[smem] * scalars + [vmem] * (len(arguments) - scalars),
+        in_specs=[smem] * scalars + [hbm] * direct + [vmem] * staged,
         out_specs=tuple(vmem for _ in shapes),
-        scratch_shapes=[pltpu.VMEM(shape, F32) for shape in scratch],
+        scratch_shapes=[pltpu.VMEM(shape, F32) for shape in scratch] + waits,
         compiler_params=pltpu.CompilerParams(vmem_limit_bytes=VMEM_LIMIT),
         cost_estimate=pl.CostEstimate(flops=flops, bytes_accessed=moved, transcendentals=0),
     )(*arguments)
@@ -544,15 +624,22 @@
 def per_device(bin_state, courant_x, courant_y, cloudy_order, block_count, gain_kernel, loss_rate):
     rows_x = bin_state.shape[1]
     tile = (ROWS, LANES)
-    rows, edges, low, high = call(
+    rows, edges, low, high, gain, loss = call(
         stage_kernel,
-        [((rows_x, *tile), F32), ((2, *tile), F32), (tile, BF16), (tile, BF16)],
-        [],
-        cloudy_order, block_count, bin_state, courant_x, courant_y,
-        scalars=2,
+        [
+            ((rows_x, *tile), F32),
+            ((2, *tile), F32),
+            (tile, BF16),
+            (tile, BF16),
+            (gain_kernel.shape, BF16),
+            (loss_rate.shape, BF16),
+        ],
+        [bin_state.shape, courant_x.shape, courant_y.shape],
+        cloudy_order, block_count, bin_state, courant_x, courant_y, gain_kernel, loss_rate,
+        scalars=2, direct=5,
     )
     before, after = exchange("gy", high, low)
-    matrices = prepare(gain_kernel, loss_rate)
+    *matrices, moves = prepare(gain, loss)
     around, to_right, to_left = call(
         widen_kernel,
         [((1, *tile), F32), ((HALO + 1, *tile), BF16), ((HALO + 1, *tile), BF16)],
@@ -565,7 +652,7 @@
         inner_kernel,
         [((inner, *tile), F32)],
         [(inner, *tile), (4, *tile), (inner, 8, LANES)],
-        rows, around, *matrices,
+        rows, around, moves, *matrices,
         flops=5 * 10**9,
     )
     total = rows_x + HALO + 1
@@ -581,7 +668,7 @@
             (total, 8, LANES),
             (total, *tile),
         ],
-        rows, edges, before, after, around, from_left, from_right, middle, *matrices,
+        rows, edges, before, after, around, from_left, from_right, middle, moves, *matrices,
         flops=20 * 10**9,
     )
     return out

time: 35.6 us -> 34.7 us (0.975)
  Pallas kernels: 18.8 us -> 16.7 us
  waiting for transfers between devices: 4.91 us -> 5.81 us
    pallas_call x4, Pallas kernels: 16.7 us -> 14.5 us  [call(): pl.pallas_call(kernel, out_shape=shapes, in_specs=[smem] * scalars + [hbm...]
    ppermute x4, waiting for transfers between devices: 4.91 us -> 5.81 us  [exchange(): return (lax.ppermute(upward, axis, up), lax.ppermute(downward, axis, down))]
  transfers between devices with their start and end apart: 4 -> 4, of which waited for: 2 -> 3; matrix products, arithmetic and copies ran while one was open for 0% -> 0% of each run, Pallas kernels for 12% -> 13%
where the time goes in v3:
time: 34.7 us; the launch traced here: 34.3 us
  Pallas kernels  16.7 us (48%)
  starting transfers between devices  5.92 us (17%)
  waiting for transfers between devices  5.81 us (17%)
  local copies, waits for them, and re-layouts  5.14 us (15%)
  between operations  0.7 us (2%)
    pallas_call x4, Pallas kernels, call(): pl.pallas_call(kernel, out_shape=shapes, in_specs=[smem] * scalars + [hbm...  14.5 us
    ppermute x4, starting transfers between devices, exchange(): return (lax.ppermute(upward, axis, up), lax.ppermute(downward, axis, down))  5.92 us
    ppermute x4, waiting for transfers between devices, exchange(): return (lax.ppermute(upward, axis, up), lax.ppermute(downward, axis, down))  5.81 us
    unnamed x12, local copies, waits for them, and re-layouts  5.14 us
    pallas_call x1, Pallas kernels, prepare(): pl.pallas_call(prepare_kernel, out_shape=(jax.ShapeDtypeStruct((NG, BINS...  2.21 us
  transfers between devices with their start and end apart: 4, of which 3 were waited for; matrix products, arithmetic and copies ran while one was open for 0% of the time, Pallas kernels for 13%

profile of v3, /device:TPU:1, one launch (start us, length us, event | category | flops | bytes accessed | tf_op | source)
XLA Modules:
  0.0 34.3 jit_solution(8369520355988642216)
XLA Ops:
  0.7 0.0 copy-start
  0.7 1.2 %copy-done = bf16[10,33,1089]{2,1,0:T(8,128)(2,1)S(1)} copy-done((bf16[10,33,1089]{2,1,0:T(8,128)(2,1)S(1)}, bf16[10,33,1089]{2,1,0:T(8,128)(2,1)}, u32[]{:S(2)}) %copy-start) | copy-done | bytes 718764
  1.8 0.0 copy-start.1
  1.8 1.0 %copy-done.1 = f32[132,8,128]{2,1,0:T(8,128)S(1)} copy-done((f32[132,8,128]{2,1,0:T(8,128)S(1)}, f32[132,8,128]{2,1,0:T(8,128)}, u32[]{:S(2)}) %copy-start.1) | copy-done | bytes 540696
  2.9 0.0 copy-start.2
  2.9 0.9 %copy-done.2 = bf16[10,33,33]{2,1,0:T(8,128)(2,1)S(1)} copy-done((bf16[10,33,33]{2,1,0:T(8,128)(2,1)S(1)}, bf16[10,33,33]{2,1,0:T(8,128)(2,1)}, u32[]{:S(2)}) %copy-start.2) | copy-done | bytes 21804
  3.8 0.0 copy-start.3
  3.8 0.7 %copy-done.3 = f32[8,128]{1,0:T(8,128)S(1)} copy-done((f32[8,128]{1,0:T(8,128)S(1)}, f32[8,128]{1,0:T(8,128)}, u32[]{:S(2)}) %copy-start.3) | copy-done | bytes 4120
  4.5 0.0 copy-start.4
  4.5 0.7 %copy-done.4 = f32[8,128]{1,0:T(8,128)S(1)} copy-done((f32[8,128]{1,0:T(8,128)S(1)}, f32[8,128]{1,0:T(8,128)}, u32[]{:S(2)}) %copy-start.4) | copy-done | bytes 4120
  5.2 0.0 copy-start.5
  5.2 0.7 %copy-done.5 = s32[1,1,8]{2,1,0:T(1,128)S(1)} copy-done((s32[1,1,8]{2,1,0:T(1,128)S(1)}, s32[1,1,8]{2,1,0:T(1,128)}, u32[]{:S(2)}) %copy-start.5) | copy-done | bytes 56
  5.8 2.1 %shard_map.73 = (f32[8,176,128]{2,1,0:T(8,128)S(1)}, f32[2,176,128]{2,1,0:T(8,128)S(1)}, bf16[176,128]{1,0:T(8,128)(2,1)S(1)}, bf16[176,128]{1,0:T(8,128)(2,1)S(...) custom-call(s32[1,1,8]{2,1,0:T(1,128)S(1)} %copy-done.5, s32[1,1]{1,0:T(1,128)S(6)} %copy.8.count, ...), custom_call_target="tpu_custom_call" | custom-call | bytes 1289420 | tf_op jit(solution)/shard_map/pallas_call | solution.py:606
  7.9 2.1 %collective-permute-start = (bf16[176,128]{1,0:T(8,128)(2,1)S(1)}, bf16[176,128]{1,0:T(8,128)(2,1)S(1)}, u32[]{:S(2)}, u32[]{:S(2)}) collective-permute-start(bf16[176,128]{1,0:T(8,128)(2,1)S(1)} %get-tuple-element.20), channel_id=1, source_target_pairs={{0,1},{1,2},{2,3},{3,0},{4,5},{5,6},{6,7},{7,4},{8,9},{9,10},{10,1... | collective-permute-start | bytes 135176 | tf_op jit(solution)/shard_map/ppermute | solution.py:621
  10.0 1.0 %collective-permute-start.1 = (bf16[176,128]{1,0:T(8,128)(2,1)S(1)}, bf16[176,128]{1,0:T(8,128)(2,1)S(1)}, u32[]{:S(2)}, u32[]{:S(2)}) collective-permute-start(bf16[176,128]{1,0:T(8,128)(2,1)S(1)} %get-tuple-element.21), channel_id=1, source_target_pairs={{1,0},{2,1},{3,2},{0,3},{5,4},{6,5},{7,6},{4,7},{9,8},{10,9},{11,1... | collective-permute-start | bytes 135176 | tf_op jit(solution)/shard_map/ppermute | solution.py:621
  11.0 2.2 %shard_map.75 = (bf16[5,1056,256]{2,1,0:T(8,128)(2,1)S(1)}, bf16[208,256]{1,0:T(8,128)(2,1)S(1)}, bf16[176,256]{1,0:T(8,128)(2,1)S(1)}, bf16[2,368,256]{2,1,0:T(8,128)(2,1)S(1)}) custom-call(bf16[10,33,1089]{2,1,0:T(8,128)(2,1)S(1)} %get-tuple-element.25.gain, bf16[10,33,33]{2,1,0:T(8,128)(2,1)S(1)} %get-tuple-element.26.loss), custom_call_target="tpu_custom_call" | custom-call | flops 2000000000 | bytes 4194304 | tf_op jit(solution)/shard_map/pallas_call | solution.py:127
  13.2 0.0 collective-permute-done.before
  13.2 0.2 collective-permute-done.1.after
  13.4 0.1 shard_map.74
  13.5 2.8 %collective-permute-start.2 = (bf16[5,176,128]{2,1,0:T(8,128)(2,1)S(1)}, bf16[5,176,128]{2,1,0:T(8,128)(2,1)S(1)}, u32[]{:S(2)}, u32[]{:S(2)}) collective-permute-start(bf16[5,176,128]{2,1,0:T(8,128)(2,1)S(1)} %get-tuple-element.23), channel_id=1, source_target_pairs={{0,4},{4,8},{8,12},{12,16},{16,20},{20,24},{24,28},{28,0},{1,5},{5... | collective-permute-start | bytes 675848 | tf_op jit(solution)/shard_map/ppermute | solution.py:621
  16.3 0.0 collective-permute-start.3
  16.3 2.1 %shard_map.76.middle = f32[4,176,128]{2,1,0:T(8,128)S(1)} custom-call(f32[8,176,128]{2,1,0:T(8,128)S(1)} %get-tuple-element.18.rows, f32[1,176,128]{2,1,0:T(8,128)S(1)} %get-tuple-element.22.around, bf16[2,368,256]{2,1,0:T(8,128)(2,1)S(1)} %get-tuple-element.27.moves, bf16[5,1056,256]{2,1,0:T(8,128)(2,1)S(1)} %get-tuple-element.28.blocks, ...), custom_call_target="tpu_custom_call" | custom-call | flops 5000000000 | bytes 4087808 | tf_op jit(solution)/shard_map/pallas_call | solution.py:606
  18.4 0.8 %collective-permute-done.2.from_left = bf16[5,176,128]{2,1,0:T(8,128)(2,1)S(1)} collective-permute-done((bf16[5,176,128]{2,1,0:T(8,128)(2,1)S(1)}, bf16[5,176,128]{2,1,0:T(8,128)(2,1)S(1)}, u32[]{:S(2)}, u32[]{:S(2)}) %collective-permute-start.2) | collective-permute-done | bytes 225312 | tf_op jit(solution)/shard_map/ppermute | solution.py:621
  19.3 4.8 %collective-permute-done.3.from_right = bf16[5,176,128]{2,1,0:T(8,128)(2,1)S(1)} collective-permute-done((bf16[5,176,128]{2,1,0:T(8,128)(2,1)S(1)}, bf16[5,176,128]{2,1,0:T(8,128)(2,1)S(1)}, u32[]{:S(2)}, u32[]{:S(2)}) %collective-permute-start.3) | collective-permute-done | bytes 225312 | tf_op jit(solution)/shard_map/ppermute | solution.py:621
  24.1 10.2 %shard_map.77 = f32[132,8,128]{2,1,0:T(8,128)} custom-call(f32[8,176,128]{2,1,0:T(8,128)S(1)} %get-tuple-element.18.rows, f32[2,176,128]{2,1,0:T(8,128)S(1)} %get-tuple-element.19.edges, bf16[176,128]{1,0:T(8,128)(2,1)S(1)} %collective-permute-done.before, bf16[176,128]{1,0:T(8,128)(2,1)S(1)} %collective-permute-done.1.after, ...), custom_call_target="tpu_custom_call" | custom-call | flops 20000000000 | bytes 5169152 | tf_op jit(solution)/shard_map/pallas_call | solution.py:606
Async XLA Ops:
  0.7 1.2 %copy-start = (bf16[10,33,1089]{2,1,0:T(8,128)(2,1)S(1)}, bf16[10,33,1089]{2,1,0:T(8,128)(2,1)}, u32[]{:S(2)}) copy-start(bf16[10,33,1089]{2,1,0:T(8,128)(2,1)} %gain_hbm.1) | copy-start | bytes 2156224
  1.8 1.0 %copy-start.1 = (f32[132,8,128]{2,1,0:T(8,128)S(1)}, f32[132,8,128]{2,1,0:T(8,128)}, u32[]{:S(2)}) copy-start(f32[132,8,128]{2,1,0:T(8,128)} %state_hbm.1) | copy-start | bytes 1622020
  2.9 0.9 %copy-start.2 = (bf16[10,33,33]{2,1,0:T(8,128)(2,1)S(1)}, bf16[10,33,33]{2,1,0:T(8,128)(2,1)}, u32[]{:S(2)}) copy-start(bf16[10,33,33]{2,1,0:T(8,128)(2,1)} %loss_hbm.1) | copy-start | bytes 65344
  3.8 0.7 %copy-start.3 = (f32[8,128]{1,0:T(8,128)S(1)}, f32[8,128]{1,0:T(8,128)}, u32[]{:S(2)}) copy-start(f32[8,128]{1,0:T(8,128)} %courant_x_hbm.1) | copy-start | bytes 12292
  4.5 0.7 %copy-start.4 = (f32[8,128]{1,0:T(8,128)S(1)}, f32[8,128]{1,0:T(8,128)}, u32[]{:S(2)}) copy-start(f32[8,128]{1,0:T(8,128)} %courant_y_hbm.1) | copy-start | bytes 12292
  5.2 0.7 %copy-start.5 = (s32[1,1,8]{2,1,0:T(1,128)S(1)}, s32[1,1,8]{2,1,0:T(1,128)}, u32[]{:S(2)}) copy-start(s32[1,1,8]{2,1,0:T(1,128)} %order.1) | copy-start | bytes 100
  7.9 5.3 %collective-permute-start = (bf16[176,128]{1,0:T(8,128)(2,1)S(1)}, bf16[176,128]{1,0:T(8,128)(2,1)S(1)}, u32[]{:S(2)}, u32[]{:S(2)}) collective-permute-start(bf16[176,128]{1,0:T(8,128)(2,1)S(1)} %get-tuple-element.20), channel_id=1, source_target_pairs={{0,1},{1,2},{2,3},{3,0},{4,5},{5,6},{6,7},{7,4},{8,9},{9,10},{10,1... | collective-permute-start | bytes 135176 | tf_op jit(solution)/shard_map/ppermute | solution.py:621
  10.0 3.4 %collective-permute-start.1 = (bf16[176,128]{1,0:T(8,128)(2,1)S(1)}, bf16[176,128]{1,0:T(8,128)(2,1)S(1)}, u32[]{:S(2)}, u32[]{:S(2)}) collective-permute-start(bf16[176,128]{1,0:T(8,128)(2,1)S(1)} %get-tuple-element.21), channel_id=1, source_target_pairs={{1,0},{2,1},{3,2},{0,3},{5,4},{6,5},{7,6},{4,7},{9,8},{10,9},{11,1... | collective-permute-start | bytes 135176 | tf_op jit(solution)/shard_map/ppermute | solution.py:621
  13.5 5.7 %collective-permute-start.2 = (bf16[5,176,128]{2,1,0:T(8,128)(2,1)S(1)}, bf16[5,176,128]{2,1,0:T(8,128)(2,1)S(1)}, u32[]{:S(2)}, u32[]{:S(2)}) collective-permute-start(bf16[5,176,128]{2,1,0:T(8,128)(2,1)S(1)} %get-tuple-element.23), channel_id=1, source_target_pairs={{0,4},{4,8},{8,12},{12,16},{16,20},{20,24},{24,28},{28,0},{1,5},{5... | collective-permute-start | bytes 675848 | tf_op jit(solution)/shard_map/ppermute | solution.py:621
  16.3 7.7 %collective-permute-start.3 = (bf16[5,176,128]{2,1,0:T(8,128)(2,1)S(1)}, bf16[5,176,128]{2,1,0:T(8,128)(2,1)S(1)}, u32[]{:S(2)}, u32[]{:S(2)}) collective-permute-start(bf16[5,176,128]{2,1,0:T(8,128)(2,1)S(1)} %get-tuple-element.24), channel_id=1, source_target_pairs={{4,0},{8,4},{12,8},{16,12},{20,16},{24,20},{28,24},{0,28},{5,1},{9... | collective-permute-start | bytes 675848 | tf_op jit(solution)/shard_map/ppermute | solution.py:621

commit v4 on v3

--- a/solution.py
+++ b/solution.py
@@ -380,8 +380,8 @@
 
 
 def stage_kernel(
-    order, count, state_hbm, courant_x_hbm, courant_y_hbm, gain_hbm, loss_hbm,
-    rows, edges, low, high, gain, loss, state, courant_x, courant_y, arrived,
+    count, order_hbm, state_hbm, courant_x_hbm, courant_y_hbm, gain_hbm, loss_hbm,
+    rows, edges, low, high, gain, loss, state, courant_x, courant_y, order, arrived,
 ):
     rows_x = state.shape[1]
     flat = state.reshape(state.shape[0] * rows_x, LANES)
@@ -390,6 +390,7 @@
         for member in range(CLASSES)
     ]
     pieces += [(courant_x_hbm, courant_x), (courant_y_hbm, courant_y)]
+    pieces += [(order_hbm, order)]
     pieces += [(gain_hbm, gain), (loss_hbm, loss)]
     copies = [
         pltpu.make_async_copy(source, target, arrived.at[number])
@@ -596,22 +597,23 @@
 
 
 def call(kernel, outs, scratch, *arguments, scalars=0, direct=0, flops=0):
+    smem = pl.BlockSpec(memory_space=pltpu.SMEM)
     vmem = pl.BlockSpec(memory_space=pltpu.VMEM)
-    smem = pl.BlockSpec(memory_space=pltpu.SMEM)
     hbm = pl.BlockSpec(memory_space=pltpu.HBM)
     shapes = tuple(jax.ShapeDtypeStruct(shape, dtype) for shape, dtype in outs)
     moved = sum(a.size * a.dtype.itemsize for a in arguments)
-    staged = len(arguments) - scalars - direct
-    waits = [pltpu.SemaphoreType.DMA((direct + CLASSES - 1,))] if direct else []
+    own = [pltpu.VMEM(piece, F32) if isinstance(piece, tuple) else piece for piece in scratch]
+    staged = scalars + direct
+    held = [pltpu.with_memory_space_constraint(a, pltpu.HBM) for a in arguments[scalars:staged]]
     return pl.pallas_call(
         kernel,
         out_shape=shapes,
-        in_specs=[smem] * scalars + [hbm] * direct + [vmem] * staged,
+        in_specs=[smem] * scalars + [hbm] * direct + [vmem] * (len(arguments) - staged),
         out_specs=tuple(vmem for _ in shapes),
-        scratch_shapes=[pltpu.VMEM(shape, F32) for shape in scratch] + waits,
+        scratch_shapes=own,
         compiler_params=pltpu.CompilerParams(vmem_limit_bytes=VMEM_LIMIT),
         cost_estimate=pl.CostEstimate(flops=flops, bytes_accessed=moved, transcendentals=0),
-    )(*arguments)
+    )(*arguments[:scalars], *held, *arguments[staged:])
 
 
 def exchange(axis, upward, downward):
@@ -634,9 +636,15 @@
             (gain_kernel.shape, BF16),
             (loss_rate.shape, BF16),
         ],
-        [bin_state.shape, courant_x.shape, courant_y.shape],
-        cloudy_order, block_count, bin_state, courant_x, courant_y, gain_kernel, loss_rate,
-        scalars=2, direct=5,
+        [
+            bin_state.shape,
+            courant_x.shape,
+            courant_y.shape,
+            pltpu.SMEM(cloudy_order.shape, jnp.int32),
+            pltpu.SemaphoreType.DMA((CLASSES + 5,)),
+        ],
+        block_count, cloudy_order, bin_state, courant_x, courant_y, gain_kernel, loss_rate,
+        scalars=1, direct=6,
     )
     before, after = exchange("gy", high, low)
     *matrices, moves = prepare(gain, loss)

time: 34.7 us -> 28.9 us (0.83)
  local copies, waits for them, and re-layouts: 5.14 us -> 0 us
  Pallas kernels: 16.7 us -> 16.2 us
    unnamed x12 -> x0, local copies, waits for them, and re-layouts: 5.14 us -> none
    pallas_call x4, Pallas kernels: 14.5 us -> 14 us  [call(): pl.pallas_call(kernel, out_shape=shapes, in_specs=[smem] * scalars + [hbm...]
  transfers between devices with their start and end apart: 4 -> 4, of which waited for: 3 -> 3; matrix products, arithmetic and copies ran while one was open for 0% -> 0% of each run, Pallas kernels for 13% -> 15%
where the time goes in v4:
time: 28.9 us; the launch traced here: 28.6 us
  Pallas kernels  16.2 us (56%)
  starting transfers between devices  5.92 us (20%)
  waiting for transfers between devices  5.82 us (20%)
  between operations  0.69 us (2%)
    pallas_call x4, Pallas kernels, call(): pl.pallas_call(kernel, out_shape=shapes, in_specs=[smem] * scalars + [hbm...  14 us
    ppermute x4, starting transfers between devices, exchange(): return (lax.ppermute(upward, axis, up), lax.ppermute(downward, axis, down))  5.92 us
    ppermute x4, waiting for transfers between devices, exchange(): return (lax.ppermute(upward, axis, up), lax.ppermute(downward, axis, down))  5.82 us
    pallas_call x1, Pallas kernels, prepare(): pl.pallas_call(prepare_kernel, out_shape=(jax.ShapeDtypeStruct((NG, BINS...  2.2 us
  transfers between devices with their start and end apart: 4, of which 3 were waited for; matrix products, arithmetic and copies ran while one was open for 0% of the time, Pallas kernels for 15%

profile of v4, /device:TPU:1, one launch (start us, length us, event | category | flops | bytes accessed | tf_op | source)
XLA Modules:
  0.0 28.6 jit_solution(14472430269886335895)
XLA Ops:
  0.7 1.6 %shard_map.73 = (f32[8,176,128]{2,1,0:T(8,128)S(1)}, f32[2,176,128]{2,1,0:T(8,128)S(1)}, bf16[176,128]{1,0:T(8,128)(2,1)S(1)}, bf16[176,128]{1,0:T(8,128)(2,1)S(...) custom-call(s32[1,1]{1,0:T(1,128)S(6)} %copy.8.count, s32[1,1,8]{2,1,0:T(1,128)} %order_hbm.1, ...), custom_call_target="tpu_custom_call" | custom-call | bytes 1289420 | tf_op jit(solution)/shard_map/pallas_call | solution.py:608
  2.3 2.1 %collective-permute-start = (bf16[176,128]{1,0:T(8,128)(2,1)S(1)}, bf16[176,128]{1,0:T(8,128)(2,1)S(1)}, u32[]{:S(2)}, u32[]{:S(2)}) collective-permute-start(bf16[176,128]{1,0:T(8,128)(2,1)S(1)} %get-tuple-element.20), channel_id=1, source_target_pairs={{0,1},{1,2},{2,3},{3,0},{4,5},{5,6},{6,7},{7,4},{8,9},{9,10},{10,1... | collective-permute-start | bytes 135176 | tf_op jit(solution)/shard_map/ppermute | solution.py:623
  4.4 1.0 %collective-permute-start.1 = (bf16[176,128]{1,0:T(8,128)(2,1)S(1)}, bf16[176,128]{1,0:T(8,128)(2,1)S(1)}, u32[]{:S(2)}, u32[]{:S(2)}) collective-permute-start(bf16[176,128]{1,0:T(8,128)(2,1)S(1)} %get-tuple-element.21), channel_id=1, source_target_pairs={{1,0},{2,1},{3,2},{0,3},{5,4},{6,5},{7,6},{4,7},{9,8},{10,9},{11,1... | collective-permute-start | bytes 135176 | tf_op jit(solution)/shard_map/ppermute | solution.py:623
  5.4 2.2 %shard_map.75 = (bf16[5,1056,256]{2,1,0:T(8,128)(2,1)S(1)}, bf16[208,256]{1,0:T(8,128)(2,1)S(1)}, bf16[176,256]{1,0:T(8,128)(2,1)S(1)}, bf16[2,368,256]{2,1,0:T(8,128)(2,1)S(1)}) custom-call(bf16[10,33,1089]{2,1,0:T(8,128)(2,1)S(1)} %get-tuple-element.25.gain, bf16[10,33,33]{2,1,0:T(8,128)(2,1)S(1)} %get-tuple-element.26.loss), custom_call_target="tpu_custom_call" | custom-call | flops 2000000000 | bytes 4194304 | tf_op jit(solution)/shard_map/pallas_call | solution.py:127
  7.6 0.0 collective-permute-done.before
  7.6 0.2 collective-permute-done.1.after
  7.8 0.1 shard_map.74
  7.9 2.8 %collective-permute-start.2 = (bf16[5,176,128]{2,1,0:T(8,128)(2,1)S(1)}, bf16[5,176,128]{2,1,0:T(8,128)(2,1)S(1)}, u32[]{:S(2)}, u32[]{:S(2)}) collective-permute-start(bf16[5,176,128]{2,1,0:T(8,128)(2,1)S(1)} %get-tuple-element.23), channel_id=1, source_target_pairs={{0,4},{4,8},{8,12},{12,16},{16,20},{20,24},{24,28},{28,0},{1,5},{5... | collective-permute-start | bytes 675848 | tf_op jit(solution)/shard_map/ppermute | solution.py:623
  10.7 0.0 collective-permute-start.3
  10.7 2.1 %shard_map.76.middle = f32[4,176,128]{2,1,0:T(8,128)S(1)} custom-call(f32[8,176,128]{2,1,0:T(8,128)S(1)} %get-tuple-element.18.rows, f32[1,176,128]{2,1,0:T(8,128)S(1)} %get-tuple-element.22.around, bf16[2,368,256]{2,1,0:T(8,128)(2,1)S(1)} %get-tuple-element.27.moves, bf16[5,1056,256]{2,1,0:T(8,128)(2,1)S(1)} %get-tuple-element.28.blocks, ...), custom_call_target="tpu_custom_call" | custom-call | flops 5000000000 | bytes 4087808 | tf_op jit(solution)/shard_map/pallas_call | solution.py:608
  12.8 0.8 %collective-permute-done.2.from_left = bf16[5,176,128]{2,1,0:T(8,128)(2,1)S(1)} collective-permute-done((bf16[5,176,128]{2,1,0:T(8,128)(2,1)S(1)}, bf16[5,176,128]{2,1,0:T(8,128)(2,1)S(1)}, u32[]{:S(2)}, u32[]{:S(2)}) %collective-permute-start.2) | collective-permute-done | bytes 225312 | tf_op jit(solution)/shard_map/ppermute | solution.py:623
  13.6 4.8 %collective-permute-done.3.from_right = bf16[5,176,128]{2,1,0:T(8,128)(2,1)S(1)} collective-permute-done((bf16[5,176,128]{2,1,0:T(8,128)(2,1)S(1)}, bf16[5,176,128]{2,1,0:T(8,128)(2,1)S(1)}, u32[]{:S(2)}, u32[]{:S(2)}) %collective-permute-start.3) | collective-permute-done | bytes 225312 | tf_op jit(solution)/shard_map/ppermute | solution.py:623
  18.4 10.2 %shard_map.77 = f32[132,8,128]{2,1,0:T(8,128)} custom-call(f32[8,176,128]{2,1,0:T(8,128)S(1)} %get-tuple-element.18.rows, f32[2,176,128]{2,1,0:T(8,128)S(1)} %get-tuple-element.19.edges, bf16[176,128]{1,0:T(8,128)(2,1)S(1)} %collective-permute-done.before, bf16[176,128]{1,0:T(8,128)(2,1)S(1)} %collective-permute-done.1.after, ...), custom_call_target="tpu_custom_call" | custom-call | flops 20000000000 | bytes 5169152 | tf_op jit(solution)/shard_map/pallas_call | solution.py:608
Async XLA Ops:
  2.3 5.3 %collective-permute-start = (bf16[176,128]{1,0:T(8,128)(2,1)S(1)}, bf16[176,128]{1,0:T(8,128)(2,1)S(1)}, u32[]{:S(2)}, u32[]{:S(2)}) collective-permute-start(bf16[176,128]{1,0:T(8,128)(2,1)S(1)} %get-tuple-element.20), channel_id=1, source_target_pairs={{0,1},{1,2},{2,3},{3,0},{4,5},{5,6},{6,7},{7,4},{8,9},{9,10},{10,1... | collective-permute-start | bytes 135176 | tf_op jit(solution)/shard_map/ppermute | solution.py:623
  4.4 3.4 %collective-permute-start.1 = (bf16[176,128]{1,0:T(8,128)(2,1)S(1)}, bf16[176,128]{1,0:T(8,128)(2,1)S(1)}, u32[]{:S(2)}, u32[]{:S(2)}) collective-permute-start(bf16[176,128]{1,0:T(8,128)(2,1)S(1)} %get-tuple-element.21), channel_id=1, source_target_pairs={{1,0},{2,1},{3,2},{0,3},{5,4},{6,5},{7,6},{4,7},{9,8},{10,9},{11,1... | collective-permute-start | bytes 135176 | tf_op jit(solution)/shard_map/ppermute | solution.py:623
  7.9 5.7 %collective-permute-start.2 = (bf16[5,176,128]{2,1,0:T(8,128)(2,1)S(1)}, bf16[5,176,128]{2,1,0:T(8,128)(2,1)S(1)}, u32[]{:S(2)}, u32[]{:S(2)}) collective-permute-start(bf16[5,176,128]{2,1,0:T(8,128)(2,1)S(1)} %get-tuple-element.23), channel_id=1, source_target_pairs={{0,4},{4,8},{8,12},{12,16},{16,20},{20,24},{24,28},{28,0},{1,5},{5... | collective-permute-start | bytes 675848 | tf_op jit(solution)/shard_map/ppermute | solution.py:623
  10.7 7.7 %collective-permute-start.3 = (bf16[5,176,128]{2,1,0:T(8,128)(2,1)S(1)}, bf16[5,176,128]{2,1,0:T(8,128)(2,1)S(1)}, u32[]{:S(2)}, u32[]{:S(2)}) collective-permute-start(bf16[5,176,128]{2,1,0:T(8,128)(2,1)S(1)} %get-tuple-element.24), channel_id=1, source_target_pairs={{4,0},{8,4},{12,8},{16,12},{20,16},{24,20},{28,24},{0,28},{5,1},{9... | collective-permute-start | bytes 675848 | tf_op jit(solution)/shard_map/ppermute | solution.py:623

commit v5 on v4

--- a/solution.py
+++ b/solution.py
@@ -22,6 +22,10 @@
 AUX = BINS
 FLAG = AUX + 4
 EDGE = 2 * LANES - GROUP
+DENSE = (0, BINS + 5, 2 * BINS + 5, 3 * BINS + 5)
+SENT = DENSE[3] + PAD
+REACH = HALO // 2
+CORNER = REACH * GROUP
 CHUNKS = tuple((OFF[member], OFF[member] + PAD) for member in range(CLASSES))
 VMEM_LIMIT = 24 << 20
 
@@ -433,20 +437,47 @@
         copy.wait()
 
 
-def widen_kernel(rows, before, after, around, to_right, to_left):
-    rows_x = rows.shape[0]
-    inner = lax.broadcasted_iota(jnp.int32, (ROWS, LANES), 1) % GROUP < GROUP // 2
-    near = jnp.where(
-        inner,
-        shifted(before[...].astype(F32), -GROUP // 2),
-        shifted(after[...].astype(F32), GROUP // 2),
-    )
-    around[0] = near
+def pack_kernel(rows, packed, dense):
+    for row in range(rows.shape[0]):
+        for (start, stop), first in zip(CHUNKS, DENSE):
+            dense[row, first : first + PAD, :] = rows[row, start:stop, :]
+        packed[row] = dense[row].astype(BF16)
+
+
+def widen_kernel(packed, before, after, around, to_right, to_left):
+    rows_x = packed.shape[0]
+    inner = lanes() % GROUP < GROUP // 2
+    block = lanes() // CORNER
+    corners = [None, None]
+    for member, (start, stop) in enumerate(CHUNKS):
+        near = jnp.where(
+            inner,
+            shifted(cells(before[start:stop].astype(F32)), -GROUP // 2),
+            shifted(cells(after[start:stop].astype(F32)), GROUP // 2),
+        )
+        around[0, start:stop, :] = near.reshape(PAD, LANES)
+        for side, first in enumerate((LANES - CORNER, 0)):
+            moved = shifted(near, CORNER * member - first)
+            old = corners[side]
+            corners[side] = moved if old is None else jnp.where(block == member, moved, old)
+    clear_gap(around)
     for index in range(HALO):
-        to_right[index] = rows[rows_x - HALO + index].astype(BF16)
-        to_left[index] = rows[index].astype(BF16)
-    to_right[HALO] = near.astype(BF16)
-    to_left[HALO] = near.astype(BF16)
+        span = slice(index * SENT, (index + 1) * SENT)
+        to_right[span, :] = packed[rows_x - HALO + index]
+        to_left[span, :] = packed[index]
+    for target, corner in zip((to_right, to_left), corners):
+        target[HALO * SENT :, :] = corner.reshape(PAD, LANES).astype(BF16)
+
+
+def unpack(sent, tiles, dense, first_lane):
+    for index in range(HALO):
+        dense[index] = sent[index * SENT : (index + 1) * SENT, :].astype(F32)
+        for (start, stop), first in zip(CHUNKS, DENSE):
+            tiles[index, start:stop, :] = dense[index, first : first + PAD, :]
+    corner = cells(sent[HALO * SENT :, :].astype(F32))
+    for member, (start, stop) in enumerate(CHUNKS):
+        moved = shifted(corner, first_lane - CORNER * member)
+        tiles[HALO, start:stop, :] = moved.reshape(PAD, LANES)
 
 
 def inner_kernel(rows, around, moves, blocks, tails, losses, out, bins, change, mask):
@@ -476,15 +507,14 @@
 
 def outer_kernel(
     rows, edges, before, after, around, from_left, from_right, middle, moves, blocks, tails, losses,
-    out, left, right, field, bins, change, mask, second,
+    out_hbm, left, right, field, bins, change, mask, second, dense, out, sent,
 ):
     rows_x = rows.shape[0]
     lane = lanes()
     outside = rows_x + HALO
-    for index in range(HALO + 1):
-        left[index] = from_left[index].astype(F32)
-        right[index] = from_right[index].astype(F32)
-    clear_gap(field, bins, second)
+    unpack(from_left, left, dense, LANES - CORNER)
+    unpack(from_right, right, dense, 0)
+    clear_gap(field, bins, second, left, right)
 
     def column(x):
         if x < 0:
@@ -590,13 +620,19 @@
     pl.run_scoped(lambda *refs: travel(later, moves, refs, second_step), *travellers())
     pl.run_scoped(second_collisions, *shapes)
     flat = out.reshape(out.shape[0] * rows_x, LANES)
-    for x in range(rows_x):
-        for member in range(CLASSES):
+    copies = []
+    for member in range(CLASSES):
+        for x in range(rows_x):
             span = pl.ds(member * BINS * rows_x + x, BINS, stride=rows_x)
             flat[span, :] = second[x + reach, OFF[member] : OFF[member] + BINS, :]
-
-
-def call(kernel, outs, scratch, *arguments, scalars=0, direct=0, flops=0):
+        part = pl.ds(member * BINS, BINS)
+        copies.append(pltpu.make_async_copy(out.at[part], out_hbm.at[part], sent.at[member]))
+        copies[-1].start()
+    for copy in copies:
+        copy.wait()
+
+
+def call(kernel, outs, scratch, *arguments, scalars=0, direct=0, flops=0, stored=False):
     smem = pl.BlockSpec(memory_space=pltpu.SMEM)
     vmem = pl.BlockSpec(memory_space=pltpu.VMEM)
     hbm = pl.BlockSpec(memory_space=pltpu.HBM)
@@ -609,7 +645,7 @@
         kernel,
         out_shape=shapes,
         in_specs=[smem] * scalars + [hbm] * direct + [vmem] * (len(arguments) - staged),
-        out_specs=tuple(vmem for _ in shapes),
+        out_specs=tuple(hbm if stored else vmem for _ in shapes),
         scratch_shapes=own,
         compiler_params=pltpu.CompilerParams(vmem_limit_bytes=VMEM_LIMIT),
         cost_estimate=pl.CostEstimate(flops=flops, bytes_accessed=moved, transcendentals=0),
@@ -648,11 +684,18 @@
     )
     before, after = exchange("gy", high, low)
     *matrices, moves = prepare(gain, loss)
+    (packed,) = call(
+        pack_kernel,
+        [((rows_x, SENT, LANES), BF16)],
+        [(rows_x, SENT, LANES)],
+        rows,
+    )
+    message = ((HALO * SENT + PAD, LANES), BF16)
     around, to_right, to_left = call(
         widen_kernel,
-        [((1, *tile), F32), ((HALO + 1, *tile), BF16), ((HALO + 1, *tile), BF16)],
+        [((1, *tile), F32), message, message],
         [],
-        rows, before, after,
+        packed, before, after,
     )
     from_left, from_right = exchange("gx", to_right, to_left)
     inner = rows_x - HALO
@@ -675,9 +718,13 @@
             (4, *tile),
             (total, 8, LANES),
             (total, *tile),
+            (HALO, SENT, LANES),
+            bin_state.shape,
+            pltpu.SemaphoreType.DMA((CLASSES,)),
         ],
         rows, edges, before, after, around, from_left, from_right, middle, moves, *matrices,
         flops=20 * 10**9,
+        stored=True,
     )
     return out
 

time: 28.9 us -> 27.4 us (0.948)
  waiting for transfers between devices: 5.82 us -> 4.29 us
    ppermute x4, waiting for transfers between devices: 5.82 us -> 4.29 us  [exchange(): return (lax.ppermute(upward, axis, up), lax.ppermute(downward, axis, down))]
    pallas_call x4 -> x5, Pallas kernels: 14 us -> 14.1 us  [call(): pl.pallas_call(kernel, out_shape=shapes, in_specs=[smem] * scalars + [hbm...]
  transfers between devices with their start and end apart: 4 -> 4, of which waited for: 3 -> 3; matrix products, arithmetic and copies ran while one was open for 0% -> 0% of each run, Pallas kernels for 15% -> 16%
where the time goes in v5:
time: 27.4 us; the launch traced here: 27.2 us
  Pallas kernels  16.3 us (59%)
  starting transfers between devices  5.92 us (22%)
  waiting for transfers between devices  4.29 us (16%)
  between operations  0.69 us (3%)
    pallas_call x5, Pallas kernels, call(): pl.pallas_call(kernel, out_shape=shapes, in_specs=[smem] * scalars + [hbm...  14.1 us
    ppermute x4, starting transfers between devices, exchange(): return (lax.ppermute(upward, axis, up), lax.ppermute(downward, axis, down))  5.92 us
    ppermute x4, waiting for transfers between devices, exchange(): return (lax.ppermute(upward, axis, up), lax.ppermute(downward, axis, down))  4.29 us
    pallas_call x1, Pallas kernels, prepare(): pl.pallas_call(prepare_kernel, out_shape=(jax.ShapeDtypeStruct((NG, BINS...  2.2 us
  transfers between devices with their start and end apart: 4, of which 3 were waited for; matrix products, arithmetic and copies ran while one was open for 0% of the time, Pallas kernels for 16%

profile of v5, /device:TPU:1, one launch (start us, length us, event | category | flops | bytes accessed | tf_op | source)
XLA Modules:
  0.0 27.2 jit_solution(14785448592589567769)
XLA Ops:
  0.7 1.6 %shard_map.73 = (f32[8,176,128]{2,1,0:T(8,128)S(1)}, f32[2,176,128]{2,1,0:T(8,128)S(1)}, bf16[176,128]{1,0:T(8,128)(2,1)S(1)}, bf16[176,128]{1,0:T(8,128)(2,1)S(...) custom-call(s32[1,1]{1,0:T(1,128)S(6)} %copy.8.count, s32[1,1,8]{2,1,0:T(1,128)} %order_hbm.1, ...), custom_call_target="tpu_custom_call" | custom-call | bytes 1289420 | tf_op jit(solution)/shard_map/pallas_call | solution.py:644
  2.3 2.1 %collective-permute-start = (bf16[176,128]{1,0:T(8,128)(2,1)S(1)}, bf16[176,128]{1,0:T(8,128)(2,1)S(1)}, u32[]{:S(2)}, u32[]{:S(2)}) collective-permute-start(bf16[176,128]{1,0:T(8,128)(2,1)S(1)} %get-tuple-element.20), channel_id=1, source_target_pairs={{0,1},{1,2},{2,3},{3,0},{4,5},{5,6},{6,7},{7,4},{8,9},{9,10},{10,1... | collective-permute-start | bytes 135176 | tf_op jit(solution)/shard_map/ppermute | solution.py:659
  4.4 1.0 %collective-permute-start.1 = (bf16[176,128]{1,0:T(8,128)(2,1)S(1)}, bf16[176,128]{1,0:T(8,128)(2,1)S(1)}, u32[]{:S(2)}, u32[]{:S(2)}) collective-permute-start(bf16[176,128]{1,0:T(8,128)(2,1)S(1)} %get-tuple-element.21), channel_id=1, source_target_pairs={{1,0},{2,1},{3,2},{0,3},{5,4},{6,5},{7,6},{4,7},{9,8},{10,9},{11,1... | collective-permute-start | bytes 135176 | tf_op jit(solution)/shard_map/ppermute | solution.py:659
  5.4 2.2 %shard_map.76 = (bf16[5,1056,256]{2,1,0:T(8,128)(2,1)S(1)}, bf16[208,256]{1,0:T(8,128)(2,1)S(1)}, bf16[176,256]{1,0:T(8,128)(2,1)S(1)}, bf16[2,368,256]{2,1,0:T(8,128)(2,1)S(1)}) custom-call(bf16[10,33,1089]{2,1,0:T(8,128)(2,1)S(1)} %get-tuple-element.25.gain, bf16[10,33,33]{2,1,0:T(8,128)(2,1)S(1)} %get-tuple-element.26.loss), custom_call_target="tpu_custom_call" | custom-call | flops 2000000000 | bytes 4194304 | tf_op jit(solution)/shard_map/pallas_call | solution.py:131
  7.6 0.1 shard_map.74.packed
  7.7 0.0 collective-permute-done.before
  7.7 0.1 collective-permute-done.1.after
  7.8 0.2 shard_map.75
  7.9 2.8 %collective-permute-start.2 = (bf16[616,128]{1,0:T(8,128)(2,1)S(1)}, bf16[616,128]{1,0:T(8,128)(2,1)S(1)}, u32[]{:S(2)}, u32[]{:S(2)}) collective-permute-start(bf16[616,128]{1,0:T(8,128)(2,1)S(1)} %get-tuple-element.23), channel_id=1, source_target_pairs={{0,4},{4,8},{8,12},{12,16},{16,20},{20,24},{24,28},{28,0},{1,5},{5... | collective-permute-start | bytes 473096 | tf_op jit(solution)/shard_map/ppermute | solution.py:659
  10.8 0.0 collective-permute-start.3
  10.8 2.1 %shard_map.77.middle = f32[4,176,128]{2,1,0:T(8,128)S(1)} custom-call(f32[8,176,128]{2,1,0:T(8,128)S(1)} %get-tuple-element.18.rows, f32[1,176,128]{2,1,0:T(8,128)S(1)} %get-tuple-element.22.around, bf16[2,368,256]{2,1,0:T(8,128)(2,1)S(1)} %get-tuple-element.27.moves, bf16[5,1056,256]{2,1,0:T(8,128)(2,1)S(1)} %get-tuple-element.28.blocks, ...), custom_call_target="tpu_custom_call" | custom-call | flops 5000000000 | bytes 4087808 | tf_op jit(solution)/shard_map/pallas_call | solution.py:644
  12.9 0.1 collective-permute-done.2.from_left
  13.0 4.1 %collective-permute-done.3.from_right = bf16[616,128]{1,0:T(8,128)(2,1)S(1)} collective-permute-done((bf16[616,128]{1,0:T(8,128)(2,1)S(1)}, bf16[616,128]{1,0:T(8,128)(2,1)S(1)}, u32[]{:S(2)}, u32[]{:S(2)}) %collective-permute-start.3) | collective-permute-done | bytes 157728 | tf_op jit(solution)/shard_map/ppermute | solution.py:659
  17.1 10.1 %shard_map.78 = f32[132,8,128]{2,1,0:T(8,128)} custom-call(f32[8,176,128]{2,1,0:T(8,128)S(1)} %get-tuple-element.18.rows, f32[2,176,128]{2,1,0:T(8,128)S(1)} %get-tuple-element.19.edges, bf16[176,128]{1,0:T(8,128)(2,1)S(1)} %collective-permute-done.before, bf16[176,128]{1,0:T(8,128)(2,1)S(1)} %collective-permute-done.1.after, ...), custom_call_target="tpu_custom_call" | custom-call | flops 20000000000 | bytes 5033984 | tf_op jit(solution)/shard_map/pallas_call | solution.py:644
Async XLA Ops:
  2.3 5.4 %collective-permute-start = (bf16[176,128]{1,0:T(8,128)(2,1)S(1)}, bf16[176,128]{1,0:T(8,128)(2,1)S(1)}, u32[]{:S(2)}, u32[]{:S(2)}) collective-permute-start(bf16[176,128]{1,0:T(8,128)(2,1)S(1)} %get-tuple-element.20), channel_id=1, source_target_pairs={{0,1},{1,2},{2,3},{3,0},{4,5},{5,6},{6,7},{7,4},{8,9},{9,10},{10,1... | collective-permute-start | bytes 135176 | tf_op jit(solution)/shard_map/ppermute | solution.py:659
  4.4 3.4 %collective-permute-start.1 = (bf16[176,128]{1,0:T(8,128)(2,1)S(1)}, bf16[176,128]{1,0:T(8,128)(2,1)S(1)}, u32[]{:S(2)}, u32[]{:S(2)}) collective-permute-start(bf16[176,128]{1,0:T(8,128)(2,1)S(1)} %get-tuple-element.21), channel_id=1, source_target_pairs={{1,0},{2,1},{3,2},{0,3},{5,4},{6,5},{7,6},{4,7},{9,8},{10,9},{11,1... | collective-permute-start | bytes 135176 | tf_op jit(solution)/shard_map/ppermute | solution.py:659
  7.9 5.0 %collective-permute-start.2 = (bf16[616,128]{1,0:T(8,128)(2,1)S(1)}, bf16[616,128]{1,0:T(8,128)(2,1)S(1)}, u32[]{:S(2)}, u32[]{:S(2)}) collective-permute-start(bf16[616,128]{1,0:T(8,128)(2,1)S(1)} %get-tuple-element.23), channel_id=1, source_target_pairs={{0,4},{4,8},{8,12},{12,16},{16,20},{20,24},{24,28},{28,0},{1,5},{5... | collective-permute-start | bytes 473096 | tf_op jit(solution)/shard_map/ppermute | solution.py:659
  10.8 6.3 %collective-permute-start.3 = (bf16[616,128]{1,0:T(8,128)(2,1)S(1)}, bf16[616,128]{1,0:T(8,128)(2,1)S(1)}, u32[]{:S(2)}, u32[]{:S(2)}) collective-permute-start(bf16[616,128]{1,0:T(8,128)(2,1)S(1)} %get-tuple-element.24), channel_id=1, source_target_pairs={{4,0},{8,4},{12,8},{16,12},{20,16},{24,20},{28,24},{0,28},{5,1},{9... | collective-permute-start | bytes 473096 | tf_op jit(solution)/shard_map/ppermute | solution.py:659

commit v6 on v5

--- a/solution.py
+++ b/solution.py
@@ -40,6 +40,12 @@
 NG = len(GROUPS)
 F32 = jnp.float32
 BF16 = jnp.bfloat16
+F8 = jnp.float8_e4m3fn
+FINE = ((0, 80, 40, False), (1, 0, 40, False), (2, 0, -80, True), (4, -40, -80, True))
+GAIN_SCALE = 4096.0
+PEAK = 256.0
+LOOK8 = 18
+TOGETHER = 3
 
 
 def prepare_kernel(gain, loss, blocks, tails, losses, moves, wide, turned, upper, last_rows):
@@ -216,6 +222,96 @@
                 emit(2 * unit + half, target, parts[target][unit][half], None)
 
 
+def collide_fine(bins, row0, blocks, tails, losses, fine, scale, slots, ends, sinks, emit):
+    for unit in range(2):
+        right = jnp.concatenate([bins[row0 + 2 * unit], bins[row0 + 2 * unit + 1]], axis=1)
+        right = jnp.concatenate(
+            [right, jnp.zeros((2 * LANES - ROWS, 2 * LANES), F32)], axis=0
+        ).astype(BF16)
+        pltpu.matmul_push_rhs(right, 0, unit)
+    for unit in range(2):
+        pltpu.matmul_acc_lhs(ends[unit], tails[...], 0)
+    for unit in range(2):
+        pltpu.matmul_acc_lhs(sinks[unit], losses[...])
+    for unit in range(2):
+        pltpu.matmul_push_rhs(fine_bins(bins, row0, unit, scale, True), 1, unit)
+    last = [[[jnp.zeros((PAD, LANES), F32) for _ in range(2)] for _ in range(2)] for _ in range(4)]
+    for unit in range(2):
+        block = pltpu.matmul_pop(ends[unit])
+        for group, (target, source, _) in enumerate(GROUPS):
+            for half in range(2):
+                factor = bins[row0 + 2 * unit + half, OFF[source] : OFF[source] + PAD, :]
+                piece = block[group * PAD : (group + 1) * PAD, half * LANES : (half + 1) * LANES]
+                last[target][unit][half] = last[target][unit][half] + piece * factor
+    drop = [pltpu.matmul_pop(sinks[unit]) for unit in range(2)]
+    for unit in range(2):
+        for half in range(2):
+            row = row0 + 2 * unit + half
+            for member in range(CLASSES):
+                rows = slice(OFF[member], OFF[member] + PAD)
+                lost = drop[unit][rows, half * LANES : (half + 1) * LANES] * bins[row, rows, :]
+                if member:
+                    bottom = jnp.sum(last[member][unit][half], axis=0, keepdims=True)
+                    bottom = jnp.concatenate([bottom, jnp.zeros((PAD - HEAD - 1, LANES), F32)], axis=0)
+                    base = jnp.concatenate([-lost[:HEAD], bottom - lost[HEAD:]], axis=0)
+                else:
+                    base = -lost
+                emit(2 * unit + half, member, None, base)
+    down = 1.0 / (scale * GAIN_SCALE)
+    place = {group: index for index, (group, *_) in enumerate(FINE)}
+    stages = (
+        ((3,), None),
+        ((4,), 1),
+        ((2,), None),
+        ((0, 1), 0),
+    )
+    depth = len(slots[0])
+    sums = [
+        [[jnp.zeros((HEAD, LANES), F32) for _ in range(2)] for _ in range(2)] for _ in stages
+    ]
+    left_over = [BINS * len(groups) for groups, _ in stages]
+    pending, count = [], 0
+
+    def drain():
+        stage, source, factor, slot = pending.pop(0)
+        for unit in range(2):
+            block = pltpu.matmul_pop(slots[unit][slot])
+            for half in range(2):
+                scaled = bins[row0 + 2 * unit + half, pl.ds(OFF[source] + factor, 1), :]
+                part = block[:, half * LANES : (half + 1) * LANES]
+                sums[stage][unit][half] = sums[stage][unit][half] + part * scaled
+        left_over[stage] -= 1
+        if left_over[stage] or not stage:
+            return
+        target = (None, 3, 2, 1)[stage]
+        for unit in range(2):
+            for half in range(2):
+                total = sums[stage][unit][half] * down
+                if target == 3:
+                    total = total + sums[0][unit][half]
+                emit(2 * unit + half, target, total, None)
+
+    for stage, (groups, staged) in enumerate(stages):
+        for factor in range(BINS):
+            for group in groups:
+                slot = count % depth
+                count += 1
+                rows = slice(factor * HEAD, (factor + 1) * HEAD)
+                left = fine[place[group], rows, :] if group in place else blocks[group, rows, :]
+                for unit in range(2):
+                    pltpu.matmul_acc_lhs(slots[unit][slot], left, staged)
+                if staged == 1:
+                    for unit in range(2):
+                        right = fine_bins(bins, row0, unit, scale, False)
+                        pltpu.matmul_push_rhs(right, 0, unit)
+                staged = None
+                pending.append((stage, GROUPS[group][1], factor, slot))
+                if len(pending) > LOOK8:
+                    drain()
+    while pending:
+        drain()
+
+
 def accumulators(depth, tail, rows):
     return (
         [pltpu.ACC(unit)((HEAD, 2 * LANES), F32) for unit in range(2) for _ in range(depth)]
@@ -241,12 +337,15 @@
     return emit
 
 
-def four_rows(bins, row0, matrices, refs, field, mask, change):
-    depth = LOOK + 2
+def four_rows(bins, row0, matrices, refs, field, mask, change, fine=None, scale=None):
+    depth = LOOK + 2 if fine is None else LOOK8 + 2
     slots = (refs[:depth], refs[depth : 2 * depth])
     ends, sinks = refs[2 * depth : 2 * depth + 2], refs[2 * depth + 2 :]
     emit = settle(field, mask, change, lambda index: row0 + index, lambda index: index)
-    collide_tiles(bins, row0, *matrices, slots, ends, sinks, emit)
+    if fine is None:
+        collide_tiles(bins, row0, *matrices, slots, ends, sinks, emit)
+    else:
+        collide_fine(bins, row0, *matrices, fine, scale, slots, ends, sinks, emit)
 
 
 def one_row(bins, row, matrices, refs, field, mask, change):
@@ -370,7 +469,9 @@
     return lax.broadcasted_iota(jnp.int32, (SUBLANES, LANES), 1)
 
 
-def put(field, bins, row, span, value):
+def put(field, bins, row, span, value, peak=None):
+    if peak is not None:
+        peak[...] = jnp.maximum(peak[...], jnp.max(value, axis=0))
     value = value.reshape(PAD, LANES)
     field[row, span, :] = value
     bins[row, span, :] = value.astype(BF16).astype(F32)
@@ -480,7 +581,53 @@
         tiles[HALO, start:stop, :] = moved.reshape(PAD, LANES)
 
 
-def inner_kernel(rows, around, moves, blocks, tails, losses, out, bins, change, mask):
+def split_gains(blocks, fine):
+    lane = lax.broadcasted_iota(jnp.int32, (HEAD, LANES), 1)
+
+    @pl.loop(0, BINS // TOGETHER)
+    def _(step):
+        for part in range(TOGETHER):
+            start = pl.multiple_of((step * TOGETHER + part) * HEAD, HEAD)
+            rows = pl.ds(start, HEAD)
+            for index, (group, first, second, high) in enumerate(FINE):
+                gain = blocks[group, rows, :LANES].astype(F32) * GAIN_SCALE
+                upper = gain.astype(F8).astype(F32)
+                rest = gain - upper
+                kept = lane >= PAD if high else lane < 2 * PAD
+                left = jnp.where(kept, upper, shifted(upper, first)) if first else upper
+                right = jnp.where(kept, rest, shifted(upper, second))
+                fine[index, rows, :] = jnp.concatenate([left, right], axis=1).astype(F8)
+
+
+def fine_bins(bins, row0, unit, scale, high):
+    parts = []
+    for member in (1, 2) if high else (0, 1):
+        span = slice(OFF[member], OFF[member] + PAD)
+        value = jnp.concatenate(
+            [bins[row0 + 2 * unit, span, :], bins[row0 + 2 * unit + 1, span, :]], axis=1
+        )
+        value = value * scale
+        upper = value.astype(F8).astype(F32)
+        parts.append((upper, value - upper))
+    (one, one_rest), (two, two_rest) = parts
+    gap = jnp.zeros((LANES - 3 * PAD, 2 * LANES), F32)
+    if high:
+        order = [one_rest, one, two, gap, two_rest, one, two, gap]
+    else:
+        order = [one, two, one_rest, gap, one, two, two_rest, gap]
+    return jnp.concatenate(order, axis=0).astype(F8)
+
+
+def scale_of(peak):
+    top, scale = jnp.max(peak[...]), jnp.float32(2.0**-40)
+    for power in (64, 32, 16, 8, 4, 2, 1):
+        larger = scale * jnp.float32(2.0**power)
+        scale = jnp.where(top * larger <= PEAK, larger, scale)
+    return scale
+
+
+def inner_kernel(rows, around, moves, blocks, tails, losses, out, fine, bins, change, mask):
+    split_gains(blocks, fine)
     rows_x = rows.shape[0]
     clear_gap(out, bins)
     places = [index + HALO // 2 for index in range(rows_x - HALO)]
@@ -506,8 +653,8 @@
 
 
 def outer_kernel(
-    rows, edges, before, after, around, from_left, from_right, middle, moves, blocks, tails, losses,
-    out_hbm, left, right, field, bins, change, mask, second, dense, out, sent,
+    rows, edges, before, after, around, from_left, from_right, middle, moves, fine, blocks, tails, losses,
+    out_hbm, left, right, field, bins, change, mask, second, dense, out, peak, sent,
 ):
     rows_x = rows.shape[0]
     lane = lanes()
@@ -550,8 +697,9 @@
                 other, at = column(x + d)
                 along_x.append(cells(other[at, span, :]))
             along_y = [cells(value[span]) for value in beside]
-            put(field, bins, x + reach, span, advance(centre, along_x, along_y, coefficients))
-
+            put(field, bins, x + reach, span, advance(centre, along_x, along_y, coefficients), peak)
+
+    peak[...] = jnp.zeros_like(peak)
     jobs = [job(x) for x in places]
     pl.run_scoped(lambda *refs: travel(jobs, moves, refs, first_step), *travellers())
     coefficients = weights(around, 0)
@@ -593,12 +741,15 @@
         mask[index + HALO] = jnp.broadcast_to(rows[row, FLAG : FLAG + 1, :], mask.shape[1:])
     matrices = (blocks, tails, losses)
 
+    def last_row(*refs):
+        one_row(bins, outside, matrices, refs, field, mask, change)
+
     def first_collisions(*refs):
-        one_row(bins, outside, matrices, refs, field, mask, change)
+        scale = scale_of(peak)
 
         @pl.loop(0, 2)
         def _(step):
-            four_rows(bins, rows_x * step, matrices, refs, field, mask, change)
+            four_rows(bins, rows_x * step, matrices, refs, field, mask, change, fine, scale)
 
     def second_step(x, beside):
         coefficients = weights(rows, x)
@@ -607,15 +758,21 @@
             centre = cells(field[x + reach, span, :])
             along_x = [cells(field[x + reach + d, span, :]) for d in (-1, -2, 1, 2)]
             along_y = [cells(value[span]) for value in beside]
-            put(second, bins, x + reach, span, advance(centre, along_x, along_y, coefficients))
+            put(second, bins, x + reach, span, advance(centre, along_x, along_y, coefficients), peak)
 
     def second_collisions(*refs):
+        scale = scale_of(peak)
+
         @pl.loop(0, rows_x // 4)
         def _(step):
-            four_rows(bins, reach + 4 * step, matrices, refs, second, mask, change)
-
-    shapes = accumulators(LOOK + 2, tails.shape[0], losses.shape[0])
+            row0 = reach + 4 * step
+            four_rows(bins, row0, matrices, refs, second, mask, change, fine, scale)
+
+    sizes = (tails.shape[0], losses.shape[0])
+    pl.run_scoped(last_row, *accumulators(LOOK + 2, *sizes))
+    shapes = accumulators(LOOK8 + 2, *sizes)
     pl.run_scoped(first_collisions, *shapes)
+    peak[...] = jnp.zeros_like(peak)
     later = [(lambda x=x: field[x + reach], lambda: field[outside], x) for x in range(rows_x)]
     pl.run_scoped(lambda *refs: travel(later, moves, refs, second_step), *travellers())
     pl.run_scoped(second_collisions, *shapes)
@@ -699,9 +856,9 @@
     )
     from_left, from_right = exchange("gx", to_right, to_left)
     inner = rows_x - HALO
-    (middle,) = call(
+    middle, fine = call(
         inner_kernel,
-        [((inner, *tile), F32)],
+        [((inner, *tile), F32), ((len(FINE), BINS * HEAD, 2 * LANES), F8)],
         [(inner, *tile), (4, *tile), (inner, 8, LANES)],
         rows, around, moves, *matrices,
         flops=5 * 10**9,
@@ -720,9 +877,10 @@
             (total, *tile),
             (HALO, SENT, LANES),
             bin_state.shape,
+            (SUBLANES, LANES),
             pltpu.SemaphoreType.DMA((CLASSES,)),
         ],
-        rows, edges, before, after, around, from_left, from_right, middle, moves, *matrices,
+        rows, edges, before, after, around, from_left, from_right, middle, moves, fine, *matrices,
         flops=20 * 10**9,
         stored=True,
     )

time: 27.4 us -> 26 us (0.949)
  waiting for transfers between devices: 4.29 us -> 2.65 us
    ppermute x4, waiting for transfers between devices: 4.29 us -> 2.65 us  [exchange(): return (lax.ppermute(upward, axis, up), lax.ppermute(downward, axis, down))]
  transfers between devices with their start and end apart: 4 -> 4, of which waited for: 3 -> 2; matrix products, arithmetic and copies ran while one was open for 0% -> 0% of each run, Pallas kernels for 16% -> 23%
where the time goes in v6:
time: 26 us; the launch traced here: 25.8 us
  Pallas kernels  16.5 us (63%)
  starting transfers between devices  5.92 us (23%)
  waiting for transfers between devices  2.65 us (10%)
  between operations  0.7 us (3%)
    pallas_call x5, Pallas kernels, call(): pl.pallas_call(kernel, out_shape=shapes, in_specs=[smem] * scalars + [hbm...  14.3 us
    ppermute x4, starting transfers between devices, exchange(): return (lax.ppermute(upward, axis, up), lax.ppermute(downward, axis, down))  5.92 us
    ppermute x4, waiting for transfers between devices, exchange(): return (lax.ppermute(upward, axis, up), lax.ppermute(downward, axis, down))  2.65 us
    pallas_call x1, Pallas kernels, prepare(): pl.pallas_call(prepare_kernel, out_shape=(jax.ShapeDtypeStruct((NG, BINS...  2.21 us
  transfers between devices with their start and end apart: 4, of which 2 were waited for; matrix products, arithmetic and copies ran while one was open for 0% of the time, Pallas kernels for 23%

profile of v6, /device:TPU:1, one launch (start us, length us, event | category | flops | bytes accessed | tf_op | source)
XLA Modules:
  0.0 25.8 jit_solution(5771563231977474437)
XLA Ops:
  0.7 1.6 %shard_map.73 = (f32[8,176,128]{2,1,0:T(8,128)S(1)}, f32[2,176,128]{2,1,0:T(8,128)S(1)}, bf16[176,128]{1,0:T(8,128)(2,1)S(1)}, bf16[176,128]{1,0:T(8,128)(2,1)S(...) custom-call(s32[1,1]{1,0:T(1,128)S(6)} %copy.8.count, s32[1,1,8]{2,1,0:T(1,128)} %order_hbm.1, ...), custom_call_target="tpu_custom_call" | custom-call | bytes 1289420 | tf_op jit(solution)/shard_map/pallas_call | solution.py:801
  2.3 2.1 %collective-permute-start = (bf16[176,128]{1,0:T(8,128)(2,1)S(1)}, bf16[176,128]{1,0:T(8,128)(2,1)S(1)}, u32[]{:S(2)}, u32[]{:S(2)}) collective-permute-start(bf16[176,128]{1,0:T(8,128)(2,1)S(1)} %get-tuple-element.22), channel_id=1, source_target_pairs={{0,1},{1,2},{2,3},{3,0},{4,5},{5,6},{6,7},{7,4},{8,9},{9,10},{10,1... | collective-permute-start | bytes 135176 | tf_op jit(solution)/shard_map/ppermute | solution.py:816
  4.4 1.0 %collective-permute-start.1 = (bf16[176,128]{1,0:T(8,128)(2,1)S(1)}, bf16[176,128]{1,0:T(8,128)(2,1)S(1)}, u32[]{:S(2)}, u32[]{:S(2)}) collective-permute-start(bf16[176,128]{1,0:T(8,128)(2,1)S(1)} %get-tuple-element.23), channel_id=1, source_target_pairs={{1,0},{2,1},{3,2},{0,3},{5,4},{6,5},{7,6},{4,7},{9,8},{10,9},{11,1... | collective-permute-start | bytes 135176 | tf_op jit(solution)/shard_map/ppermute | solution.py:816
  5.4 2.2 %shard_map.76 = (bf16[5,1056,256]{2,1,0:T(8,128)(2,1)S(1)}, bf16[208,256]{1,0:T(8,128)(2,1)S(1)}, bf16[176,256]{1,0:T(8,128)(2,1)S(1)}, bf16[2,368,256]{2,1,0:T(8,128)(2,1)S(1)}) custom-call(bf16[10,33,1089]{2,1,0:T(8,128)(2,1)S(1)} %get-tuple-element.27.gain, bf16[10,33,33]{2,1,0:T(8,128)(2,1)S(1)} %get-tuple-element.28.loss), custom_call_target="tpu_custom_call" | custom-call | flops 2000000000 | bytes 4194304 | tf_op jit(solution)/shard_map/pallas_call | solution.py:137
  7.6 0.1 shard_map.74.packed
  7.7 0.0 collective-permute-done.before
  7.7 0.1 collective-permute-done.1.after
  7.8 0.2 shard_map.75
  7.9 2.8 %collective-permute-start.2 = (bf16[616,128]{1,0:T(8,128)(2,1)S(1)}, bf16[616,128]{1,0:T(8,128)(2,1)S(1)}, u32[]{:S(2)}, u32[]{:S(2)}) collective-permute-start(bf16[616,128]{1,0:T(8,128)(2,1)S(1)} %get-tuple-element.25), channel_id=1, source_target_pairs={{0,4},{4,8},{8,12},{12,16},{16,20},{20,24},{24,28},{28,0},{1,5},{5... | collective-permute-start | bytes 473096 | tf_op jit(solution)/shard_map/ppermute | solution.py:816
  10.8 0.0 collective-permute-start.3
  10.8 3.7 %shard_map.77 = (f32[4,176,128]{2,1,0:T(8,128)S(1)}, f8e4m3fn[4,1056,256]{2,1,0:T(32,128)(4,1)S(1)}) custom-call(f32[8,176,128]{2,1,0:T(8,128)S(1)} %get-tuple-element.20.rows, f32[1,176,128]{2,1,0:T(8,128)S(1)} %get-tuple-element.24.around, bf16[2,368,256]{2,1,0:T(8,128)(2,1)S(1)} %get-tuple-element.29.moves, ...), custom_call_target="tpu_custom_call" | custom-call | flops 5000000000 | bytes 4087808 | tf_op jit(solution)/shard_map/pallas_call | solution.py:801
  14.5 0.0 collective-permute-done.2.from_left
  14.5 2.5 %collective-permute-done.3.from_right = bf16[616,128]{1,0:T(8,128)(2,1)S(1)} collective-permute-done((bf16[616,128]{1,0:T(8,128)(2,1)S(1)}, bf16[616,128]{1,0:T(8,128)(2,1)S(1)}, u32[]{:S(2)}, u32[]{:S(2)}) %collective-permute-start.3) | collective-permute-done | bytes 157728 | tf_op jit(solution)/shard_map/ppermute | solution.py:816
  17.1 8.7 %shard_map.78 = f32[132,8,128]{2,1,0:T(8,128)} custom-call(f32[8,176,128]{2,1,0:T(8,128)S(1)} %get-tuple-element.20.rows, f32[2,176,128]{2,1,0:T(8,128)S(1)} %get-tuple-element.21.edges, bf16[176,128]{1,0:T(8,128)(2,1)S(1)} %collective-permute-done.before, bf16[176,128]{1,0:T(8,128)(2,1)S(1)} %collective-permute-done.1.after, ...), custom_call_target="tpu_custom_call" | custom-call | flops 20000000000 | bytes 6115328 | tf_op jit(solution)/shard_map/pallas_call | solution.py:801
Async XLA Ops:
  2.3 5.4 %collective-permute-start = (bf16[176,128]{1,0:T(8,128)(2,1)S(1)}, bf16[176,128]{1,0:T(8,128)(2,1)S(1)}, u32[]{:S(2)}, u32[]{:S(2)}) collective-permute-start(bf16[176,128]{1,0:T(8,128)(2,1)S(1)} %get-tuple-element.22), channel_id=1, source_target_pairs={{0,1},{1,2},{2,3},{3,0},{4,5},{5,6},{6,7},{7,4},{8,9},{9,10},{10,1... | collective-permute-start | bytes 135176 | tf_op jit(solution)/shard_map/ppermute | solution.py:816
  4.4 3.4 %collective-permute-start.1 = (bf16[176,128]{1,0:T(8,128)(2,1)S(1)}, bf16[176,128]{1,0:T(8,128)(2,1)S(1)}, u32[]{:S(2)}, u32[]{:S(2)}) collective-permute-start(bf16[176,128]{1,0:T(8,128)(2,1)S(1)} %get-tuple-element.23), channel_id=1, source_target_pairs={{1,0},{2,1},{3,2},{0,3},{5,4},{6,5},{7,6},{4,7},{9,8},{10,9},{11,1... | collective-permute-start | bytes 135176 | tf_op jit(solution)/shard_map/ppermute | solution.py:816
  7.9 6.6 %collective-permute-start.2 = (bf16[616,128]{1,0:T(8,128)(2,1)S(1)}, bf16[616,128]{1,0:T(8,128)(2,1)S(1)}, u32[]{:S(2)}, u32[]{:S(2)}) collective-permute-start(bf16[616,128]{1,0:T(8,128)(2,1)S(1)} %get-tuple-element.25), channel_id=1, source_target_pairs={{0,4},{4,8},{8,12},{12,16},{16,20},{20,24},{24,28},{28,0},{1,5},{5... | collective-permute-start | bytes 473096 | tf_op jit(solution)/shard_map/ppermute | solution.py:816
  10.8 6.3 %collective-permute-start.3 = (bf16[616,128]{1,0:T(8,128)(2,1)S(1)}, bf16[616,128]{1,0:T(8,128)(2,1)S(1)}, u32[]{:S(2)}, u32[]{:S(2)}) collective-permute-start(bf16[616,128]{1,0:T(8,128)(2,1)S(1)} %get-tuple-element.26), channel_id=1, source_target_pairs={{4,0},{8,4},{12,8},{16,12},{20,16},{24,20},{28,24},{0,28},{5,1},{9... | collective-permute-start | bytes 473096 | tf_op jit(solution)/shard_map/ppermute | solution.py:816

commit v7 on v6

--- a/solution.py
+++ b/solution.py
@@ -42,10 +42,11 @@
 BF16 = jnp.bfloat16
 F8 = jnp.float8_e4m3fn
 FINE = ((0, 80, 40, False), (1, 0, 40, False), (2, 0, -80, True), (4, -40, -80, True))
+STAGES = (((3,), None), ((4,), 1), ((2,), None), ((0, 1), 0))
 GAIN_SCALE = 4096.0
 PEAK = 256.0
 LOOK8 = 18
-TOGETHER = 3
+TOGETHER = 11
 
 
 def prepare_kernel(gain, loss, blocks, tails, losses, moves, wide, turned, upper, last_rows):
@@ -234,7 +235,8 @@
     for unit in range(2):
         pltpu.matmul_acc_lhs(sinks[unit], losses[...])
     for unit in range(2):
-        pltpu.matmul_push_rhs(fine_bins(bins, row0, unit, scale, True), 1, unit)
+        rows = (row0 + 2 * unit, row0 + 2 * unit + 1)
+        pltpu.matmul_push_rhs(fine_bins(bins, rows, scale, True), 1, unit)
     last = [[[jnp.zeros((PAD, LANES), F32) for _ in range(2)] for _ in range(2)] for _ in range(4)]
     for unit in range(2):
         block = pltpu.matmul_pop(ends[unit])
@@ -259,12 +261,7 @@
                 emit(2 * unit + half, member, None, base)
     down = 1.0 / (scale * GAIN_SCALE)
     place = {group: index for index, (group, *_) in enumerate(FINE)}
-    stages = (
-        ((3,), None),
-        ((4,), 1),
-        ((2,), None),
-        ((0, 1), 0),
-    )
+    stages = STAGES
     depth = len(slots[0])
     sums = [
         [[jnp.zeros((HEAD, LANES), F32) for _ in range(2)] for _ in range(2)] for _ in stages
@@ -302,7 +299,8 @@
                     pltpu.matmul_acc_lhs(slots[unit][slot], left, staged)
                 if staged == 1:
                     for unit in range(2):
-                        right = fine_bins(bins, row0, unit, scale, False)
+                        pair = (row0 + 2 * unit, row0 + 2 * unit + 1)
+                        right = fine_bins(bins, pair, scale, False)
                         pltpu.matmul_push_rhs(right, 0, unit)
                 staged = None
                 pending.append((stage, GROUPS[group][1], factor, slot))
@@ -348,9 +346,9 @@
         collide_fine(bins, row0, *matrices, fine, scale, slots, ends, sinks, emit)
 
 
-def one_row(bins, row, matrices, refs, field, mask, change):
+def one_row(bins, row, matrices, refs, field, mask, change, fine, scale):
     blocks, tails, losses = matrices
-    depth = LOOK + 2
+    depth = LOOK8 + 2
     slots = (refs[:depth], refs[depth : 2 * depth])
     end, sink = refs[2 * depth], refs[2 * depth + 3]
     right = bins[row]
@@ -360,12 +358,14 @@
         pltpu.matmul_push_rhs(right, 0, unit)
     pltpu.matmul_acc_lhs(end, tails[...], 0)
     pltpu.matmul_acc_lhs(sink, losses[...], 0)
+    for unit in range(2):
+        pltpu.matmul_push_rhs(fine_bins(bins, (row,), scale, True), 1, unit)
     emit = settle(field, mask, change, lambda index: row, lambda index: 0)
     block = pltpu.matmul_pop(end)[:, :LANES]
     last = [jnp.zeros((PAD, LANES), F32) for _ in range(CLASSES)]
     for group, (target, source, _) in enumerate(GROUPS):
-        scale = bins[row, OFF[source] : OFF[source] + PAD, :]
-        last[target] = last[target] + block[group * PAD : (group + 1) * PAD] * scale
+        column = bins[row, OFF[source] : OFF[source] + PAD, :]
+        last[target] = last[target] + block[group * PAD : (group + 1) * PAD] * column
     drop = pltpu.matmul_pop(sink)[:, :LANES]
     for member in range(CLASSES):
         span = slice(OFF[member], OFF[member] + PAD)
@@ -375,33 +375,38 @@
             bottom = jnp.concatenate([bottom, jnp.zeros((PAD - HEAD - 1, LANES), F32)], axis=0)
             base = jnp.concatenate([base[:HEAD], bottom + base[HEAD:]], axis=0)
         emit(0, member, None, base)
-    parts = {t: [jnp.zeros((HEAD, LANES), F32) for _ in range(2)] for t in (1, 2, 3)}
+    place = {group: index for index, (group, *_) in enumerate(FINE)}
+    sums = [[jnp.zeros((HEAD, LANES), F32) for _ in range(2)] for _ in STAGES]
     pending, count = [], 0
 
     def drain():
-        target, source, factor, unit, slot = pending.pop(0)
+        stage, source, factor, unit, slot = pending.pop(0)
         part = pltpu.matmul_pop(slots[unit][slot])[:, :LANES]
-        scale = bins[row, OFF[source] + factor : OFF[source] + factor + 1, :]
-        parts[target][unit] = parts[target][unit] + part * scale
-
-    for target in (1, 2, 3):
-        order = [
-            (group, source, factor)
-            for factor in range(BINS)
-            for group, (aim, source, _) in enumerate(GROUPS)
-            if aim == target
-        ]
-        for group, source, factor in order:
-            unit, slot = count % 2, (count // 2) % len(slots[0])
-            count += 1
-            left = blocks[group, factor * HEAD : (factor + 1) * HEAD, :]
-            pltpu.matmul_acc_lhs(slots[unit][slot], left)
-            pending.append((target, source, factor, unit, slot))
-            if len(pending) > 2 * LOOK:
-                drain()
-        while pending:
-            drain()
-        emit(0, target, parts[target][0] + parts[target][1], None)
+        factors = bins[row, OFF[source] + factor : OFF[source] + factor + 1, :]
+        sums[stage][unit] = sums[stage][unit] + part * factors
+
+    for stage, (groups, staged) in enumerate(STAGES):
+        fresh = [staged, staged]
+        for factor in range(BINS):
+            for group in groups:
+                unit, slot = count % 2, (count // 2) % len(slots[0])
+                count += 1
+                rows = slice(factor * HEAD, (factor + 1) * HEAD)
+                left = fine[place[group], rows, :] if group in place else blocks[group, rows, :]
+                pltpu.matmul_acc_lhs(slots[unit][slot], left, fresh[unit])
+                if fresh[unit] == 1:
+                    pltpu.matmul_push_rhs(fine_bins(bins, (row,), scale, False), 0, unit)
+                fresh[unit] = None
+                pending.append((stage, GROUPS[group][1], factor, unit, slot))
+                if len(pending) > 2 * LOOK8:
+                    drain()
+    while pending:
+        drain()
+    down = 1.0 / (scale * GAIN_SCALE)
+    wide, *narrow = [first + second for first, second in sums]
+    for target, total in zip((3, 2, 1), narrow):
+        total = total * down
+        emit(0, target, total + wide if target == 3 else total, None)
 
 
 def weights(tile, row):
@@ -599,14 +604,14 @@
                 fine[index, rows, :] = jnp.concatenate([left, right], axis=1).astype(F8)
 
 
-def fine_bins(bins, row0, unit, scale, high):
+def fine_bins(bins, rows, scale, high):
     parts = []
     for member in (1, 2) if high else (0, 1):
         span = slice(OFF[member], OFF[member] + PAD)
-        value = jnp.concatenate(
-            [bins[row0 + 2 * unit, span, :], bins[row0 + 2 * unit + 1, span, :]], axis=1
-        )
-        value = value * scale
+        halves = [bins[row, span, :] * scale for row in rows]
+        if len(halves) == 1:
+            halves.append(jnp.zeros_like(halves[0]))
+        value = jnp.concatenate(halves, axis=1)
         upper = value.astype(F8).astype(F32)
         parts.append((upper, value - upper))
     (one, one_rest), (two, two_rest) = parts
@@ -626,22 +631,76 @@
     return scale
 
 
-def inner_kernel(rows, around, moves, blocks, tails, losses, out, fine, bins, change, mask):
+STEPS_AWAY = (-1, -2, 1, 2)
+
+
+def border_columns(rows_x):
+    return list(range(REACH)) + list(range(rows_x - REACH, rows_x))
+
+
+def flank(edges, before, after, around, partial):
+    middle, (_, for_y) = weights(around, 0)
+    inside = lanes() % GROUP
+    half = GROUP // 2
+    for start, stop in CHUNKS:
+        span = slice(start, stop)
+        lower, upper = cells(before[span, :].astype(F32)), cells(after[span, :].astype(F32))
+        first, last = cells(edges[0, span, :]), cells(edges[1, span, :])
+        along_y = (
+            jnp.where(
+                inside < half + LEV,
+                shifted(jnp.where(inside < half + LEV, lower, last), -LEV),
+                shifted(upper, half + LEV),
+            ),
+            jnp.where(inside < half, lower, last),
+            jnp.where(
+                inside < LEV,
+                shifted(lower, -half - LEV),
+                shifted(jnp.where(inside < LEV, first, upper), LEV),
+            ),
+            jnp.where(inside < half, first, upper),
+        )
+        total = middle * cells(around[0, span, :])
+        for value, factor in zip(along_y, for_y):
+            total = total + factor * value
+        partial[0, span, :] = total.reshape(PAD, LANES)
+    clear_gap(partial)
+
+
+def inner_kernel(
+    rows, edges, before, after, around, moves, blocks, tails, losses,
+    out, fine, partial, early, bins, change, mask,
+):
     split_gains(blocks, fine)
+    flank(edges, before, after, around, partial)
     rows_x = rows.shape[0]
     clear_gap(out, bins)
     places = [index + HALO // 2 for index in range(rows_x - HALO)]
 
+    places += border_columns(rows_x)
+
     def finish(index, along_y):
         row = places[index]
         coefficients = weights(rows, row)
-        mask[index] = jnp.broadcast_to(rows[row, FLAG : FLAG + 1, :], mask.shape[1:])
+        within = index < rows_x - HALO
+        if within:
+            mask[index] = jnp.broadcast_to(rows[row, FLAG : FLAG + 1, :], mask.shape[1:])
         for start, stop in CHUNKS:
             span = slice(start, stop)
             centre = cells(rows[row, span, :])
-            along_x = [cells(rows[row + d, span, :]) for d in (-1, -2, 1, 2)]
             beside = [cells(value[span]) for value in along_y]
-            put(out, bins, index, span, advance(centre, along_x, beside, coefficients))
+            if within:
+                along_x = [cells(rows[row + d, span, :]) for d in STEPS_AWAY]
+                put(out, bins, index, span, advance(centre, along_x, beside, coefficients))
+                continue
+            middle, (for_x, for_y) = coefficients
+            total = middle * centre
+            for value, factor in zip(beside, for_y):
+                total = total + factor * value
+            for d, factor in zip(STEPS_AWAY, for_x):
+                if 0 <= row + d < rows_x:
+                    total = total + factor * cells(rows[row + d, span, :])
+            early[index - rows_x + HALO, span, :] = total.reshape(PAD, LANES)
 
     jobs = [(lambda row=row: rows[row], lambda: around[0], row) for row in places]
     pl.run_scoped(lambda *refs: travel(jobs, moves, refs, finish), *travellers())
@@ -653,7 +712,7 @@
 
 
 def outer_kernel(
-    rows, edges, before, after, around, from_left, from_right, middle, moves, fine, blocks, tails, losses,
+    rows, partial, early, around, from_left, from_right, middle, moves, fine, blocks, tails, losses,
     out_hbm, left, right, field, bins, change, mask, second, dense, out, peak, sent,
 ):
     rows_x = rows.shape[0]
@@ -662,6 +721,7 @@
     unpack(from_left, left, dense, LANES - CORNER)
     unpack(from_right, right, dense, 0)
     clear_gap(field, bins, second, left, right)
+    peak[...] = jnp.zeros_like(peak)
 
     def column(x):
         if x < 0:
@@ -678,7 +738,7 @@
         return (lambda: around[0]), x
 
     reach = HALO // 2
-    places = list(range(-reach, reach)) + list(range(rows_x - reach, rows_x + reach))
+    places = list(range(-reach, 0)) + list(range(rows_x, rows_x + reach))
 
     def job(x):
         tile, row = column(x)
@@ -699,32 +759,24 @@
             along_y = [cells(value[span]) for value in beside]
             put(field, bins, x + reach, span, advance(centre, along_x, along_y, coefficients), peak)
 
-    peak[...] = jnp.zeros_like(peak)
     jobs = [job(x) for x in places]
     pl.run_scoped(lambda *refs: travel(jobs, moves, refs, first_step), *travellers())
-    coefficients = weights(around, 0)
+    for index, x in enumerate(border_columns(rows_x)):
+        _, (for_x, _) = weights(rows, x)
+        mask[x + reach] = jnp.broadcast_to(rows[x, FLAG : FLAG + 1, :], mask.shape[1:])
+        for start, stop in CHUNKS:
+            span = slice(start, stop)
+            total = cells(early[index, span, :])
+            for d, factor in zip(STEPS_AWAY, for_x):
+                if not 0 <= x + d < rows_x:
+                    tile, row = column(x + d)
+                    total = total + factor * cells(tile[row, span, :])
+            put(field, bins, x + reach, span, jnp.maximum(total, 0.0), peak)
+    _, (for_x, _) = weights(around, 0)
     mask[outside] = jnp.broadcast_to(around[0, FLAG : FLAG + 1, :], mask.shape[1:])
-    inside = lane % GROUP
-    half = GROUP // 2
     for start, stop in CHUNKS:
         span = slice(start, stop)
-        lower, upper = cells(before[span, :].astype(F32)), cells(after[span, :].astype(F32))
-        first, last = cells(edges[0, span, :]), cells(edges[1, span, :])
         centre = cells(around[0, span, :])
-        along_y = (
-            jnp.where(
-                inside < half + LEV,
-                shifted(jnp.where(inside < half + LEV, lower, last), -LEV),
-                shifted(upper, half + LEV),
-            ),
-            jnp.where(inside < half, lower, last),
-            jnp.where(
-                inside < LEV,
-                shifted(lower, -half - LEV),
-                shifted(jnp.where(inside < LEV, first, upper), LEV),
-            ),
-            jnp.where(inside < half, first, upper),
-        )
         beyond = jnp.where(
             lane >= LANES // 2, cells(left[HALO, span, :]), cells(right[HALO, span, :])
         )
@@ -734,18 +786,19 @@
             shifted(jnp.where(lane < GROUP, beyond, centre), -GROUP),
             shifted(jnp.where(lane < 2 * GROUP, beyond, centre), -2 * GROUP),
         )
-        put(field, bins, outside, span, advance(centre, along_x, along_y, coefficients))
+        total = cells(partial[0, span, :])
+        for value, factor in zip(along_x, for_x):
+            total = total + factor * value
+        put(field, bins, outside, span, jnp.maximum(total, 0.0), peak)
     for index in range(rows_x - HALO):
         field[index + HALO] = middle[index]
         row = index + reach
         mask[index + HALO] = jnp.broadcast_to(rows[row, FLAG : FLAG + 1, :], mask.shape[1:])
     matrices = (blocks, tails, losses)
 
-    def last_row(*refs):
-        one_row(bins, outside, matrices, refs, field, mask, change)
-
     def first_collisions(*refs):
         scale = scale_of(peak)
+        one_row(bins, outside, matrices, refs, field, mask, change, fine, scale)
 
         @pl.loop(0, 2)
         def _(step):
@@ -769,7 +822,6 @@
             four_rows(bins, row0, matrices, refs, second, mask, change, fine, scale)
 
     sizes = (tails.shape[0], losses.shape[0])
-    pl.run_scoped(last_row, *accumulators(LOOK + 2, *sizes))
     shapes = accumulators(LOOK8 + 2, *sizes)
     pl.run_scoped(first_collisions, *shapes)
     peak[...] = jnp.zeros_like(peak)
@@ -856,11 +908,11 @@
     )
     from_left, from_right = exchange("gx", to_right, to_left)
     inner = rows_x - HALO
-    middle, fine = call(
+    middle, fine, partial, early = call(
         inner_kernel,
-        [((inner, *tile), F32), ((len(FINE), BINS * HEAD, 2 * LANES), F8)],
+        [((inner, *tile), F32), ((len(FINE), BINS * HEAD, 2 * LANES), F8), ((1, *tile), F32), ((2 * REACH, *tile), F32)],
         [(inner, *tile), (4, *tile), (inner, 8, LANES)],
-        rows, around, moves, *matrices,
+        rows, edges, before, after, around, moves, *matrices,
         flops=5 * 10**9,
     )
     total = rows_x + HALO + 1
@@ -880,7 +932,7 @@
             (SUBLANES, LANES),
             pltpu.SemaphoreType.DMA((CLASSES,)),
         ],
-        rows, edges, before, after, around, from_left, from_right, middle, moves, fine, *matrices,
+        rows, partial, early, around, from_left, from_right, middle, moves, fine, *matrices,
         flops=20 * 10**9,
         stored=True,
     )

time: 26 us -> 25.5 us (0.981)
  Pallas kernels: 16.5 us -> 15.6 us
  waiting for transfers between devices: 2.65 us -> 3.12 us
    pallas_call x5, Pallas kernels: 14.3 us -> 13.3 us  [call(): pl.pallas_call(kernel, out_shape=shapes, in_specs=[smem] * scalars + [hbm...]
    ppermute x4, waiting for transfers between devices: 2.65 us -> 3.12 us  [exchange(): return (lax.ppermute(upward, axis, up), lax.ppermute(downward, axis, down))]
  transfers between devices with their start and end apart: 4 -> 4, of which waited for: 2 -> 2; matrix products, arithmetic and copies ran while one was open for 0% -> 0% of each run, Pallas kernels for 23% -> 22%
where the time goes in v7:
time: 25.5 us; the launch traced here: 25.3 us
  Pallas kernels  15.6 us (61%)
  starting transfers between devices  5.92 us (23%)
  waiting for transfers between devices  3.12 us (12%)
  between operations  0.7 us (3%)
    pallas_call x5, Pallas kernels, call(): pl.pallas_call(kernel, out_shape=shapes, in_specs=[smem] * scalars + [hbm...  13.3 us
    ppermute x4, starting transfers between devices, exchange(): return (lax.ppermute(upward, axis, up), lax.ppermute(downward, axis, down))  5.92 us
    ppermute x4, waiting for transfers between devices, exchange(): return (lax.ppermute(upward, axis, up), lax.ppermute(downward, axis, down))  3.12 us
    pallas_call x1, Pallas kernels, prepare(): pl.pallas_call(prepare_kernel, out_shape=(jax.ShapeDtypeStruct((NG, BINS...  2.21 us
  transfers between devices with their start and end apart: 4, of which 2 were waited for; matrix products, arithmetic and copies ran while one was open for 0% of the time, Pallas kernels for 22%

profile of v7, /device:TPU:1, one launch (start us, length us, event | category | flops | bytes accessed | tf_op | source)
XLA Modules:
  0.0 25.3 jit_solution(13317176471919671309)
XLA Ops:
  0.7 1.6 %shard_map.73 = (f32[8,176,128]{2,1,0:T(8,128)S(1)}, f32[2,176,128]{2,1,0:T(8,128)S(1)}, bf16[176,128]{1,0:T(8,128)(2,1)S(1)}, bf16[176,128]{1,0:T(8,128)(2,1)S(...) custom-call(s32[1,1]{1,0:T(1,128)S(6)} %copy.8.count, s32[1,1,8]{2,1,0:T(1,128)} %order_hbm.1, ...), custom_call_target="tpu_custom_call" | custom-call | bytes 1289420 | tf_op jit(solution)/shard_map/pallas_call | solution.py:853
  2.3 2.1 %collective-permute-start = (bf16[176,128]{1,0:T(8,128)(2,1)S(1)}, bf16[176,128]{1,0:T(8,128)(2,1)S(1)}, u32[]{:S(2)}, u32[]{:S(2)}) collective-permute-start(bf16[176,128]{1,0:T(8,128)(2,1)S(1)} %get-tuple-element.24), channel_id=1, source_target_pairs={{0,1},{1,2},{2,3},{3,0},{4,5},{5,6},{6,7},{7,4},{8,9},{9,10},{10,1... | collective-permute-start | bytes 135176 | tf_op jit(solution)/shard_map/ppermute | solution.py:868
  4.4 1.0 %collective-permute-start.1 = (bf16[176,128]{1,0:T(8,128)(2,1)S(1)}, bf16[176,128]{1,0:T(8,128)(2,1)S(1)}, u32[]{:S(2)}, u32[]{:S(2)}) collective-permute-start(bf16[176,128]{1,0:T(8,128)(2,1)S(1)} %get-tuple-element.25), channel_id=1, source_target_pairs={{1,0},{2,1},{3,2},{0,3},{5,4},{6,5},{7,6},{4,7},{9,8},{10,9},{11,1... | collective-permute-start | bytes 135176 | tf_op jit(solution)/shard_map/ppermute | solution.py:868
  5.4 2.2 %shard_map.76 = (bf16[5,1056,256]{2,1,0:T(8,128)(2,1)S(1)}, bf16[208,256]{1,0:T(8,128)(2,1)S(1)}, bf16[176,256]{1,0:T(8,128)(2,1)S(1)}, bf16[2,368,256]{2,1,0:T(8,128)(2,1)S(1)}) custom-call(bf16[10,33,1089]{2,1,0:T(8,128)(2,1)S(1)} %get-tuple-element.27.gain, bf16[10,33,33]{2,1,0:T(8,128)(2,1)S(1)} %get-tuple-element.28.loss), custom_call_target="tpu_custom_call" | custom-call | flops 2000000000 | bytes 4194304 | tf_op jit(solution)/shard_map/pallas_call | solution.py:138
  7.6 0.1 shard_map.74.packed
  7.7 0.0 collective-permute-done.before
  7.7 0.1 collective-permute-done.1.after
  7.8 0.2 shard_map.75
  7.9 2.8 %collective-permute-start.2 = (bf16[616,128]{1,0:T(8,128)(2,1)S(1)}, bf16[616,128]{1,0:T(8,128)(2,1)S(1)}, u32[]{:S(2)}, u32[]{:S(2)}) collective-permute-start(bf16[616,128]{1,0:T(8,128)(2,1)S(1)} %get-tuple-element.35), channel_id=1, source_target_pairs={{0,4},{4,8},{8,12},{12,16},{16,20},{20,24},{24,28},{28,0},{1,5},{5... | collective-permute-start | bytes 473096 | tf_op jit(solution)/shard_map/ppermute | solution.py:868
  10.8 0.0 collective-permute-start.3
  10.8 3.2 %shard_map.77 = (f32[4,176,128]{2,1,0:T(8,128)S(1)}, f8e4m3fn[4,1056,256]{2,1,0:T(32,128)(4,1)S(1)}, f32[1,176,128]{2,1,0:T(8,128)S(1)}, f32[4,176,128]{2,1,0:T(8,128)S(1)}) custom-call(f32[8,176,128]{2,1,0:T(8,128)S(1)} %get-tuple-element.22.rows, f32[2,176,128]{2,1,0:T(8,128)S(1)} %get-tuple-element.23.edges, ...), custom_call_target="tpu_custom_call" | custom-call | flops 5000000000 | bytes 4358144 | tf_op jit(solution)/shard_map/pallas_call | solution.py:853
  14.0 0.0 collective-permute-done.2.from_left
  14.0 3.0 %collective-permute-done.3.from_right = bf16[616,128]{1,0:T(8,128)(2,1)S(1)} collective-permute-done((bf16[616,128]{1,0:T(8,128)(2,1)S(1)}, bf16[616,128]{1,0:T(8,128)(2,1)S(1)}, u32[]{:S(2)}, u32[]{:S(2)}) %collective-permute-start.3) | collective-permute-done | bytes 157728 | tf_op jit(solution)/shard_map/ppermute | solution.py:868
  17.1 8.2 %shard_map.78 = f32[132,8,128]{2,1,0:T(8,128)} custom-call(f32[8,176,128]{2,1,0:T(8,128)S(1)} %get-tuple-element.22.rows, f32[1,176,128]{2,1,0:T(8,128)S(1)} %get-tuple-element.33.partial, f32[4,176,128]{2,1,0:T(8,128)S(1)} %get-tuple-element.34.early, f32[1,176,128]{2,1,0:T(8,128)S(1)} %get-tuple-element.26.around, ...), custom_call_target="tpu_custom_call" | custom-call | flops 20000000000 | bytes 6295552 | tf_op jit(solution)/shard_map/pallas_call | solution.py:853
Async XLA Ops:
  2.3 5.4 %collective-permute-start = (bf16[176,128]{1,0:T(8,128)(2,1)S(1)}, bf16[176,128]{1,0:T(8,128)(2,1)S(1)}, u32[]{:S(2)}, u32[]{:S(2)}) collective-permute-start(bf16[176,128]{1,0:T(8,128)(2,1)S(1)} %get-tuple-element.24), channel_id=1, source_target_pairs={{0,1},{1,2},{2,3},{3,0},{4,5},{5,6},{6,7},{7,4},{8,9},{9,10},{10,1... | collective-permute-start | bytes 135176 | tf_op jit(solution)/shard_map/ppermute | solution.py:868
  4.4 3.4 %collective-permute-start.1 = (bf16[176,128]{1,0:T(8,128)(2,1)S(1)}, bf16[176,128]{1,0:T(8,128)(2,1)S(1)}, u32[]{:S(2)}, u32[]{:S(2)}) collective-permute-start(bf16[176,128]{1,0:T(8,128)(2,1)S(1)} %get-tuple-element.25), channel_id=1, source_target_pairs={{1,0},{2,1},{3,2},{0,3},{5,4},{6,5},{7,6},{4,7},{9,8},{10,9},{11,1... | collective-permute-start | bytes 135176 | tf_op jit(solution)/shard_map/ppermute | solution.py:868
  7.9 6.1 %collective-permute-start.2 = (bf16[616,128]{1,0:T(8,128)(2,1)S(1)}, bf16[616,128]{1,0:T(8,128)(2,1)S(1)}, u32[]{:S(2)}, u32[]{:S(2)}) collective-permute-start(bf16[616,128]{1,0:T(8,128)(2,1)S(1)} %get-tuple-element.35), channel_id=1, source_target_pairs={{0,4},{4,8},{8,12},{12,16},{16,20},{20,24},{24,28},{28,0},{1,5},{5... | collective-permute-start | bytes 473096 | tf_op jit(solution)/shard_map/ppermute | solution.py:868
  10.8 6.3 %collective-permute-start.3 = (bf16[616,128]{1,0:T(8,128)(2,1)S(1)}, bf16[616,128]{1,0:T(8,128)(2,1)S(1)}, u32[]{:S(2)}, u32[]{:S(2)}) collective-permute-start(bf16[616,128]{1,0:T(8,128)(2,1)S(1)} %get-tuple-element.36), channel_id=1, source_target_pairs={{4,0},{8,4},{12,8},{16,12},{20,16},{24,20},{28,24},{0,28},{5,1},{9... | collective-permute-start | bytes 473096 | tf_op jit(solution)/shard_map/ppermute | solution.py:868

commit v8 on v7

--- a/solution.py
+++ b/solution.py
@@ -871,6 +871,7 @@
 def per_device(bin_state, courant_x, courant_y, cloudy_order, block_count, gain_kernel, loss_rate):
     rows_x = bin_state.shape[1]
     tile = (ROWS, LANES)
+    roomy = ((CLASSES - 1) * BINS + PAD, *bin_state.shape[1:])
     rows, edges, low, high, gain, loss = call(
         stage_kernel,
         [
@@ -882,7 +883,7 @@
             (loss_rate.shape, BF16),
         ],
         [
-            bin_state.shape,
+            roomy,
             courant_x.shape,
             courant_y.shape,
             pltpu.SMEM(cloudy_order.shape, jnp.int32),
@@ -928,7 +929,7 @@
             (total, 8, LANES),
             (total, *tile),
             (HALO, SENT, LANES),
-            bin_state.shape,
+            roomy,
             (SUBLANES, LANES),
             pltpu.SemaphoreType.DMA((CLASSES,)),
         ],

time: 25.5 us -> 25.5 us (level)
  no operation moved by 1% of the time
where the time goes in v8:
time: 25.5 us; the launch traced here: 25.3 us
  Pallas kernels  15.6 us (61%)
  starting transfers between devices  5.92 us (23%)
  waiting for transfers between devices  3.13 us (12%)
  between operations  0.7 us (3%)
    pallas_call x5, Pallas kernels, call(): pl.pallas_call(kernel, out_shape=shapes, in_specs=[smem] * scalars + [hbm...  13.4 us
    ppermute x4, starting transfers between devices, exchange(): return (lax.ppermute(upward, axis, up), lax.ppermute(downward, axis, down))  5.92 us
    ppermute x4, waiting for transfers between devices, exchange(): return (lax.ppermute(upward, axis, up), lax.ppermute(downward, axis, down))  3.13 us
    pallas_call x1, Pallas kernels, prepare(): pl.pallas_call(prepare_kernel, out_shape=(jax.ShapeDtypeStruct((NG, BINS...  2.21 us
  transfers between devices with their start and end apart: 4, of which 2 were waited for; matrix products, arithmetic and copies ran while one was open for 0% of the time, Pallas kernels for 22%

profile of v8, /device:TPU:1, one launch (start us, length us, event | category | flops | bytes accessed | tf_op | source)
XLA Modules:
  0.0 25.3 jit_solution(8723151226294735253)
XLA Ops:
  0.7 1.6 %shard_map.73 = (f32[8,176,128]{2,1,0:T(8,128)S(1)}, f32[2,176,128]{2,1,0:T(8,128)S(1)}, bf16[176,128]{1,0:T(8,128)(2,1)S(1)}, bf16[176,128]{1,0:T(8,128)(2,1)S(...) custom-call(s32[1,1]{1,0:T(1,128)S(6)} %copy.8.count, s32[1,1,8]{2,1,0:T(1,128)} %order_hbm.1, ...), custom_call_target="tpu_custom_call" | custom-call | bytes 1289420 | tf_op jit(solution)/shard_map/pallas_call | solution.py:853
  2.3 2.1 %collective-permute-start = (bf16[176,128]{1,0:T(8,128)(2,1)S(1)}, bf16[176,128]{1,0:T(8,128)(2,1)S(1)}, u32[]{:S(2)}, u32[]{:S(2)}) collective-permute-start(bf16[176,128]{1,0:T(8,128)(2,1)S(1)} %get-tuple-element.24), channel_id=1, source_target_pairs={{0,1},{1,2},{2,3},{3,0},{4,5},{5,6},{6,7},{7,4},{8,9},{9,10},{10,1... | collective-permute-start | bytes 135176 | tf_op jit(solution)/shard_map/ppermute | solution.py:868
  4.4 1.0 %collective-permute-start.1 = (bf16[176,128]{1,0:T(8,128)(2,1)S(1)}, bf16[176,128]{1,0:T(8,128)(2,1)S(1)}, u32[]{:S(2)}, u32[]{:S(2)}) collective-permute-start(bf16[176,128]{1,0:T(8,128)(2,1)S(1)} %get-tuple-element.25), channel_id=1, source_target_pairs={{1,0},{2,1},{3,2},{0,3},{5,4},{6,5},{7,6},{4,7},{9,8},{10,9},{11,1... | collective-permute-start | bytes 135176 | tf_op jit(solution)/shard_map/ppermute | solution.py:868
  5.4 2.2 %shard_map.76 = (bf16[5,1056,256]{2,1,0:T(8,128)(2,1)S(1)}, bf16[208,256]{1,0:T(8,128)(2,1)S(1)}, bf16[176,256]{1,0:T(8,128)(2,1)S(1)}, bf16[2,368,256]{2,1,0:T(8,128)(2,1)S(1)}) custom-call(bf16[10,33,1089]{2,1,0:T(8,128)(2,1)S(1)} %get-tuple-element.27.gain, bf16[10,33,33]{2,1,0:T(8,128)(2,1)S(1)} %get-tuple-element.28.loss), custom_call_target="tpu_custom_call" | custom-call | flops 2000000000 | bytes 4194304 | tf_op jit(solution)/shard_map/pallas_call | solution.py:138
  7.6 0.1 shard_map.74.packed
  7.7 0.0 collective-permute-done.before
  7.7 0.1 collective-permute-done.1.after
  7.8 0.2 shard_map.75
  7.9 2.8 %collective-permute-start.2 = (bf16[616,128]{1,0:T(8,128)(2,1)S(1)}, bf16[616,128]{1,0:T(8,128)(2,1)S(1)}, u32[]{:S(2)}, u32[]{:S(2)}) collective-permute-start(bf16[616,128]{1,0:T(8,128)(2,1)S(1)} %get-tuple-element.35), channel_id=1, source_target_pairs={{0,4},{4,8},{8,12},{12,16},{16,20},{20,24},{24,28},{28,0},{1,5},{5... | collective-permute-start | bytes 473096 | tf_op jit(solution)/shard_map/ppermute | solution.py:868
  10.8 0.0 collective-permute-start.3
  10.8 3.2 %shard_map.77 = (f32[4,176,128]{2,1,0:T(8,128)S(1)}, f8e4m3fn[4,1056,256]{2,1,0:T(32,128)(4,1)S(1)}, f32[1,176,128]{2,1,0:T(8,128)S(1)}, f32[4,176,128]{2,1,0:T(8,128)S(1)}) custom-call(f32[8,176,128]{2,1,0:T(8,128)S(1)} %get-tuple-element.22.rows, f32[2,176,128]{2,1,0:T(8,128)S(1)} %get-tuple-element.23.edges, ...), custom_call_target="tpu_custom_call" | custom-call | flops 5000000000 | bytes 4358144 | tf_op jit(solution)/shard_map/pallas_call | solution.py:853
  14.0 0.0 collective-permute-done.2.from_left
  14.0 3.0 %collective-permute-done.3.from_right = bf16[616,128]{1,0:T(8,128)(2,1)S(1)} collective-permute-done((bf16[616,128]{1,0:T(8,128)(2,1)S(1)}, bf16[616,128]{1,0:T(8,128)(2,1)S(1)}, u32[]{:S(2)}, u32[]{:S(2)}) %collective-permute-start.3) | collective-permute-done | bytes 157728 | tf_op jit(solution)/shard_map/ppermute | solution.py:868
  17.1 8.3 %shard_map.78 = f32[132,8,128]{2,1,0:T(8,128)} custom-call(f32[8,176,128]{2,1,0:T(8,128)S(1)} %get-tuple-element.22.rows, f32[1,176,128]{2,1,0:T(8,128)S(1)} %get-tuple-element.33.partial, f32[4,176,128]{2,1,0:T(8,128)S(1)} %get-tuple-element.34.early, f32[1,176,128]{2,1,0:T(8,128)S(1)} %get-tuple-element.26.around, ...), custom_call_target="tpu_custom_call" | custom-call | flops 20000000000 | bytes 6295552 | tf_op jit(solution)/shard_map/pallas_call | solution.py:853
Async XLA Ops:
  2.3 5.4 %collective-permute-start = (bf16[176,128]{1,0:T(8,128)(2,1)S(1)}, bf16[176,128]{1,0:T(8,128)(2,1)S(1)}, u32[]{:S(2)}, u32[]{:S(2)}) collective-permute-start(bf16[176,128]{1,0:T(8,128)(2,1)S(1)} %get-tuple-element.24), channel_id=1, source_target_pairs={{0,1},{1,2},{2,3},{3,0},{4,5},{5,6},{6,7},{7,4},{8,9},{9,10},{10,1... | collective-permute-start | bytes 135176 | tf_op jit(solution)/shard_map/ppermute | solution.py:868
  4.4 3.4 %collective-permute-start.1 = (bf16[176,128]{1,0:T(8,128)(2,1)S(1)}, bf16[176,128]{1,0:T(8,128)(2,1)S(1)}, u32[]{:S(2)}, u32[]{:S(2)}) collective-permute-start(bf16[176,128]{1,0:T(8,128)(2,1)S(1)} %get-tuple-element.25), channel_id=1, source_target_pairs={{1,0},{2,1},{3,2},{0,3},{5,4},{6,5},{7,6},{4,7},{9,8},{10,9},{11,1... | collective-permute-start | bytes 135176 | tf_op jit(solution)/shard_map/ppermute | solution.py:868
  7.9 6.1 %collective-permute-start.2 = (bf16[616,128]{1,0:T(8,128)(2,1)S(1)}, bf16[616,128]{1,0:T(8,128)(2,1)S(1)}, u32[]{:S(2)}, u32[]{:S(2)}) collective-permute-start(bf16[616,128]{1,0:T(8,128)(2,1)S(1)} %get-tuple-element.35), channel_id=1, source_target_pairs={{0,4},{4,8},{8,12},{12,16},{16,20},{20,24},{24,28},{28,0},{1,5},{5... | collective-permute-start | bytes 473096 | tf_op jit(solution)/shard_map/ppermute | solution.py:868
  10.8 6.3 %collective-permute-start.3 = (bf16[616,128]{1,0:T(8,128)(2,1)S(1)}, bf16[616,128]{1,0:T(8,128)(2,1)S(1)}, u32[]{:S(2)}, u32[]{:S(2)}) collective-permute-start(bf16[616,128]{1,0:T(8,128)(2,1)S(1)} %get-tuple-element.36), channel_id=1, source_target_pairs={{4,0},{8,4},{12,8},{16,12},{20,16},{24,20},{28,24},{0,28},{5,1},{9... | collective-permute-start | bytes 473096 | tf_op jit(solution)/shard_map/ppermute | solution.py:868
